TPU v7x, 128 devices: a whole 4x4x4 slice. The times are simulated.
128 devices in a mesh: req: 32 (over x, y, core), head: 4 (over z).
Axes of the slice: x: 4, y: 4, z: 4, core: 2. Of those that a mesh axis runs over, the one named last changes fastest.
Arguments:
- prefill_query: bfloat16 [16384, 2048], P('req', 'head'), may hold values from -16 to 16
- prefill_new_pairs: bfloat16 [16384, 2, 1024], P('req', None, 'head'), may hold values from -16 to 16
- prefill_cache: bfloat16 [32, 2, 2048, 1024], P('req', None, None, 'head'), may hold values from -16 to 16
- prefill_start: int32 [32], P('req'), may hold values from 0 to 2048, as said below
- decode_query: bfloat16 [96, 2048], P('req', 'head'), may hold values from -16 to 16
- decode_fresh: bfloat16 [96, 2, 1024], P('req', None, 'head'), may hold values from -16 to 16
- decode_cache: bfloat16 [96, 2, 2048, 1024], P('req', None, None, 'head'), may hold values from -16 to 16
- decode_length: int32 [96], P('req'), may hold values from 2 to 2048
- decode_slot: int32 [96], P('req'), may hold values from 0 to 95, each once
- prefill_states: bfloat16 [16384, 2048], P('req', 'head'), may hold values from -32 to 32
- decode_states: bfloat16 [96, 2048], P('req', 'head'), may hold values from -32 to 32
- output_proj: bfloat16 [2048, 2048], P('head', 'req'), may hold values from -0.125 to 0.125
- norm_gain: bfloat16 [2048], replicated, may hold values from 0.099609375 to 1.8984375
- gate_weight: bfloat16 [2048, 6144], P('req', 'head'), may hold values from -0.125 to 0.125
- up_weight: bfloat16 [2048, 6144], P('req', 'head'), may hold values from -0.125 to 0.125
- down_weight: bfloat16 [6144, 2048], P('head', 'req'), may hold values from -0.078125 to 0.078125
Outputs:
- prefill_result: bfloat16 [16384, 2048], P('req', 'head')
- decode_result: bfloat16 [96, 2048], P('req', 'head')
Inputs may be any that keep to these rules, and one draw needn't show every extreme that they name: `decode_slot`: a permutation; the cache of slot s is held by req index s // 3. `prefill_start`: a multiple of 512.
All inputs are finite; a program needn't handle non-finite values.
Results may differ from a plain program's by a relative error of at most 0.0094.
Values may be sent and summed in bfloat16 or wider, within the bound.
No kernel may reach another device: no remote copies, remote signals or barrier semaphores. Data moves between devices by JAX's collectives and lax.ppermute only.
A program may use at most 128 MiB of HBM per device.

v0:
```python
import math

import jax
import jax.numpy as jnp
from jax import lax
from jax.experimental import pallas as pl
from jax.experimental.pallas import tpu as pltpu
from jax.sharding import Mesh
from jax.sharding import PartitionSpec as P


F32 = jnp.float32
BF16 = jnp.bfloat16
HEAD_SIZE = 128
NEW = 512
EXTRA = 16
SPLIT = 256
BLOCK = 512
WIDTH = 2048
CACHE = 2048
HIDDEN = 1536
PIECE = 80
rope_base = 1000000.0
norm_eps = 1e-06
EXP_SCALE = math.log2(math.e) / math.sqrt(HEAD_SIZE)
UNSEEN = -1e30
NT = (((1,), (1,)), ((), ()))
TN = (((0,), (0,)), ((), ()))
VMEM_LIMIT = 58 * 1024 * 1024

START, LENGTH, SLOT, AT_X, AT_Y, AT_CORE, AT_HEAD, OWNER = 0, 1, 4, 7, 8, 9, 10, 11


def mm(a, b, dims=(((1,), (0,)), ((), ()))):
    return lax.dot_general(a, b, dims, preferred_element_type=F32)


def rope_tables(positions, head_size):
    half_size = head_size // 2
    lane_index = jnp.arange(half_size, dtype=F32)
    inverse = jnp.power(F32(rope_base), -2.0 * lane_index / head_size)
    angles = positions.astype(F32)[:, None] * inverse[None, :]
    cosine, sine = jnp.cos(angles), jnp.sin(angles)
    return (
        jnp.concatenate([cosine, cosine], axis=1),
        jnp.concatenate([-sine, sine], axis=1),
    )


def turn(values, cosine, signed_sine):
    return values * cosine + pltpu.roll(values, HEAD_SIZE // 2, 1) * signed_sine


def prefill_kernel(info, q_ref, kf_ref, vf_ref, c_ref, cos_ref, sin_ref, o_ref, kr, qr):
    cosine, sine = cos_ref[...], sin_ref[...]
    kr[...] = turn(kf_ref[...].astype(F32), cosine, sine).astype(BF16)
    for h in range(2):
        lanes = slice(h * HEAD_SIZE, (h + 1) * HEAD_SIZE)
        qr[:, lanes] = turn(q_ref[:, lanes].astype(F32), cosine, sine).astype(BF16)
    start = info[START]

    def run(length, masked):
        old_keys = c_ref[0, 0, :length, :]
        old_values = c_ref[0, 1, :length, :]
        for r in range(NEW // SPLIT):
            seen = (r + 1) * SPLIT
            for h in range(2):
                q = qr[r * SPLIT : seen, h * HEAD_SIZE : (h + 1) * HEAD_SIZE]
                old = mm(q, old_keys, NT)
                if masked:
                    at = lax.broadcasted_iota(jnp.int32, old.shape, 1)
                    old = jnp.where(at < start, old, UNSEEN)
                new = mm(q, kr[:seen, :], NT)
                row = lax.broadcasted_iota(jnp.int32, new.shape, 0) + r * SPLIT
                col = lax.broadcasted_iota(jnp.int32, new.shape, 1)
                new = jnp.where(col <= row, new, UNSEEN)
                top = jnp.maximum(
                    jnp.max(old, axis=1, keepdims=True), jnp.max(new, axis=1, keepdims=True)
                )
                old = jnp.exp2((old - top) * EXP_SCALE)
                new = jnp.exp2((new - top) * EXP_SCALE)
                total = jnp.sum(old, axis=1, keepdims=True) + jnp.sum(new, axis=1, keepdims=True)
                blend = mm(old.astype(BF16), old_values) + mm(new.astype(BF16), vf_ref[:seen, :])
                o_ref[r * SPLIT : seen, h * HEAD_SIZE : (h + 1) * HEAD_SIZE] = (
                    blend / total
                ).astype(BF16)

    @pl.when(start >= CACHE)
    def _():
        run(CACHE, False)

    @pl.when(start < CACHE)
    def _():
        run(CACHE - NEW, True)


def prefill_call(info, query, fresh, cache, cosine, sine):
    grid = pltpu.PrefetchScalarGridSpec(
        num_scalar_prefetch=1,
        grid=(2,),
        in_specs=[
            pl.BlockSpec((NEW, 2 * HEAD_SIZE), lambda i, s: (0, i)),
            pl.BlockSpec((NEW, HEAD_SIZE), lambda i, s: (0, i)),
            pl.BlockSpec((NEW, HEAD_SIZE), lambda i, s: (0, 2 + i)),
            pl.BlockSpec((1, 2, CACHE, HEAD_SIZE), lambda i, s: (0, 0, 0, i)),
            pl.BlockSpec((NEW, HEAD_SIZE), lambda i, s: (0, 0)),
            pl.BlockSpec((NEW, HEAD_SIZE), lambda i, s: (0, 0)),
        ],
        out_specs=pl.BlockSpec((NEW, 2 * HEAD_SIZE), lambda i, s: (0, i)),
        scratch_shapes=[
            pltpu.VMEM((NEW, HEAD_SIZE), BF16),
            pltpu.VMEM((NEW, 2 * HEAD_SIZE), BF16),
        ],
    )
    return pl.pallas_call(
        prefill_kernel,
        grid_spec=grid,
        out_shape=jax.ShapeDtypeStruct((NEW, 4 * HEAD_SIZE), BF16),
        compiler_params=pltpu.CompilerParams(vmem_limit_bytes=VMEM_LIMIT),
        cost_estimate=pl.CostEstimate(
            flops=4 * NEW * 4 * HEAD_SIZE * (CACHE + NEW),
            transcendentals=NEW * 4 * (CACHE + NEW),
            bytes_accessed=4 * 1024 * 1024,
        ),
        name="prefill_attention",
    )(info, query, fresh, fresh, cache, cosine, sine)


def decode_kernel(info, t0_ref, t1_ref, c_ref, cos_ref, sin_ref, o_ref, q_sc, f_sc, o_sc):
    s = pl.program_id(0)

    @pl.when(s == 0)
    def _():
        both = [r[...] for r in (t0_ref, t1_ref)]
        packed = jnp.concatenate([v[:, :8, :].reshape(128, BLOCK) for v in both], axis=0)
        code = jnp.concatenate([v[:, 8:, :128].reshape(128, 128) for v in both], axis=0)
        code = code[:, :8].astype(F32)
        want = info[OWNER] * 3 + lax.broadcasted_iota(jnp.int32, code.shape, 1)
        lane = lax.broadcasted_iota(jnp.int32, code.shape, 1)
        want = jnp.where(lane < 3, want, 1000).astype(F32)
        q = mm((code == want).astype(F32).astype(BF16), packed, TN)
        f = mm((code == want + 96.0).astype(F32).astype(BF16), packed, TN)
        cosine, sine = cos_ref[...], sin_ref[...]
        for h in range(4):
            lanes = slice(h * HEAD_SIZE, (h + 1) * HEAD_SIZE)
            q_sc[:, lanes] = turn(q[:, lanes], cosine, sine).astype(BF16).astype(F32)
            if h < 2:
                f_sc[:, lanes] = turn(f[:, lanes], cosine, sine).astype(BF16).astype(F32)
            else:
                f_sc[:, lanes] = f[:, lanes]
        o_sc[...] = jnp.zeros_like(o_sc)

    length = info[LENGTH + s]
    mine = lax.broadcasted_iota(jnp.int32, (8, BLOCK), 0) == s
    q = jnp.sum(jnp.where(mine, q_sc[...], 0.0), axis=0, keepdims=True)
    f = jnp.sum(jnp.where(mine, f_sc[...], 0.0), axis=0, keepdims=True)
    row = lax.broadcasted_iota(jnp.int32, (8, HEAD_SIZE), 0)

    def place(a, b):
        left = jnp.broadcast_to(q[:, a * HEAD_SIZE : (a + 1) * HEAD_SIZE], (8, HEAD_SIZE))
        right = jnp.broadcast_to(q[:, b * HEAD_SIZE : (b + 1) * HEAD_SIZE], (8, HEAD_SIZE))
        return jnp.where(row == a, left, jnp.where(row == b, right, 0.0))

    wide = jnp.concatenate([place(0, 1), place(2, 3)], axis=1)
    scores = mm(wide.astype(BF16), c_ref[0, 0], NT)
    at = lax.broadcasted_iota(jnp.int32, scores.shape, 1)
    scores = jnp.where(at < length, scores, UNSEEN)
    own = jnp.sum(wide * f[:, : 2 * HEAD_SIZE], axis=1, keepdims=True)
    top = jnp.maximum(jnp.max(scores, axis=1, keepdims=True), own)
    raw = jnp.exp2((scores - top) * EXP_SCALE)
    raw_own = jnp.exp2((own - top) * EXP_SCALE)
    total = jnp.sum(raw, axis=1, keepdims=True) + raw_own
    blend = mm(raw.astype(BF16), c_ref[0, 1])
    blend = blend + raw_own.astype(BF16).astype(F32) * f[:, 2 * HEAD_SIZE :]
    blend = blend / total
    upper = jnp.concatenate([blend[0:1, :HEAD_SIZE], blend[1:2, :HEAD_SIZE]], axis=1)
    lower = jnp.concatenate([blend[2:3, HEAD_SIZE:], blend[3:4, HEAD_SIZE:]], axis=1)
    row = lax.broadcasted_iota(jnp.int32, (8, 2 * HEAD_SIZE), 0)
    o_sc[...] = jnp.where(row == s, upper, jnp.where(row == s + 3, lower, o_sc[...]))

    @pl.when(s == 2)
    def _():
        o_ref[...] = o_sc[...].astype(BF16)


def decode_call(info, piece, other, cache, cosine, sine):
    grid = pltpu.PrefetchScalarGridSpec(
        num_scalar_prefetch=1,
        grid=(3,),
        in_specs=[
            pl.BlockSpec((16, 16, BLOCK), lambda i, s: (0, 4, 0)),
            pl.BlockSpec((16, 16, BLOCK), lambda i, s: (0, 4, 0)),
            pl.BlockSpec((1, 2, CACHE, 2 * HEAD_SIZE), lambda i, s: (i, 0, 0, 0)),
            pl.BlockSpec((8, HEAD_SIZE), lambda i, s: (NEW // 8, 0)),
            pl.BlockSpec((8, HEAD_SIZE), lambda i, s: (NEW // 8, 0)),
        ],
        out_specs=pl.BlockSpec((8, 2 * HEAD_SIZE), lambda i, s: (0, 0)),
        scratch_shapes=[
            pltpu.VMEM((8, 4 * HEAD_SIZE), F32),
            pltpu.VMEM((8, 4 * HEAD_SIZE), F32),
            pltpu.VMEM((8, 2 * HEAD_SIZE), F32),
        ],
    )
    return pl.pallas_call(
        decode_kernel,
        grid_spec=grid,
        out_shape=jax.ShapeDtypeStruct((8, 2 * HEAD_SIZE), BF16),
        compiler_params=pltpu.CompilerParams(vmem_limit_bytes=VMEM_LIMIT),
        cost_estimate=pl.CostEstimate(
            flops=3 * 4 * 256 * CACHE * 256, transcendentals=0, bytes_accessed=7 * 1024 * 1024
        ),
        name="decode_attention",
    )(info, piece, other, cache, cosine, sine)


def project_rows(info, a_ref, w_ref, ps_ref, outs):
    for k, out in enumerate(outs):
        at = pl.multiple_of(lax.bitwise_xor(info[AT_HEAD], k) * BLOCK, BLOCK)
        part = mm(a_ref[...], w_ref[pl.ds(at, BLOCK), :], NT)
        if k == 0:
            out[...] = part + ps_ref[...].astype(F32)
        else:
            out[...] = part.astype(BF16)


def project_first(info, a_ref, ps_ref, w0_ref, w1_ref, own, o1, o2, o3, w_out):
    x, y, core = (info[i] for i in (AT_X, AT_Y, AT_CORE))
    for xi in range(4):
        for yi in range(4):
            place = (lax.bitwise_xor(x, xi) * 4 + lax.bitwise_xor(y, yi)) * PIECE
            place = pl.multiple_of(place, 16)
            to = (xi * 8 + yi * 2) * 64

            @pl.when(core == 0)
            def _():
                w_out[to : to + 64, :] = w0_ref[pl.ds(place, 64), :]
                w_out[to + 64 : to + 128, :] = w1_ref[pl.ds(place, 64), :]

            @pl.when(core == 1)
            def _():
                w_out[to : to + 64, :] = w1_ref[pl.ds(place, 64), :]
                w_out[to + 64 : to + 128, :] = w0_ref[pl.ds(place, 64), :]

    project_rows(info, a_ref, w_out, ps_ref, (own, o1, o2, o3))


def project_second(info, a_ref, ps_ref, w_ref, own, o1, o2, o3):
    project_rows(info, a_ref, w_ref, ps_ref, (own, o1, o2, o3))


VM = pl.BlockSpec(memory_space=pltpu.VMEM)
SM = pl.BlockSpec(memory_space=pltpu.SMEM)
PARAMS = pltpu.CompilerParams(vmem_limit_bytes=VMEM_LIMIT)


def shaped(rows, cols, dtype):
    return jax.ShapeDtypeStruct((rows, cols), dtype)


def project_call(chunk, info, att, prefill_states, *weights):
    rows = pl.BlockSpec((SPLIT, BLOCK), lambda i, s: (chunk, 0))
    whole = pl.BlockSpec((SPLIT, BLOCK), lambda i, s: (0, 0))
    full = pl.BlockSpec((WIDTH, BLOCK), lambda i, s: (0, 0))
    if chunk == 0:
        kernel, extra = project_first, [pl.BlockSpec((16 * PIECE, BLOCK), lambda i, s: (0, 0))] * 2
    else:
        kernel, extra = project_second, [full]
    out_specs = [whole] * 4
    out_shape = [shaped(SPLIT, BLOCK, F32)] + [shaped(SPLIT, BLOCK, BF16)] * 3
    if chunk == 0:
        out_specs.append(full)
        out_shape.append(shaped(WIDTH, BLOCK, BF16))
    grid = pltpu.PrefetchScalarGridSpec(
        num_scalar_prefetch=1,
        grid=(1,),
        in_specs=[rows, rows] + extra,
        out_specs=out_specs,
    )
    return pl.pallas_call(
        kernel,
        grid_spec=grid,
        out_shape=out_shape,
        compiler_params=PARAMS,
        cost_estimate=pl.CostEstimate(
            flops=2 * SPLIT * BLOCK * WIDTH, transcendentals=0, bytes_accessed=6 * 1024 * 1024
        ),
    )(info, att, prefill_states, *weights)


def return_kernel(info, dec_ref, w_ref, ds_ref, out_ref, a_sc):
    head, owner = info[AT_HEAD], info[OWNER]
    shape = (256, EXTRA)
    row = lax.broadcasted_iota(jnp.int32, shape, 0)
    lane = lax.broadcasted_iota(jnp.int32, shape, 1)
    mine = jnp.full(shape, -1, jnp.int32)
    for t in range(3):
        mine = jnp.where(lane == t, info[SLOT + t], mine)
    piece, place = row >> 3, row & 7
    mask = ((piece >> 2) & 3) * 8 + (piece & 3) * 2 + (piece >> 4)
    first = (mask ^ owner) * 3
    for g in range(2):
        at = place - 3 * g
        pick = (at >= 0) & (at < 3) & (first + at == mine)
        chosen = mm(pick.astype(F32).astype(BF16), dec_ref[...], TN)
        a_sc[:, g * 2 * HEAD_SIZE : (g + 1) * 2 * HEAD_SIZE] = chosen.astype(BF16)
    part = mm(a_sc[...], w_ref[...], NT)
    for j in range(4):
        block = part[:8, j * BLOCK : (j + 1) * BLOCK]
        block = block + jnp.where(head == j, ds_ref[...].astype(F32), 0.0)
        out_ref[8 * j : 8 * j + 8, :] = block.astype(BF16)


def return_call(info, dec, w, states):
    return pl.pallas_call(
        return_kernel,
        in_specs=[SM] + [VM] * 3,
        out_specs=VM,
        out_shape=shaped(32, BLOCK, BF16),
        scratch_shapes=[pltpu.VMEM((EXTRA, BLOCK), BF16)],
        compiler_params=PARAMS,
        name="return_rows",
    )(info, dec, w, states)


def combine_kernel(info, gain_ref, *refs):
    own_ref, r1, r2, r3 = refs[-6:-2]
    summed_ref, g_ref = refs[-2:]
    total = own_ref[...] + r1[...].astype(F32) + r2[...].astype(F32) + r3[...].astype(F32)
    summed_ref[...] = total
    at = pl.multiple_of(info[AT_HEAD] * BLOCK, BLOCK)
    g_ref[:SPLIT, :] = (total * gain_ref[:, pl.ds(at, BLOCK)].astype(F32)).astype(BF16)
    if len(refs) == 7:
        g_ref[SPLIT:, :] = refs[0][...]


def combine_call(info, gain, own, parts, late=()):
    sent = SPLIT + 32 * len(late)
    return pl.pallas_call(
        combine_kernel,
        in_specs=[SM] + [VM] * (5 + len(late)),
        out_specs=[VM] * 2,
        out_shape=[shaped(SPLIT, BLOCK, F32), shaped(sent, BLOCK, BF16)],
        compiler_params=PARAMS,
    )(info, gain, *late, own, *parts)


STEP = 512
GATE_STEPS = HIDDEN // STEP


def ffn_kernel(late, info, *refs):
    parts, (gain_ref, wg, wu, wd) = refs[:4], refs[4:8]
    outs, (n_sc, r_sc, h_sc) = refs[8:12], refs[-3:]
    i = pl.program_id(0)
    head = info[AT_HEAD]

    @pl.when(i == 0)
    def _():
        squares = jnp.zeros((SPLIT, 1), F32)
        for k, part in enumerate(parts):
            at = pl.multiple_of(lax.bitwise_xor(head, k) * BLOCK, BLOCK)
            value = part[:SPLIT, :]
            n_sc[:SPLIT, pl.ds(at, BLOCK)] = value
            plain = value.astype(F32) / gain_ref[:, pl.ds(at, BLOCK)].astype(F32)
            squares = squares + jnp.sum(plain * plain, axis=1, keepdims=True)
        r_sc[:SPLIT, :] = jnp.broadcast_to(
            lax.rsqrt(squares * (1.0 / WIDTH) + norm_eps), (SPLIT, 128)
        )
        if late:
            squares = jnp.zeros((8, 1), F32)
            for j in range(4):
                rows = slice(SPLIT + 8 * j, SPLIT + 8 * j + 8)
                lanes = slice(j * BLOCK, (j + 1) * BLOCK)
                both = sum(part[rows, :].astype(F32) for part in parts)
                total = both + pltpu.roll(both, 5, 0)
                squares = squares + jnp.sum(total * total, axis=1, keepdims=True)
                scaled = total * gain_ref[:, lanes].astype(F32)
                scaled = jnp.concatenate([scaled, jnp.zeros_like(scaled)], axis=0)
                n_sc[SPLIT:, lanes] = scaled.astype(BF16)

                @pl.when(head == j)
                def _():
                    refs[12][...] = total

            scale = lax.rsqrt(squares * (1.0 / WIDTH) + norm_eps)
            r_sc[SPLIT : SPLIT + 8, :] = jnp.broadcast_to(scale, (8, 128))
            r_sc[SPLIT + 8 :, :] = jnp.zeros((8, 128), F32)

    @pl.when(i < GATE_STEPS)
    def _():
        scale = r_sc[:, :1]
        gate = mm(n_sc[...], wg[...]) * scale
        upper = mm(n_sc[...], wu[...]) * scale
        hidden = (gate / (1.0 + jnp.exp(-gate)) * upper).astype(BF16)
        h_sc[:, pl.ds(pl.multiple_of(i * STEP, STEP), STEP)] = hidden

    for k, out in enumerate(outs):

        @pl.when(i == GATE_STEPS + k)
        def _():
            out[...] = mm(h_sc[...], wd[...], NT).astype(out.dtype)


def ffn_call(late, info, parts, gain, weights):
    rows = SPLIT + EXTRA * late
    sent = SPLIT + 32 * late
    last = GATE_STEPS - 1

    def down_map(i, s):
        return (lax.bitwise_xor(s[AT_HEAD], jnp.maximum(i - GATE_STEPS, 0)), 2)

    whole = pl.BlockSpec((sent, BLOCK), lambda i, s: (0, 0))
    out = pl.BlockSpec((rows, BLOCK), lambda i, s: (0, 0))
    small = pl.BlockSpec((8, BLOCK), lambda i, s: (0, 0))
    grid = pltpu.PrefetchScalarGridSpec(
        num_scalar_prefetch=1,
        grid=(GATE_STEPS + 4,),
        in_specs=[whole] * 4
        + [
            pl.BlockSpec((1, WIDTH), lambda i, s: (0, 0)),
            pl.BlockSpec((WIDTH, STEP), lambda i, s: (0, jnp.minimum(i, last))),
            pl.BlockSpec((WIDTH, STEP), lambda i, s: (0, GATE_STEPS + jnp.minimum(i, last))),
            pl.BlockSpec((BLOCK, HIDDEN), down_map),
        ],
        out_specs=[out] * 4 + [small] * late,
        scratch_shapes=[
            pltpu.VMEM((rows, WIDTH), BF16),
            pltpu.VMEM((rows, 128), F32),
            pltpu.VMEM((rows, HIDDEN), BF16),
        ],
    )

    def kernel(*refs):
        ffn_kernel(late, *refs)

    return pl.pallas_call(
        kernel,
        grid_spec=grid,
        out_shape=[shaped(rows, BLOCK, F32)]
        + [shaped(rows, BLOCK, BF16)] * 3
        + [shaped(8, BLOCK, F32)] * late,
        compiler_params=PARAMS,
        cost_estimate=pl.CostEstimate(
            flops=6 * rows * HIDDEN * WIDTH,
            transcendentals=rows * HIDDEN,
            bytes_accessed=20 * 1024 * 1024,
        ),
    )(info, *parts, gain, weights, weights, weights)


def finish_first(s_ref, own, r1, r2, r3, p_ref):
    total = own[...] + r1[...].astype(F32) + r2[...].astype(F32) + r3[...].astype(F32)
    p_ref[...] = (s_ref[...] + total).astype(BF16)


def finish_second(old_ref, s_ref, l_ref, own, r1, r2, r3, p_ref, d_ref):
    total = own[...] + r1[...].astype(F32) + r2[...].astype(F32) + r3[...].astype(F32)
    p_ref[...] = (s_ref[...] + total[:SPLIT, :]).astype(BF16)
    d_ref[...] = (l_ref[...] + total[SPLIT : SPLIT + 8, :]).astype(BF16)[:3, :]


def finish_call(summed, own, parts, old=None, late=None):
    rows = SPLIT if old is None else SPLIT + EXTRA

    def block(n):
        return pl.BlockSpec((n, BLOCK), lambda i: (0, 0))

    first = pl.BlockSpec((SPLIT, BLOCK), lambda i: (0 if old is None else 1, 0))
    in_specs = [block(SPLIT)] + [block(rows)] * 4
    if old is None:
        return pl.pallas_call(
            finish_first,
            grid=(1,),
            in_specs=in_specs,
            out_specs=first,
            out_shape=shaped(NEW, BLOCK, BF16),
            compiler_params=PARAMS,
            name="finish_0",
        )(summed, own, *parts)
    return pl.pallas_call(
        finish_second,
        grid=(1,),
        in_specs=[pl.BlockSpec(memory_space=pl.ANY), block(SPLIT), block(8)] + [block(rows)] * 4,
        out_specs=[first, block(3)],
        out_shape=[shaped(NEW, BLOCK, BF16), shaped(3, BLOCK, BF16)],
        input_output_aliases={0: 0},
        compiler_params=PARAMS,
        name="finish_1",
    )(old, summed, late, own, *parts)


SIZE = {"x": 4, "y": 4, "core": 2, "head": 4}


def swap(value, axis, k):
    return lax.ppermute(value, axis, [(i, i ^ k) for i in range(SIZE[axis])])


def spread(value):
    for axis in ("y", "x"):
        others = [swap(value, axis, k) for k in (1, 2, 3)]
        value = jnp.concatenate([value] + others, axis=0)
    return value, swap(value, "core", 1)


def body(
    prefill_query,
    prefill_new_pairs,
    prefill_cache,
    prefill_start,
    decode_query,
    decode_fresh,
    decode_cache,
    decode_length,
    decode_slot,
    prefill_states,
    decode_states,
    output_proj,
    norm_gain,
    gate_weight,
    up_weight,
    down_weight,
):
    at = [lax.axis_index(a) for a in ("x", "y", "core", "head")]
    owner = at[0] * 8 + at[1] * 2 + at[2]
    info = jnp.concatenate(
        [prefill_start, decode_length, decode_slot, jnp.stack(at + [owner]).astype(jnp.int32)]
    )

    packed = jnp.concatenate([gate_weight, up_weight, down_weight.T], axis=1)
    weights = lax.all_gather(packed, ("x", "y", "core"), axis=0, tiled=True)

    code = decode_slot.astype(BF16)[:, None]
    unused = jnp.full((2, BLOCK), 255.0, BF16)
    piece = jnp.concatenate(
        [
            output_proj.T,
            decode_query,
            decode_fresh.reshape(3, BLOCK),
            unused,
            jnp.broadcast_to(code, (3, BLOCK)),
            jnp.broadcast_to((code + 96.0).astype(BF16), (3, BLOCK)),
            unused,
        ],
        axis=0,
    )
    piece, other = spread(piece)
    both = [v.reshape(16, PIECE, BLOCK) for v in (piece, other)]

    positions = jnp.concatenate(
        [
            prefill_start + jnp.arange(NEW, dtype=jnp.int32),
            decode_length,
            jnp.zeros((5,), jnp.int32),
        ]
    )
    cosine, sine = rope_tables(positions, HEAD_SIZE)
    fresh = prefill_new_pairs.reshape(NEW, BLOCK)
    att = prefill_call(info, prefill_query, fresh, prefill_cache, cosine, sine)
    gain = norm_gain.reshape(1, WIDTH)

    def exchanged(parts):
        return [swap(p, "head", k + 1) for k, p in enumerate(parts)]

    def shared(value):
        return [value] + [swap(value, "head", k) for k in (1, 2, 3)]

    own0, *parts0, w_all = project_call(0, info, att, prefill_states, piece, other)
    parts0 = exchanged(parts0)
    own1, *parts1 = project_call(1, info, att, prefill_states, w_all)
    parts1 = exchanged(parts1)

    decoded = decode_call(info, *both, decode_cache, cosine, sine)
    decoded = jnp.concatenate(spread(decoded), axis=0)
    states = jnp.pad(decode_states, ((3, 2), (0, 0)))
    late = return_call(info, decoded, w_all, states)

    summed0, scaled0 = combine_call(info, gain, own0, parts0)
    scaled0 = shared(scaled0)
    summed1, scaled1 = combine_call(info, gain, own1, parts1, (late,))
    scaled1 = shared(scaled1)
    own0, *parts0 = ffn_call(0, info, scaled0, gain, weights)
    parts0 = exchanged(parts0)
    own1, *parts1, late = ffn_call(1, info, scaled1, gain, weights)
    parts1 = exchanged(parts1)
    result = finish_call(summed0, own0, parts0)
    return finish_call(summed1, own1, parts1, result, late)


def solution(mesh):
    inner = Mesh(mesh.devices.reshape(4, 4, 2, 4), ("x", "y", "core", "head"))
    req = ("x", "y", "core")
    in_specs = (
        P(req, "head"),
        P(req, None, "head"),
        P(req, None, None, "head"),
        P(req),
        P(req, "head"),
        P(req, None, "head"),
        P(req, None, None, "head"),
        P(req),
        P(req),
        P(req, "head"),
        P(req, "head"),
        P("head", req),
        P(),
        P(req, "head"),
        P(req, "head"),
        P("head", req),
    )
    out_specs = (P(req, "head"), P(req, "head"))

    return jax.shard_map(body, mesh=inner, in_specs=in_specs, out_specs=out_specs, check_vma=False)
```

profile of v0, /device:TPU:1, one launch (start us, length us, event | category | flops | bytes accessed | tf_op | source)
XLA Modules:
  0.0 212.6 jit_solution(15225643050773810056)
XLA Ops:
  11.8 2.6 %collective-permute-start.1 = (bf16[80,512]{1,0:T(8,128)(2,1)S(1)}, bf16[80,512]{1,0:T(8,128)(2,1)S(1)}, u32[]{:S(2)}, u32[]{:S(2)}) collective-permute-start(bf16[80,512]{1,0:T(8,128)(2,1)S(1)} %concatenate.48), channel_id=1, source_target_pairs={{0,16},{8,24},{16,0},{24,8},{1,17},{9,25},{17,1},{25,9},{2,18},{10... | collective-permute-start | bytes 245768 | tf_op jit(solution)/shard_map/ppermute | solution.py:496
  14.4 3.3 %collective-permute-done.1 = bf16[80,512]{1,0:T(8,128)(2,1)S(1)} collective-permute-done((bf16[80,512]{1,0:T(8,128)(2,1)S(1)}, bf16[80,512]{1,0:T(8,128)(2,1)S(1)}, u32[]{:S(2)}, u32[]{:S(2)}) %collective-permute-start.1) | collective-permute-done | bytes 81952 | tf_op jit(solution)/shard_map/ppermute | solution.py:496
  21.4 2.5 %collective-permute-start.4 = (bf16[320,512]{1,0:T(8,128)(2,1)S(1)}, bf16[320,512]{1,0:T(8,128)(2,1)S(1)}, u32[]{:S(2)}, u32[]{:S(2)}) collective-permute-start(bf16[320,512]{1,0:T(8,128)(2,1)S(1)} %concatenate.49), channel_id=1, source_target_pairs={{0,64},{32,96},{64,0},{96,32},{1,65},{33,97},{65,1},{97,33},{2,66}... | collective-permute-start | bytes 983048 | tf_op jit(solution)/shard_map/ppermute | solution.py:496
  24.1 5.9 %collective-permute-done.3 = bf16[320,512]{1,0:T(8,128)(2,1)S(1)} collective-permute-done((bf16[320,512]{1,0:T(8,128)(2,1)S(1)}, bf16[320,512]{1,0:T(8,128)(2,1)S(1)}, u32[]{:S(2)}, u32[]{:S(2)}) %collective-permute-start.3) | collective-permute-done | bytes 327712 | tf_op jit(solution)/shard_map/ppermute | solution.py:496
  30.0 16.8 %collective-permute-done.4 = bf16[320,512]{1,0:T(8,128)(2,1)S(1)} collective-permute-done((bf16[320,512]{1,0:T(8,128)(2,1)S(1)}, bf16[320,512]{1,0:T(8,128)(2,1)S(1)}, u32[]{:S(2)}, u32[]{:S(2)}) %collective-permute-start.4) | collective-permute-done | bytes 327712 | tf_op jit(solution)/shard_map/ppermute | solution.py:496
  47.7 4.2 %collective-permute-start.6 = (bf16[1280,512]{1,0:T(8,128)(2,1)S(1)}, bf16[1280,512]{1,0:T(8,128)(2,1)S(1)}, u32[]{:S(2)}, u32[]{:S(2)}) collective-permute-start(bf16[1280,512]{1,0:T(8,128)(2,1)S(1)} %concatenate.50.w0_ref), channel_id=1, source_target_pairs={{0,4},{4,0},{1,5},{5,1},{2,6},{6,2},{3,7},{7,3},{8,12},{12,8},{9,1... | collective-permute-start | bytes 3932168 | tf_op jit(solution)/shard_map/ppermute | solution.py:496
  56.3 11.3 %prefill_attention.1.a_ref = bf16[512,512]{1,0:T(8,128)(2,1)} custom-call(s32[12]{0:T(128)} %concatenate.43.info.refs_0_, bf16[512,512]{1,0:T(8,128)(2,1)} %q_ref.1, bf16[512,512]{1,0:T(8,128)(2,1)} %bitcast.21, bf16[512,512]{1,0:T(8,128)(2,1)} %bitcast.22, bf16[1,2,2048,256]{3,2,1,0:T(8,128)(2,1)} %c_ref.2, f32[520,128]{1,0:T(8,128)} %get-tuple-element.63.cos_ref, ...), custom_call_target="tpu_custom_call" | custom-call | flops 2684354560 | bytes 4194304 | tf_op jit(solution)/shard_map/prefill_attention/pallas_call | solution.py:115
  68.6 6.8 %decode_attention.1 = bf16[8,256]{1,0:T(8,128)(2,1)} custom-call(s32[12]{0:T(128)} %concatenate.43.info.refs_0_, bf16[16,80,512]{2,1,0:T(8,128)(2,1)} %bitcast.15, bf16[16,80,512]{2,1,0:T(8,128)(2,1)} %bitcast.16, bf16[3,2,2048,256]{3,2,1,0:T(8,128)(2,1)} %c_ref.3, f32[520,128]{1,0:T(8,128)} %get-tuple-element.63.cos_ref, f32[520,128]{1,0:T(8,128)} %get-tuple-element.64.sin_ref), custom_call_target="tpu_custom_call" | custom-call | flops 1610612736 | bytes 7340032 | tf_op jit(solution)/shard_map/decode_attention/pallas_call | solution.py:204
  75.4 3.8 %collective-permute-start.18 = (bf16[8,256]{1,0:T(8,128)(2,1)}, bf16[8,256]{1,0:T(8,128)(2,1)S(1)}, u32[]{:S(2)}, u32[]{:S(2)}) collective-permute-start(bf16[8,256]{1,0:T(8,128)(2,1)} %decode_attention.1), channel_id=1, source_target_pairs={{0,24},{8,16},{16,8},{24,0},{1,25},{9,17},{17,9},{25,1},{2,26},{10... | collective-permute-start | bytes 12296 | tf_op jit(solution)/shard_map/ppermute | solution.py:496
  79.2 5.1 %shard_map.167 = (f32[256,512]{1,0:T(8,128)}, bf16[256,512]{1,0:T(8,128)(2,1)}, bf16[256,512]{1,0:T(8,128)(2,1)}, bf16[256,512]{1,0:T(8,128)(2,1)}, bf16[2048,512]{1,0:T(8,128)(2,1)}) custom-call(s32[12]{0:T(128)} %concatenate.43.info.refs_0_, bf16[512,512]{1,0:T(8,128)(2,1)} %prefill_attention.1.a_ref, bf16[512,512]{1,0:T(8,128)(2,1)} %ps_ref.3, ...), custom_call_target="tpu_custom_call" | custom-call | flops 536870912 | bytes 6291456 | tf_op jit(solution)/shard_map/pallas_call | solution.py:279
  84.3 4.0 %shard_map.170 = (f32[256,512]{1,0:T(8,128)}, bf16[256,512]{1,0:T(8,128)(2,1)}, bf16[256,512]{1,0:T(8,128)(2,1)}, bf16[256,512]{1,0:T(8,128)(2,1)}) custom-call(s32[12]{0:T(128)} %concatenate.43.info.refs_0_, bf16[512,512]{1,0:T(8,128)(2,1)} %prefill_attention.1.a_ref, bf16[512,512]{1,0:T(8,128)(2,1)} %ps_ref.3, bf16[2048,512]{1,0:T(8,128)(2,1)} %get-tuple-element.34.w_ref), custom_call_target="tpu_custom_call" | custom-call | flops 536870912 | bytes 6291456 | tf_op jit(solution)/shard_map/pallas_call | solution.py:279
  90.8 3.2 %collective-permute-start.8 = (bf16[256,512]{1,0:T(8,128)(2,1)S(1)}, bf16[256,512]{1,0:T(8,128)(2,1)S(1)}, u32[]{:S(2)}, u32[]{:S(2)}) collective-permute-start(bf16[256,512]{1,0:T(8,128)(2,1)S(1)} %copy-done.31), channel_id=1, source_target_pairs={{0,2},{1,3},{2,0},{3,1},{4,6},{5,7},{6,4},{7,5},{8,10},{9,11},{10,... | collective-permute-start | bytes 786440 | tf_op jit(solution)/shard_map/ppermute | solution.py:496
  94.6 3.0 %collective-permute-done.19 = bf16[32,256]{1,0:T(8,128)(2,1)S(1)} collective-permute-done((bf16[32,256]{1,0:T(8,128)(2,1)S(1)}, bf16[32,256]{1,0:T(8,128)(2,1)S(1)}, u32[]{:S(2)}, u32[]{:S(2)}) %collective-permute-start.19) | collective-permute-done | bytes 16416 | tf_op jit(solution)/shard_map/ppermute | solution.py:496
  97.7 4.1 %collective-permute-done.20 = bf16[32,256]{1,0:T(8,128)(2,1)S(1)} collective-permute-done((bf16[32,256]{1,0:T(8,128)(2,1)S(1)}, bf16[32,256]{1,0:T(8,128)(2,1)S(1)}, u32[]{:S(2)}, u32[]{:S(2)}) %collective-permute-start.20) | collective-permute-done | bytes 16416 | tf_op jit(solution)/shard_map/ppermute | solution.py:496
  101.8 3.9 %collective-permute-done.21 = bf16[32,256]{1,0:T(8,128)(2,1)S(1)} collective-permute-done((bf16[32,256]{1,0:T(8,128)(2,1)S(1)}, bf16[32,256]{1,0:T(8,128)(2,1)S(1)}, u32[]{:S(2)}, u32[]{:S(2)}) %collective-permute-start.21) | collective-permute-done | bytes 16416 | tf_op jit(solution)/shard_map/ppermute | solution.py:496
  105.7 5.3 %collective-permute-start.22 = (bf16[128,256]{1,0:T(8,128)(2,1)S(1)}, bf16[128,256]{1,0:T(8,128)(2,1)S(1)}, u32[]{:S(2)}, u32[]{:S(2)}) collective-permute-start(bf16[128,256]{1,0:T(8,128)(2,1)S(1)} %get-tuple-element.46), channel_id=1, source_target_pairs={{0,4},{4,0},{1,5},{5,1},{2,6},{6,2},{3,7},{7,3},{8,12},{12,8},{9,1... | collective-permute-start | bytes 196616 | tf_op jit(solution)/shard_map/ppermute | solution.py:496
  117.6 3.0 %collective-permute-start.11 = (bf16[256,512]{1,0:T(8,128)(2,1)}, bf16[256,512]{1,0:T(8,128)(2,1)S(1)}, u32[]{:S(2)}, u32[]{:S(2)}) collective-permute-start(bf16[256,512]{1,0:T(8,128)(2,1)} %get-tuple-element.29.refs_1_), channel_id=1, source_target_pairs={{0,2},{1,3},{2,0},{3,1},{4,6},{5,7},{6,4},{7,5},{8,10},{9,11},{10,... | collective-permute-start | bytes 786440 | tf_op jit(solution)/shard_map/ppermute | solution.py:496
  122.3 3.1 %return_rows.1.refs_0_ = bf16[32,512]{1,0:T(8,128)(2,1)} custom-call(s32[12]{0:T(128)} %concatenate.43.info.refs_0_, bf16[256,256]{1,0:T(8,128)(2,1)} %copy-done.22, bf16[2048,512]{1,0:T(8,128)(2,1)} %get-tuple-element.34.w_ref, bf16[8,512]{1,0:T(8,128)(2,1)} %pad.4.ds_ref), custom_call_target="tpu_custom_call" | custom-call | tf_op jit(solution)/shard_map/return_rows/pallas_call | solution.py:314
  131.0 2.7 %collective-permute-start.27 = (bf16[288,512]{1,0:T(8,128)(2,1)}, bf16[288,512]{1,0:T(8,128)(2,1)S(1)}, u32[]{:S(2)}, u32[]{:S(2)}) collective-permute-start(bf16[288,512]{1,0:T(8,128)(2,1)} %get-tuple-element.40.refs_1_), channel_id=1, source_target_pairs={{0,2},{1,3},{2,0},{3,1},{4,6},{5,7},{6,4},{7,5},{8,10},{9,11},{10,... | collective-permute-start | bytes 884744 | tf_op jit(solution)/shard_map/ppermute | solution.py:496
  134.7 3.8 %collective-permute-done.12.refs_4_ = bf16[256,512]{1,0:T(8,128)(2,1)S(1)} collective-permute-done((bf16[256,512]{1,0:T(8,128)(2,1)}, bf16[256,512]{1,0:T(8,128)(2,1)S(1)}, u32[]{:S(2)}, u32[]{:S(2)}) %collective-permute-start.12) | collective-permute-done | bytes 262176 | tf_op jit(solution)/shard_map/ppermute | solution.py:496
  139.2 14.7 %shard_map.169 = (f32[256,512]{1,0:T(8,128)}, bf16[256,512]{1,0:T(8,128)(2,1)}, bf16[256,512]{1,0:T(8,128)(2,1)}, bf16[256,512]{1,0:T(8,128)(2,1)}) custom-call(s32[12]{0:T(128)} %concatenate.43.info.refs_0_, bf16[256,512]{1,0:T(8,128)(2,1)} %get-tuple-element.29.refs_1_, bf16[256,512]{1,0:T(8,128)(2,1)} %copy-done.10, bf16[256,512]{1,0:T(8,128)(2,1)} %copy-done.11, ...), custom_call_target="tpu_custom_call" | custom-call | flops 4831838208 | bytes 20971520 | tf_op jit(solution)/shard_map/pallas_call | solution.py:436
  155.5 15.3 %shard_map.172 = (f32[272,512]{1,0:T(8,128)}, bf16[272,512]{1,0:T(8,128)(2,1)}, bf16[272,512]{1,0:T(8,128)(2,1)}, bf16[272,512]{1,0:T(8,128)(2,1)}, f32[8,512]{1,0:T(8,128)}) custom-call(s32[12]{0:T(128)} %concatenate.43.info.refs_0_, bf16[288,512]{1,0:T(8,128)(2,1)} %get-tuple-element.40.refs_1_, bf16[288,512]{1,0:T(8,128)(2,1)} %copy-done.4, ...), custom_call_target="tpu_custom_call" | custom-call | flops 5133828096 | bytes 20971520 | tf_op jit(solution)/shard_map/pallas_call | solution.py:436
  177.4 14.2 %collective-permute-done.14.r2 = bf16[256,512]{1,0:T(8,128)(2,1)S(1)} collective-permute-done((bf16[256,512]{1,0:T(8,128)(2,1)S(1)}, bf16[256,512]{1,0:T(8,128)(2,1)S(1)}, u32[]{:S(2)}, u32[]{:S(2)}) %collective-permute-start.14) | collective-permute-done | bytes 262176 | tf_op jit(solution)/shard_map/ppermute | solution.py:496
  191.6 8.0 %collective-permute-done.15.r3 = bf16[256,512]{1,0:T(8,128)(2,1)S(1)} collective-permute-done((bf16[256,512]{1,0:T(8,128)(2,1)S(1)}, bf16[256,512]{1,0:T(8,128)(2,1)S(1)}, u32[]{:S(2)}, u32[]{:S(2)}) %collective-permute-start.15) | collective-permute-done | bytes 262176 | tf_op jit(solution)/shard_map/ppermute | solution.py:496
  (153 shorter events, 47.1 us)
Async XLA Ops:
  7.2 131.3 %all-gather.2.cloned.1.call-start = ((), (), s32[]{:S(2)}) async-start(), calls=%async_computation | async-start | bytes 19464192 | tf_op jit(solution)/shard_map/all_gather | solution.py:531
  21.4 25.4 %collective-permute-start.4 = (bf16[320,512]{1,0:T(8,128)(2,1)S(1)}, bf16[320,512]{1,0:T(8,128)(2,1)S(1)}, u32[]{:S(2)}, u32[]{:S(2)}) collective-permute-start(bf16[320,512]{1,0:T(8,128)(2,1)S(1)} %concatenate.49), channel_id=1, source_target_pairs={{0,64},{32,96},{64,0},{96,32},{1,65},{33,97},{65,1},{97,33},{2,66}... | collective-permute-start | bytes 983048 | tf_op jit(solution)/shard_map/ppermute | solution.py:496
  23.9 22.9 %collective-permute-start.5 = (bf16[320,512]{1,0:T(8,128)(2,1)S(1)}, bf16[320,512]{1,0:T(8,128)(2,1)S(1)}, u32[]{:S(2)}, u32[]{:S(2)}) collective-permute-start(bf16[320,512]{1,0:T(8,128)(2,1)S(1)} %concatenate.49), channel_id=1, source_target_pairs={{0,96},{32,64},{64,32},{96,0},{1,97},{33,65},{65,33},{97,1},{2,98}... | collective-permute-start | bytes 983048 | tf_op jit(solution)/shard_map/ppermute | solution.py:496
  47.7 19.8 %collective-permute-start.6 = (bf16[1280,512]{1,0:T(8,128)(2,1)S(1)}, bf16[1280,512]{1,0:T(8,128)(2,1)S(1)}, u32[]{:S(2)}, u32[]{:S(2)}) collective-permute-start(bf16[1280,512]{1,0:T(8,128)(2,1)S(1)} %concatenate.50.w0_ref), channel_id=1, source_target_pairs={{0,4},{4,0},{1,5},{5,1},{2,6},{6,2},{3,7},{7,3},{8,12},{12,8},{9,1... | collective-permute-start | bytes 3932168 | tf_op jit(solution)/shard_map/ppermute | solution.py:496
  75.3 15.5 %collective-permute-start.16 = (bf16[8,256]{1,0:T(8,128)(2,1)}, bf16[8,256]{1,0:T(8,128)(2,1)S(1)}, u32[]{:S(2)}, u32[]{:S(2)}) collective-permute-start(bf16[8,256]{1,0:T(8,128)(2,1)} %decode_attention.1), channel_id=1, source_target_pairs={{0,8},{8,0},{16,24},{24,16},{1,9},{9,1},{17,25},{25,17},{2,10},{10... | collective-permute-start | bytes 12296 | tf_op jit(solution)/shard_map/ppermute | solution.py:496
  75.4 18.7 %collective-permute-start.17 = (bf16[8,256]{1,0:T(8,128)(2,1)}, bf16[8,256]{1,0:T(8,128)(2,1)S(1)}, u32[]{:S(2)}, u32[]{:S(2)}) collective-permute-start(bf16[8,256]{1,0:T(8,128)(2,1)} %decode_attention.1), channel_id=1, source_target_pairs={{0,16},{8,24},{16,0},{24,8},{1,17},{9,25},{17,1},{25,9},{2,18},{10... | collective-permute-start | bytes 12296 | tf_op jit(solution)/shard_map/ppermute | solution.py:496
  75.4 19.1 %collective-permute-start.18 = (bf16[8,256]{1,0:T(8,128)(2,1)}, bf16[8,256]{1,0:T(8,128)(2,1)S(1)}, u32[]{:S(2)}, u32[]{:S(2)}) collective-permute-start(bf16[8,256]{1,0:T(8,128)(2,1)} %decode_attention.1), channel_id=1, source_target_pairs={{0,24},{8,16},{16,8},{24,0},{1,25},{9,17},{17,9},{25,1},{2,26},{10... | collective-permute-start | bytes 12296 | tf_op jit(solution)/shard_map/ppermute | solution.py:496
  88.4 32.2 %collective-permute-start.23 = (bf16[256,512]{1,0:T(8,128)(2,1)}, bf16[256,512]{1,0:T(8,128)(2,1)S(1)}, u32[]{:S(2)}, u32[]{:S(2)}) collective-permute-start(bf16[256,512]{1,0:T(8,128)(2,1)} %get-tuple-element.36), channel_id=1, source_target_pairs={{0,1},{1,0},{2,3},{3,2},{4,5},{5,4},{6,7},{7,6},{8,9},{9,8},{10,11... | collective-permute-start | bytes 786440 | tf_op jit(solution)/shard_map/ppermute | solution.py:496
  90.7 20.9 %collective-permute-start.7 = (bf16[256,512]{1,0:T(8,128)(2,1)S(1)}, bf16[256,512]{1,0:T(8,128)(2,1)S(1)}, u32[]{:S(2)}, u32[]{:S(2)}) collective-permute-start(bf16[256,512]{1,0:T(8,128)(2,1)S(1)} %copy-done.32), channel_id=1, source_target_pairs={{0,1},{1,0},{2,3},{3,2},{4,5},{5,4},{6,7},{7,6},{8,9},{9,8},{10,11... | collective-permute-start | bytes 786440 | tf_op jit(solution)/shard_map/ppermute | solution.py:496
  90.8 22.9 %collective-permute-start.8 = (bf16[256,512]{1,0:T(8,128)(2,1)S(1)}, bf16[256,512]{1,0:T(8,128)(2,1)S(1)}, u32[]{:S(2)}, u32[]{:S(2)}) collective-permute-start(bf16[256,512]{1,0:T(8,128)(2,1)S(1)} %copy-done.31), channel_id=1, source_target_pairs={{0,2},{1,3},{2,0},{3,1},{4,6},{5,7},{6,4},{7,5},{8,10},{9,11},{10,... | collective-permute-start | bytes 786440 | tf_op jit(solution)/shard_map/ppermute | solution.py:496
  94.0 20.1 %collective-permute-start.9 = (bf16[256,512]{1,0:T(8,128)(2,1)S(1)}, bf16[256,512]{1,0:T(8,128)(2,1)S(1)}, u32[]{:S(2)}, u32[]{:S(2)}) collective-permute-start(bf16[256,512]{1,0:T(8,128)(2,1)S(1)} %copy-done.30), channel_id=1, source_target_pairs={{0,3},{1,2},{2,1},{3,0},{4,7},{5,6},{6,5},{7,4},{8,11},{9,10},{10,... | collective-permute-start | bytes 786440 | tf_op jit(solution)/shard_map/ppermute | solution.py:496
  113.7 14.1 %collective-permute-start.25 = (bf16[256,512]{1,0:T(8,128)(2,1)}, bf16[256,512]{1,0:T(8,128)(2,1)S(1)}, u32[]{:S(2)}, u32[]{:S(2)}) collective-permute-start(bf16[256,512]{1,0:T(8,128)(2,1)} %get-tuple-element.38), channel_id=1, source_target_pairs={{0,3},{1,2},{2,1},{3,0},{4,7},{5,6},{6,5},{7,4},{8,11},{9,10},{10,... | collective-permute-start | bytes 786440 | tf_op jit(solution)/shard_map/ppermute | solution.py:496
  117.2 16.6 %collective-permute-start.10 = (bf16[256,512]{1,0:T(8,128)(2,1)}, bf16[256,512]{1,0:T(8,128)(2,1)S(1)}, u32[]{:S(2)}, u32[]{:S(2)}) collective-permute-start(bf16[256,512]{1,0:T(8,128)(2,1)} %get-tuple-element.29.refs_1_), channel_id=1, source_target_pairs={{0,1},{1,0},{2,3},{3,2},{4,5},{5,4},{6,7},{7,6},{8,9},{9,8},{10,11... | collective-permute-start | bytes 786440 | tf_op jit(solution)/shard_map/ppermute | solution.py:496
  117.6 17.1 %collective-permute-start.11 = (bf16[256,512]{1,0:T(8,128)(2,1)}, bf16[256,512]{1,0:T(8,128)(2,1)S(1)}, u32[]{:S(2)}, u32[]{:S(2)}) collective-permute-start(bf16[256,512]{1,0:T(8,128)(2,1)} %get-tuple-element.29.refs_1_), channel_id=1, source_target_pairs={{0,2},{1,3},{2,0},{3,1},{4,6},{5,7},{6,4},{7,5},{8,10},{9,11},{10,... | collective-permute-start | bytes 786440 | tf_op jit(solution)/shard_map/ppermute | solution.py:496
  120.6 17.9 %collective-permute-start.12 = (bf16[256,512]{1,0:T(8,128)(2,1)}, bf16[256,512]{1,0:T(8,128)(2,1)S(1)}, u32[]{:S(2)}, u32[]{:S(2)}) collective-permute-start(bf16[256,512]{1,0:T(8,128)(2,1)} %get-tuple-element.29.refs_1_), channel_id=1, source_target_pairs={{0,3},{1,2},{2,1},{3,0},{4,7},{5,6},{6,5},{7,4},{8,11},{9,10},{10,... | collective-permute-start | bytes 786440 | tf_op jit(solution)/shard_map/ppermute | solution.py:496
  130.8 23.2 %collective-permute-start.26 = (bf16[288,512]{1,0:T(8,128)(2,1)}, bf16[288,512]{1,0:T(8,128)(2,1)S(1)}, u32[]{:S(2)}, u32[]{:S(2)}) collective-permute-start(bf16[288,512]{1,0:T(8,128)(2,1)} %get-tuple-element.40.refs_1_), channel_id=1, source_target_pairs={{0,1},{1,0},{2,3},{3,2},{4,5},{5,4},{6,7},{7,6},{8,9},{9,8},{10,11... | collective-permute-start | bytes 884744 | tf_op jit(solution)/shard_map/ppermute | solution.py:496
  131.0 23.0 %collective-permute-start.27 = (bf16[288,512]{1,0:T(8,128)(2,1)}, bf16[288,512]{1,0:T(8,128)(2,1)S(1)}, u32[]{:S(2)}, u32[]{:S(2)}) collective-permute-start(bf16[288,512]{1,0:T(8,128)(2,1)} %get-tuple-element.40.refs_1_), channel_id=1, source_target_pairs={{0,2},{1,3},{2,0},{3,1},{4,6},{5,7},{6,4},{7,5},{8,10},{9,11},{10,... | collective-permute-start | bytes 884744 | tf_op jit(solution)/shard_map/ppermute | solution.py:496
  133.7 20.3 %collective-permute-start.28 = (bf16[288,512]{1,0:T(8,128)(2,1)}, bf16[288,512]{1,0:T(8,128)(2,1)S(1)}, u32[]{:S(2)}, u32[]{:S(2)}) collective-permute-start(bf16[288,512]{1,0:T(8,128)(2,1)} %get-tuple-element.40.refs_1_), channel_id=1, source_target_pairs={{0,3},{1,2},{2,1},{3,0},{4,7},{5,6},{6,5},{7,4},{8,11},{9,10},{10,... | collective-permute-start | bytes 884744 | tf_op jit(solution)/shard_map/ppermute | solution.py:496
  153.8 22.8 %collective-permute-start.13 = (bf16[256,512]{1,0:T(8,128)(2,1)}, bf16[256,512]{1,0:T(8,128)(2,1)S(1)}, u32[]{:S(2)}, u32[]{:S(2)}) collective-permute-start(bf16[256,512]{1,0:T(8,128)(2,1)} %get-tuple-element.31), channel_id=1, source_target_pairs={{0,1},{1,0},{2,3},{3,2},{4,5},{5,4},{6,7},{7,6},{8,9},{9,8},{10,11... | collective-permute-start | bytes 786440 | tf_op jit(solution)/shard_map/ppermute | solution.py:496
  170.8 31.7 %collective-permute-start.29 = (bf16[272,512]{1,0:T(8,128)(2,1)}, bf16[272,512]{1,0:T(8,128)(2,1)S(1)}, u32[]{:S(2)}, u32[]{:S(2)}) collective-permute-start(bf16[272,512]{1,0:T(8,128)(2,1)} %get-tuple-element.43), channel_id=1, source_target_pairs={{0,1},{1,0},{2,3},{3,2},{4,5},{5,4},{6,7},{7,6},{8,9},{9,8},{10,11... | collective-permute-start | bytes 835592 | tf_op jit(solution)/shard_map/ppermute | solution.py:496
  172.2 30.3 %collective-permute-start.30 = (bf16[272,512]{1,0:T(8,128)(2,1)}, bf16[272,512]{1,0:T(8,128)(2,1)S(1)}, u32[]{:S(2)}, u32[]{:S(2)}) collective-permute-start(bf16[272,512]{1,0:T(8,128)(2,1)} %get-tuple-element.44), channel_id=1, source_target_pairs={{0,2},{1,3},{2,0},{3,1},{4,6},{5,7},{6,4},{7,5},{8,10},{9,11},{10,... | collective-permute-start | bytes 835592 | tf_op jit(solution)/shard_map/ppermute | solution.py:496
  174.1 28.4 %collective-permute-start.31 = (bf16[272,512]{1,0:T(8,128)(2,1)}, bf16[272,512]{1,0:T(8,128)(2,1)S(1)}, u32[]{:S(2)}, u32[]{:S(2)}) collective-permute-start(bf16[272,512]{1,0:T(8,128)(2,1)} %get-tuple-element.45), channel_id=1, source_target_pairs={{0,3},{1,2},{2,1},{3,0},{4,7},{5,6},{6,5},{7,4},{8,11},{9,10},{10,... | collective-permute-start | bytes 835592 | tf_op jit(solution)/shard_map/ppermute | solution.py:496
  174.7 16.9 %collective-permute-start.14 = (bf16[256,512]{1,0:T(8,128)(2,1)S(1)}, bf16[256,512]{1,0:T(8,128)(2,1)S(1)}, u32[]{:S(2)}, u32[]{:S(2)}) collective-permute-start(bf16[256,512]{1,0:T(8,128)(2,1)S(1)} %copy-done.34), channel_id=1, source_target_pairs={{0,2},{1,3},{2,0},{3,1},{4,6},{5,7},{6,4},{7,5},{8,10},{9,11},{10,... | collective-permute-start | bytes 786440 | tf_op jit(solution)/shard_map/ppermute | solution.py:496
  176.7 22.9 %collective-permute-start.15 = (bf16[256,512]{1,0:T(8,128)(2,1)S(1)}, bf16[256,512]{1,0:T(8,128)(2,1)S(1)}, u32[]{:S(2)}, u32[]{:S(2)}) collective-permute-start(bf16[256,512]{1,0:T(8,128)(2,1)S(1)} %copy-done.33), channel_id=1, source_target_pairs={{0,3},{1,2},{2,1},{3,0},{4,7},{5,6},{6,5},{7,4},{8,11},{9,10},{10,... | collective-permute-start | bytes 786440 | tf_op jit(solution)/shard_map/ppermute | solution.py:496
  (44 other events, 342.4 us)
Sparse Core Ops, SparseCore 0:
  10.3 90.9 all-gather.1
where the time goes:
time: 214 us; the launch traced here: 213 us
  Pallas kernels  69.4 us (32%)
  waiting for transfers between devices  67.9 us (32%)
  starting transfers between devices  45.3 us (21%)
  between operations  15 us (7%)
  local copies, waits for them, and re-layouts  11 us (5%)
  other arithmetic  4.17 us (2%)
    ppermute x32, waiting for transfers between devices, swap(): return lax.ppermute(value, axis, [(i, i ^ k) for i in range(SIZE[axis])])  67.9 us
    ppermute x32, starting transfers between devices, swap(): return lax.ppermute(value, axis, [(i, i ^ k) for i in range(SIZE[axis])])  45.2 us
    pallas_call x2, Pallas kernels, ffn_call(): pl.pallas_call(kernel, grid_spec=grid, out_shape=[shaped(rows, BLOCK, F32...  30 us
    pallas_call x1, Pallas kernels, prefill_call(): pl.pallas_call(prefill_kernel, grid_spec=grid, out_shape=jax.ShapeDtypeSt...  11.3 us
    pallas_call x2, Pallas kernels, project_call(): pl.pallas_call(kernel, grid_spec=grid, out_shape=out_shape, compiler_para...  9.11 us
    unnamed x78, local copies, waits for them, and re-layouts  7.92 us
    pallas_call x1, Pallas kernels, decode_call(): pl.pallas_call(decode_kernel, grid_spec=grid, out_shape=jax.ShapeDtypeStr...  6.76 us
    pallas_call x2, Pallas kernels, combine_call(): pl.pallas_call(combine_kernel, in_specs=[SM] + [VM] * (5 + len(late)), ou...  4.62 us
  transfers between devices with their start and end apart: 33, of which 11 were waited for; matrix products, arithmetic and copies ran while one was open for 3% of the time, Pallas kernels for 32%

commit v1 on v0

--- a/solution.py
+++ b/solution.py
@@ -26,7 +26,11 @@
 UNSEEN = -1e30
 NT = (((1,), (1,)), ((), ()))
 TN = (((0,), (0,)), ((), ()))
-VMEM_LIMIT = 58 * 1024 * 1024
+
+
+def limit(mib):
+    return pltpu.CompilerParams(vmem_limit_bytes=mib * 1024 * 1024)
+
 
 START, LENGTH, SLOT, AT_X, AT_Y, AT_CORE, AT_HEAD, OWNER = 0, 1, 4, 7, 8, 9, 10, 11
 
@@ -116,7 +120,7 @@
         prefill_kernel,
         grid_spec=grid,
         out_shape=jax.ShapeDtypeStruct((NEW, 4 * HEAD_SIZE), BF16),
-        compiler_params=pltpu.CompilerParams(vmem_limit_bytes=VMEM_LIMIT),
+        compiler_params=limit(32),
         cost_estimate=pl.CostEstimate(
             flops=4 * NEW * 4 * HEAD_SIZE * (CACHE + NEW),
             transcendentals=NEW * 4 * (CACHE + NEW),
@@ -205,7 +209,7 @@
         decode_kernel,
         grid_spec=grid,
         out_shape=jax.ShapeDtypeStruct((8, 2 * HEAD_SIZE), BF16),
-        compiler_params=pltpu.CompilerParams(vmem_limit_bytes=VMEM_LIMIT),
+        compiler_params=limit(16),
         cost_estimate=pl.CostEstimate(
             flops=3 * 4 * 256 * CACHE * 256, transcendentals=0, bytes_accessed=7 * 1024 * 1024
         ),
@@ -213,17 +217,8 @@
     )(info, piece, other, cache, cosine, sine)
 
 
-def project_rows(info, a_ref, w_ref, ps_ref, outs):
-    for k, out in enumerate(outs):
-        at = pl.multiple_of(lax.bitwise_xor(info[AT_HEAD], k) * BLOCK, BLOCK)
-        part = mm(a_ref[...], w_ref[pl.ds(at, BLOCK), :], NT)
-        if k == 0:
-            out[...] = part + ps_ref[...].astype(F32)
-        else:
-            out[...] = part.astype(BF16)
-
-
-def project_first(info, a_ref, ps_ref, w0_ref, w1_ref, own, o1, o2, o3, w_out):
+def project_kernel(info, a_ref, ps_ref, w0_ref, w1_ref, *outs):
+    own0, own1, w_out = outs[0], outs[4], outs[8]
     x, y, core = (info[i] for i in (AT_X, AT_Y, AT_CORE))
     for xi in range(4):
         for yi in range(4):
@@ -241,49 +236,38 @@
                 w_out[to : to + 64, :] = w1_ref[pl.ds(place, 64), :]
                 w_out[to + 64 : to + 128, :] = w0_ref[pl.ds(place, 64), :]
 
-    project_rows(info, a_ref, w_out, ps_ref, (own, o1, o2, o3))
-
-
-def project_second(info, a_ref, ps_ref, w_ref, own, o1, o2, o3):
-    project_rows(info, a_ref, w_ref, ps_ref, (own, o1, o2, o3))
+    for k in range(4):
+        at = pl.multiple_of(lax.bitwise_xor(info[AT_HEAD], k) * BLOCK, BLOCK)
+        part = mm(a_ref[...], w_out[pl.ds(at, BLOCK), :], NT)
+        if k == 0:
+            part = part + ps_ref[...].astype(F32)
+            own0[...] = part[:SPLIT, :]
+            own1[...] = part[SPLIT:, :]
+        else:
+            outs[k][...] = part[:SPLIT, :].astype(BF16)
+            outs[4 + k][...] = part[SPLIT:, :].astype(BF16)
 
 
 VM = pl.BlockSpec(memory_space=pltpu.VMEM)
 SM = pl.BlockSpec(memory_space=pltpu.SMEM)
-PARAMS = pltpu.CompilerParams(vmem_limit_bytes=VMEM_LIMIT)
 
 
 def shaped(rows, cols, dtype):
     return jax.ShapeDtypeStruct((rows, cols), dtype)
 
 
-def project_call(chunk, info, att, prefill_states, *weights):
-    rows = pl.BlockSpec((SPLIT, BLOCK), lambda i, s: (chunk, 0))
-    whole = pl.BlockSpec((SPLIT, BLOCK), lambda i, s: (0, 0))
-    full = pl.BlockSpec((WIDTH, BLOCK), lambda i, s: (0, 0))
-    if chunk == 0:
-        kernel, extra = project_first, [pl.BlockSpec((16 * PIECE, BLOCK), lambda i, s: (0, 0))] * 2
-    else:
-        kernel, extra = project_second, [full]
-    out_specs = [whole] * 4
-    out_shape = [shaped(SPLIT, BLOCK, F32)] + [shaped(SPLIT, BLOCK, BF16)] * 3
-    if chunk == 0:
-        out_specs.append(full)
-        out_shape.append(shaped(WIDTH, BLOCK, BF16))
-    grid = pltpu.PrefetchScalarGridSpec(
-        num_scalar_prefetch=1,
-        grid=(1,),
-        in_specs=[rows, rows] + extra,
-        out_specs=out_specs,
-    )
+def project_call(info, att, prefill_states, *weights):
+    half = [shaped(SPLIT, BLOCK, F32)] + [shaped(SPLIT, BLOCK, BF16)] * 3
     return pl.pallas_call(
-        kernel,
-        grid_spec=grid,
-        out_shape=out_shape,
-        compiler_params=PARAMS,
+        project_kernel,
+        in_specs=[SM] + [VM] * 4,
+        out_specs=[VM] * 9,
+        out_shape=half + half + [shaped(WIDTH, BLOCK, BF16)],
+        compiler_params=limit(20),
         cost_estimate=pl.CostEstimate(
-            flops=2 * SPLIT * BLOCK * WIDTH, transcendentals=0, bytes_accessed=6 * 1024 * 1024
+            flops=2 * NEW * BLOCK * WIDTH, transcendentals=0, bytes_accessed=6 * 1024 * 1024
         ),
+        name="project",
     )(info, att, prefill_states, *weights)
 
 
@@ -317,7 +301,7 @@
         out_specs=VM,
         out_shape=shaped(32, BLOCK, BF16),
         scratch_shapes=[pltpu.VMEM((EXTRA, BLOCK), BF16)],
-        compiler_params=PARAMS,
+        compiler_params=limit(10),
         name="return_rows",
     )(info, dec, w, states)
 
@@ -340,17 +324,17 @@
         in_specs=[SM] + [VM] * (5 + len(late)),
         out_specs=[VM] * 2,
         out_shape=[shaped(SPLIT, BLOCK, F32), shaped(sent, BLOCK, BF16)],
-        compiler_params=PARAMS,
+        compiler_params=limit(8),
     )(info, gain, *late, own, *parts)
 
 
-STEP = 512
-GATE_STEPS = HIDDEN // STEP
+STEP = 256
+STEPS = WIDTH // STEP
 
 
 def ffn_kernel(late, info, *refs):
-    parts, (gain_ref, wg, wu, wd) = refs[:4], refs[4:8]
-    outs, (n_sc, r_sc, h_sc) = refs[8:12], refs[-3:]
+    parts, (gain_ref, w_ref) = refs[:4], refs[4:6]
+    outs, (n_sc, r_sc, acc, d_sc, h_sc) = refs[6:10], refs[-5:]
     i = pl.program_id(0)
     head = info[AT_HEAD]
 
@@ -380,52 +364,55 @@
 
                 @pl.when(head == j)
                 def _():
-                    refs[12][...] = total
+                    refs[10][...] = total
 
             scale = lax.rsqrt(squares * (1.0 / WIDTH) + norm_eps)
             r_sc[SPLIT : SPLIT + 8, :] = jnp.broadcast_to(scale, (8, 128))
             r_sc[SPLIT + 8 :, :] = jnp.zeros((8, 128), F32)
 
-    @pl.when(i < GATE_STEPS)
+    at = pl.multiple_of(i * STEP, STEP)
+    product = mm(n_sc[:, pl.ds(at, STEP)], w_ref[:, : 2 * HIDDEN])
+    d_sc[pl.ds(at, STEP), :] = w_ref[:, 2 * HIDDEN :]
+
+    @pl.when(i == 0)
+    def _():
+        acc[...] = product
+
+    @pl.when(i > 0)
+    def _():
+        acc[...] = acc[...] + product
+
+    @pl.when(i == STEPS - 1)
     def _():
         scale = r_sc[:, :1]
-        gate = mm(n_sc[...], wg[...]) * scale
-        upper = mm(n_sc[...], wu[...]) * scale
-        hidden = (gate / (1.0 + jnp.exp(-gate)) * upper).astype(BF16)
-        h_sc[:, pl.ds(pl.multiple_of(i * STEP, STEP), STEP)] = hidden
-
-    for k, out in enumerate(outs):
-
-        @pl.when(i == GATE_STEPS + k)
-        def _():
-            out[...] = mm(h_sc[...], wd[...], NT).astype(out.dtype)
+        gate = acc[:, :HIDDEN] * scale
+        upper = acc[:, HIDDEN:] * scale
+        h_sc[...] = (gate / (1.0 + jnp.exp(-gate)) * upper).astype(BF16)
+        for k, out in enumerate(outs):
+            block = pl.multiple_of(lax.bitwise_xor(head, k) * BLOCK, BLOCK)
+            out[...] = mm(h_sc[...], d_sc[pl.ds(block, BLOCK), :], NT).astype(out.dtype)
 
 
 def ffn_call(late, info, parts, gain, weights):
     rows = SPLIT + EXTRA * late
     sent = SPLIT + 32 * late
-    last = GATE_STEPS - 1
-
-    def down_map(i, s):
-        return (lax.bitwise_xor(s[AT_HEAD], jnp.maximum(i - GATE_STEPS, 0)), 2)
-
     whole = pl.BlockSpec((sent, BLOCK), lambda i, s: (0, 0))
     out = pl.BlockSpec((rows, BLOCK), lambda i, s: (0, 0))
     small = pl.BlockSpec((8, BLOCK), lambda i, s: (0, 0))
     grid = pltpu.PrefetchScalarGridSpec(
         num_scalar_prefetch=1,
-        grid=(GATE_STEPS + 4,),
+        grid=(STEPS,),
         in_specs=[whole] * 4
         + [
             pl.BlockSpec((1, WIDTH), lambda i, s: (0, 0)),
-            pl.BlockSpec((WIDTH, STEP), lambda i, s: (0, jnp.minimum(i, last))),
-            pl.BlockSpec((WIDTH, STEP), lambda i, s: (0, GATE_STEPS + jnp.minimum(i, last))),
-            pl.BlockSpec((BLOCK, HIDDEN), down_map),
+            pl.BlockSpec((STEP, 3 * HIDDEN), lambda i, s: (i, 0)),
         ],
         out_specs=[out] * 4 + [small] * late,
         scratch_shapes=[
             pltpu.VMEM((rows, WIDTH), BF16),
             pltpu.VMEM((rows, 128), F32),
+            pltpu.VMEM((rows, 2 * HIDDEN), F32),
+            pltpu.VMEM((WIDTH, HIDDEN), BF16),
             pltpu.VMEM((rows, HIDDEN), BF16),
         ],
     )
@@ -439,13 +426,13 @@
         out_shape=[shaped(rows, BLOCK, F32)]
         + [shaped(rows, BLOCK, BF16)] * 3
         + [shaped(8, BLOCK, F32)] * late,
-        compiler_params=PARAMS,
+        compiler_params=limit(32),
         cost_estimate=pl.CostEstimate(
             flops=6 * rows * HIDDEN * WIDTH,
             transcendentals=rows * HIDDEN,
             bytes_accessed=20 * 1024 * 1024,
         ),
-    )(info, *parts, gain, weights, weights, weights)
+    )(info, *parts, gain, pltpu.with_memory_space_constraint(weights, pltpu.HBM))
 
 
 def finish_first(s_ref, own, r1, r2, r3, p_ref):
@@ -474,7 +461,7 @@
             in_specs=in_specs,
             out_specs=first,
             out_shape=shaped(NEW, BLOCK, BF16),
-            compiler_params=PARAMS,
+            compiler_params=limit(6),
             name="finish_0",
         )(summed, own, *parts)
     return pl.pallas_call(
@@ -484,7 +471,7 @@
         out_specs=[first, block(3)],
         out_shape=[shaped(NEW, BLOCK, BF16), shaped(3, BLOCK, BF16)],
         input_output_aliases={0: 0},
-        compiler_params=PARAMS,
+        compiler_params=limit(6),
         name="finish_1",
     )(old, summed, late, own, *parts)
 
@@ -498,8 +485,10 @@
 
 def spread(value):
     for axis in ("y", "x"):
+        value = lax.optimization_barrier(value)
         others = [swap(value, axis, k) for k in (1, 2, 3)]
         value = jnp.concatenate([value] + others, axis=0)
+    value = lax.optimization_barrier(value)
     return value, swap(value, "core", 1)
 
 
@@ -565,10 +554,11 @@
     def shared(value):
         return [value] + [swap(value, "head", k) for k in (1, 2, 3)]
 
-    own0, *parts0, w_all = project_call(0, info, att, prefill_states, piece, other)
-    parts0 = exchanged(parts0)
-    own1, *parts1 = project_call(1, info, att, prefill_states, w_all)
-    parts1 = exchanged(parts1)
+    own0, q1, q2, q3, own1, p1, p2, p3, w_all = project_call(
+        info, att, prefill_states, piece, other
+    )
+    parts0 = exchanged([q1, q2, q3])
+    parts1 = exchanged([p1, p2, p3])
 
     decoded = decode_call(info, *both, decode_cache, cosine, sine)
     decoded = jnp.concatenate(spread(decoded), axis=0)

time: 214 us -> 193 us (0.902)
  Pallas kernels: 69.4 us -> 48.4 us
  waiting for transfers between devices: 67.9 us -> 76.5 us
  local copies, waits for them, and re-layouts: 11 us -> 3.04 us
    ppermute x32, waiting for transfers between devices: 67.9 us -> 76.5 us  [swap(): return lax.ppermute(value, axis, [(i, i ^ k) for i in range(SIZE[axis])])]
    pallas_call x2 -> x1, Pallas kernels: 9.11 us -> 2.07 us  [project_call(): pl.pallas_call(project_kernel, in_specs=[SM] + [VM] * 4, out_specs=[VM] *...]
    unnamed x78 -> x26, local copies, waits for them, and re-layouts: 7.92 us -> 2.73 us
    pallas_call x2, Pallas kernels: 4.62 us -> 1.39 us  [combine_call(): pl.pallas_call(combine_kernel, in_specs=[SM] + [VM] * (5 + len(late)), ou...]
    pallas_call x1, Pallas kernels: 6.76 us -> 3.77 us  [decode_call(): pl.pallas_call(decode_kernel, grid_spec=grid, out_shape=jax.ShapeDtypeStr...]
    pallas_call x1, Pallas kernels: 11.3 us -> 8.61 us  [prefill_call(): pl.pallas_call(prefill_kernel, grid_spec=grid, out_shape=jax.ShapeDtypeSt...]
  transfers between devices with their start and end apart: 33 -> 33, of which waited for: 11 -> 13; matrix products, arithmetic and copies ran while one was open for 3% -> 2% of each run, Pallas kernels for 32% -> 25%
where the time goes in v1:
time: 193 us; the launch traced here: 192 us
  waiting for transfers between devices  76.5 us (40%)
  Pallas kernels  48.4 us (25%)
  starting transfers between devices  45.3 us (23%)
  between operations  15 us (8%)
  other arithmetic  3.42 us (2%)
  local copies, waits for them, and re-layouts  3.04 us (2%)
    ppermute x32, waiting for transfers between devices, swap(): return lax.ppermute(value, axis, [(i, i ^ k) for i in range(SIZE[axis])])  76.5 us
    ppermute x32, starting transfers between devices, swap(): return lax.ppermute(value, axis, [(i, i ^ k) for i in range(SIZE[axis])])  45.2 us
    pallas_call x2, Pallas kernels, ffn_call(): pl.pallas_call(kernel, grid_spec=grid, out_shape=[shaped(rows, BLOCK, F32...  29.5 us
    pallas_call x1, Pallas kernels, prefill_call(): pl.pallas_call(prefill_kernel, grid_spec=grid, out_shape=jax.ShapeDtypeSt...  8.61 us
  transfers between devices with their start and end apart: 33, of which 13 were waited for; matrix products, arithmetic and copies ran while one was open for 2% of the time, Pallas kernels for 25%

profile of v1, /device:TPU:1, one launch (start us, length us, event | category | flops | bytes accessed | tf_op | source)
XLA Modules:
  0.0 191.6 jit_solution(5010291756133587198)
XLA Ops:
  9.5 2.2 %collective-permute-start = (bf16[80,512]{1,0:T(8,128)(2,1)S(1)}, bf16[80,512]{1,0:T(8,128)(2,1)S(1)}, u32[]{:S(2)}, u32[]{:S(2)}) collective-permute-start(bf16[80,512]{1,0:T(8,128)(2,1)S(1)} %concatenate.44), channel_id=1, source_target_pairs={{0,8},{8,0},{16,24},{24,16},{1,9},{9,1},{17,25},{25,17},{2,10},{10... | collective-permute-start | bytes 245768 | tf_op jit(solution)/shard_map/ppermute | solution.py:483
  11.7 2.6 %collective-permute-start.1 = (bf16[80,512]{1,0:T(8,128)(2,1)S(1)}, bf16[80,512]{1,0:T(8,128)(2,1)S(1)}, u32[]{:S(2)}, u32[]{:S(2)}) collective-permute-start(bf16[80,512]{1,0:T(8,128)(2,1)S(1)} %concatenate.44), channel_id=1, source_target_pairs={{0,16},{8,24},{16,0},{24,8},{1,17},{9,25},{17,1},{25,9},{2,18},{10... | collective-permute-start | bytes 245768 | tf_op jit(solution)/shard_map/ppermute | solution.py:483
  14.3 3.3 %collective-permute-done.1 = bf16[80,512]{1,0:T(8,128)(2,1)S(1)} collective-permute-done((bf16[80,512]{1,0:T(8,128)(2,1)S(1)}, bf16[80,512]{1,0:T(8,128)(2,1)S(1)}, u32[]{:S(2)}, u32[]{:S(2)}) %collective-permute-start.1) | collective-permute-done | bytes 81952 | tf_op jit(solution)/shard_map/ppermute | solution.py:483
  17.7 2.3 %collective-permute-done.2 = bf16[80,512]{1,0:T(8,128)(2,1)S(1)} collective-permute-done((bf16[80,512]{1,0:T(8,128)(2,1)S(1)}, bf16[80,512]{1,0:T(8,128)(2,1)S(1)}, u32[]{:S(2)}, u32[]{:S(2)}) %collective-permute-start.2) | collective-permute-done | bytes 81952 | tf_op jit(solution)/shard_map/ppermute | solution.py:483
  21.3 2.5 %collective-permute-start.4 = (bf16[320,512]{1,0:T(8,128)(2,1)S(1)}, bf16[320,512]{1,0:T(8,128)(2,1)S(1)}, u32[]{:S(2)}, u32[]{:S(2)}) collective-permute-start(bf16[320,512]{1,0:T(8,128)(2,1)S(1)} %pad_maximum_fusion.2), channel_id=1, source_target_pairs={{0,64},{32,96},{64,0},{96,32},{1,65},{33,97},{65,1},{97,33},{2,66}... | collective-permute-start | bytes 983048 | tf_op jit(solution)/shard_map/ppermute | solution.py:483
  24.0 5.8 %collective-permute-done.3 = bf16[320,512]{1,0:T(8,128)(2,1)S(1)} collective-permute-done((bf16[320,512]{1,0:T(8,128)(2,1)S(1)}, bf16[320,512]{1,0:T(8,128)(2,1)S(1)}, u32[]{:S(2)}, u32[]{:S(2)}) %collective-permute-start.3) | collective-permute-done | bytes 327712 | tf_op jit(solution)/shard_map/ppermute | solution.py:483
  29.8 16.8 %collective-permute-done.4 = bf16[320,512]{1,0:T(8,128)(2,1)S(1)} collective-permute-done((bf16[320,512]{1,0:T(8,128)(2,1)S(1)}, bf16[320,512]{1,0:T(8,128)(2,1)S(1)}, u32[]{:S(2)}, u32[]{:S(2)}) %collective-permute-start.4) | collective-permute-done | bytes 327712 | tf_op jit(solution)/shard_map/ppermute | solution.py:483
  46.7 4.3 %collective-permute-start.6 = (bf16[1280,512]{1,0:T(8,128)(2,1)S(1)}, bf16[1280,512]{1,0:T(8,128)(2,1)S(1)}, u32[]{:S(2)}, u32[]{:S(2)}) collective-permute-start(bf16[1280,512]{1,0:T(8,128)(2,1)S(1)} %pad_maximum_fusion.w0_ref), channel_id=1, source_target_pairs={{0,4},{4,0},{1,5},{5,1},{2,6},{6,2},{3,7},{7,3},{8,12},{12,8},{9,1... | collective-permute-start | bytes 3932168 | tf_op jit(solution)/shard_map/ppermute | solution.py:483
  55.7 8.6 %prefill_attention.1.a_ref = bf16[512,512]{1,0:T(8,128)(2,1)S(1)} custom-call(s32[12]{0:T(128)S(1)} %concatenate.39.info.refs_0_, bf16[512,512]{1,0:T(8,128)(2,1)S(1)} %copy-done.1, bf16[512,512]{1,0:T(8,128)(2,1)S(1)} %bitcast.19, bf16[512,512]{1,0:T(8,128)(2,1)S(1)} %bitcast.20, bf16[1,2,2048,256]{3,2,1,0:T(8,128)(2,1)S(1)} %copy-done, ...), custom_call_target="tpu_custom_call" | custom-call | flops 2684354560 | bytes 4194304 | tf_op jit(solution)/shard_map/prefill_attention/pallas_call | solution.py:119
  64.4 3.8 %decode_attention.1 = bf16[8,256]{1,0:T(8,128)(2,1)S(1)} custom-call(s32[12]{0:T(128)S(1)} %concatenate.39.info.refs_0_, bf16[16,80,512]{2,1,0:T(8,128)(2,1)S(1)} %bitcast.17, bf16[16,80,512]{2,1,0:T(8,128)(2,1)S(1)} %bitcast.18, bf16[3,2,2048,256]{3,2,1,0:T(8,128)(2,1)S(1)} %bitcast.16, f32[520,128]{1,0:T(8,128)S(1)} %get-tuple-element.49.cos_ref, ...), custom_call_target="tpu_custom_call" | custom-call | flops 1610612736 | bytes 7340032 | tf_op jit(solution)/shard_map/decode_attention/pallas_call | solution.py:208
  68.8 3.3 %collective-permute-start.18 = (bf16[8,256]{1,0:T(8,128)(2,1)S(1)}, bf16[8,256]{1,0:T(8,128)(2,1)S(1)}, u32[]{:S(2)}, u32[]{:S(2)}) collective-permute-start(bf16[8,256]{1,0:T(8,128)(2,1)S(1)} %decode_attention.1), channel_id=1, source_target_pairs={{0,24},{8,16},{16,8},{24,0},{1,25},{9,17},{17,9},{25,1},{2,26},{10... | collective-permute-start | bytes 12296 | tf_op jit(solution)/shard_map/ppermute | solution.py:483
  76.3 3.3 %collective-permute-start.8 = (bf16[256,512]{1,0:T(8,128)(2,1)S(1)}, bf16[256,512]{1,0:T(8,128)(2,1)S(1)}, u32[]{:S(2)}, u32[]{:S(2)}) collective-permute-start(bf16[256,512]{1,0:T(8,128)(2,1)S(1)} %get-tuple-element.26), channel_id=1, source_target_pairs={{0,2},{1,3},{2,0},{3,1},{4,6},{5,7},{6,4},{7,5},{8,10},{9,11},{10,... | collective-permute-start | bytes 786440 | tf_op jit(solution)/shard_map/ppermute | solution.py:483
  80.1 3.5 %collective-permute-done.19 = bf16[32,256]{1,0:T(8,128)(2,1)S(1)} collective-permute-done((bf16[32,256]{1,0:T(8,128)(2,1)S(1)}, bf16[32,256]{1,0:T(8,128)(2,1)S(1)}, u32[]{:S(2)}, u32[]{:S(2)}) %collective-permute-start.19) | collective-permute-done | bytes 16416 | tf_op jit(solution)/shard_map/ppermute | solution.py:483
  83.5 4.6 %collective-permute-done.20 = bf16[32,256]{1,0:T(8,128)(2,1)S(1)} collective-permute-done((bf16[32,256]{1,0:T(8,128)(2,1)S(1)}, bf16[32,256]{1,0:T(8,128)(2,1)S(1)}, u32[]{:S(2)}, u32[]{:S(2)}) %collective-permute-start.20) | collective-permute-done | bytes 16416 | tf_op jit(solution)/shard_map/ppermute | solution.py:483
  88.3 4.6 %collective-permute-done.21 = bf16[32,256]{1,0:T(8,128)(2,1)S(1)} collective-permute-done((bf16[32,256]{1,0:T(8,128)(2,1)S(1)}, bf16[32,256]{1,0:T(8,128)(2,1)S(1)}, u32[]{:S(2)}, u32[]{:S(2)}) %collective-permute-start.21) | collective-permute-done | bytes 16416 | tf_op jit(solution)/shard_map/ppermute | solution.py:483
  92.9 5.3 %collective-permute-start.22 = (bf16[128,256]{1,0:T(8,128)(2,1)S(1)}, bf16[128,256]{1,0:T(8,128)(2,1)S(1)}, u32[]{:S(2)}, u32[]{:S(2)}) collective-permute-start(bf16[128,256]{1,0:T(8,128)(2,1)S(1)} %pad_maximum_fusion.6), channel_id=1, source_target_pairs={{0,4},{4,0},{1,5},{5,1},{2,6},{6,2},{3,7},{7,3},{8,12},{12,8},{9,1... | collective-permute-start | bytes 196616 | tf_op jit(solution)/shard_map/ppermute | solution.py:483
  101.9 3.0 %collective-permute-start.11 = (bf16[256,512]{1,0:T(8,128)(2,1)S(1)}, bf16[256,512]{1,0:T(8,128)(2,1)S(1)}, u32[]{:S(2)}, u32[]{:S(2)}) collective-permute-start(bf16[256,512]{1,0:T(8,128)(2,1)S(1)} %get-tuple-element.29.refs_1_), channel_id=1, source_target_pairs={{0,2},{1,3},{2,0},{3,1},{4,6},{5,7},{6,4},{7,5},{8,10},{9,11},{10,... | collective-permute-start | bytes 786440 | tf_op jit(solution)/shard_map/ppermute | solution.py:483
  107.7 6.3 %collective-permute-done.25.refs_4_ = bf16[256,512]{1,0:T(8,128)(2,1)S(1)} collective-permute-done((bf16[256,512]{1,0:T(8,128)(2,1)S(1)}, bf16[256,512]{1,0:T(8,128)(2,1)S(1)}, u32[]{:S(2)}, u32[]{:S(2)}) %collective-permute-start.25) | collective-permute-done | bytes 262176 | tf_op jit(solution)/shard_map/ppermute | solution.py:483
  114.8 2.9 %collective-permute-start.27 = (bf16[288,512]{1,0:T(8,128)(2,1)S(1)}, bf16[288,512]{1,0:T(8,128)(2,1)S(1)}, u32[]{:S(2)}, u32[]{:S(2)}) collective-permute-start(bf16[288,512]{1,0:T(8,128)(2,1)S(1)} %get-tuple-element.40.refs_1_), channel_id=1, source_target_pairs={{0,2},{1,3},{2,0},{3,1},{4,6},{5,7},{6,4},{7,5},{8,10},{9,11},{10,... | collective-permute-start | bytes 884744 | tf_op jit(solution)/shard_map/ppermute | solution.py:483
  119.0 6.2 %collective-permute-done.12.refs_4_ = bf16[256,512]{1,0:T(8,128)(2,1)S(1)} collective-permute-done((bf16[256,512]{1,0:T(8,128)(2,1)S(1)}, bf16[256,512]{1,0:T(8,128)(2,1)S(1)}, u32[]{:S(2)}, u32[]{:S(2)}) %collective-permute-start.12) | collective-permute-done | bytes 262176 | tf_op jit(solution)/shard_map/ppermute | solution.py:483
  125.2 14.4 %shard_map.168 = (f32[256,512]{1,0:T(8,128)S(1)}, bf16[256,512]{1,0:T(8,128)(2,1)S(1)}, bf16[256,512]{1,0:T(8,128)(2,1)S(1)}, bf16[256,512]{1,0:T(8,128)(2,1)S(1)}) custom-call(s32[12]{0:T(128)S(1)} %concatenate.39.info.refs_0_, bf16[256,512]{1,0:T(8,128)(2,1)S(1)} %get-tuple-element.29.refs_1_, bf16[256,512]{1,0:T(8,128)(2,1)S(1)} %collective-permute-done.10.refs_2_, ...), custom_call_target="tpu_custom_call" | custom-call | flops 4831838208 | bytes 20971520 | tf_op jit(solution)/shard_map/pallas_call | solution.py:423
  139.7 15.0 %shard_map.170 = (f32[272,512]{1,0:T(8,128)S(1)}, bf16[272,512]{1,0:T(8,128)(2,1)S(1)}, bf16[272,512]{1,0:T(8,128)(2,1)S(1)}, bf16[272,512]{1,0:T(8,128)(2,1)S(1)}, f32[8,512]{1,0:T(8,128)S(1)}) custom-call(s32[12]{0:T(128)S(1)} %concatenate.39.info.refs_0_, bf16[288,512]{1,0:T(8,128)(2,1)S(1)} %get-tuple-element.40.refs_1_, ...), custom_call_target="tpu_custom_call" | custom-call | flops 5133828096 | bytes 20971520 | tf_op jit(solution)/shard_map/pallas_call | solution.py:423
  161.3 13.8 %collective-permute-done.14.r2 = bf16[256,512]{1,0:T(8,128)(2,1)S(1)} collective-permute-done((bf16[256,512]{1,0:T(8,128)(2,1)S(1)}, bf16[256,512]{1,0:T(8,128)(2,1)S(1)}, u32[]{:S(2)}, u32[]{:S(2)}) %collective-permute-start.14) | collective-permute-done | bytes 262176 | tf_op jit(solution)/shard_map/ppermute | solution.py:483
  175.1 7.9 %collective-permute-done.15.r3 = bf16[256,512]{1,0:T(8,128)(2,1)S(1)} collective-permute-done((bf16[256,512]{1,0:T(8,128)(2,1)S(1)}, bf16[256,512]{1,0:T(8,128)(2,1)S(1)}, u32[]{:S(2)}, u32[]{:S(2)}) %collective-permute-start.15) | collective-permute-done | bytes 262176 | tf_op jit(solution)/shard_map/ppermute | solution.py:483
  (101 shorter events, 30.3 us)
Async XLA Ops:
  7.2 118.0 %all-gather.2.cloned.1.call-start = ((), (), s32[]{:S(2)}) async-start(), calls=%async_computation | async-start | bytes 19464192 | tf_op jit(solution)/shard_map/all_gather | solution.py:520
  20.0 9.7 %collective-permute-start.3 = (bf16[320,512]{1,0:T(8,128)(2,1)S(1)}, bf16[320,512]{1,0:T(8,128)(2,1)S(1)}, u32[]{:S(2)}, u32[]{:S(2)}) collective-permute-start(bf16[320,512]{1,0:T(8,128)(2,1)S(1)} %pad_maximum_fusion.2), channel_id=1, source_target_pairs={{0,32},{32,0},{64,96},{96,64},{1,33},{33,1},{65,97},{97,65},{2,34}... | collective-permute-start | bytes 983048 | tf_op jit(solution)/shard_map/ppermute | solution.py:483
  21.3 25.3 %collective-permute-start.4 = (bf16[320,512]{1,0:T(8,128)(2,1)S(1)}, bf16[320,512]{1,0:T(8,128)(2,1)S(1)}, u32[]{:S(2)}, u32[]{:S(2)}) collective-permute-start(bf16[320,512]{1,0:T(8,128)(2,1)S(1)} %pad_maximum_fusion.2), channel_id=1, source_target_pairs={{0,64},{32,96},{64,0},{96,32},{1,65},{33,97},{65,1},{97,33},{2,66}... | collective-permute-start | bytes 983048 | tf_op jit(solution)/shard_map/ppermute | solution.py:483
  23.8 22.8 %collective-permute-start.5 = (bf16[320,512]{1,0:T(8,128)(2,1)S(1)}, bf16[320,512]{1,0:T(8,128)(2,1)S(1)}, u32[]{:S(2)}, u32[]{:S(2)}) collective-permute-start(bf16[320,512]{1,0:T(8,128)(2,1)S(1)} %pad_maximum_fusion.2), channel_id=1, source_target_pairs={{0,96},{32,64},{64,32},{96,0},{1,97},{33,65},{65,33},{97,1},{2,98}... | collective-permute-start | bytes 983048 | tf_op jit(solution)/shard_map/ppermute | solution.py:483
  46.7 17.7 %collective-permute-start.6 = (bf16[1280,512]{1,0:T(8,128)(2,1)S(1)}, bf16[1280,512]{1,0:T(8,128)(2,1)S(1)}, u32[]{:S(2)}, u32[]{:S(2)}) collective-permute-start(bf16[1280,512]{1,0:T(8,128)(2,1)S(1)} %pad_maximum_fusion.w0_ref), channel_id=1, source_target_pairs={{0,4},{4,0},{1,5},{5,1},{2,6},{6,2},{3,7},{7,3},{8,12},{12,8},{9,1... | collective-permute-start | bytes 3932168 | tf_op jit(solution)/shard_map/ppermute | solution.py:483
  68.3 11.3 %collective-permute-start.17 = (bf16[8,256]{1,0:T(8,128)(2,1)S(1)}, bf16[8,256]{1,0:T(8,128)(2,1)S(1)}, u32[]{:S(2)}, u32[]{:S(2)}) collective-permute-start(bf16[8,256]{1,0:T(8,128)(2,1)S(1)} %decode_attention.1), channel_id=1, source_target_pairs={{0,16},{8,24},{16,0},{24,8},{1,17},{9,25},{17,1},{25,9},{2,18},{10... | collective-permute-start | bytes 12296 | tf_op jit(solution)/shard_map/ppermute | solution.py:483
  68.8 11.2 %collective-permute-start.18 = (bf16[8,256]{1,0:T(8,128)(2,1)S(1)}, bf16[8,256]{1,0:T(8,128)(2,1)S(1)}, u32[]{:S(2)}, u32[]{:S(2)}) collective-permute-start(bf16[8,256]{1,0:T(8,128)(2,1)S(1)} %decode_attention.1), channel_id=1, source_target_pairs={{0,24},{8,16},{16,8},{24,0},{1,25},{9,17},{17,9},{25,1},{2,26},{10... | collective-permute-start | bytes 12296 | tf_op jit(solution)/shard_map/ppermute | solution.py:483
  74.2 30.6 %collective-permute-start.23 = (bf16[256,512]{1,0:T(8,128)(2,1)S(1)}, bf16[256,512]{1,0:T(8,128)(2,1)S(1)}, u32[]{:S(2)}, u32[]{:S(2)}) collective-permute-start(bf16[256,512]{1,0:T(8,128)(2,1)S(1)} %get-tuple-element.36), channel_id=1, source_target_pairs={{0,1},{1,0},{2,3},{3,2},{4,5},{5,4},{6,7},{7,6},{8,9},{9,8},{10,11... | collective-permute-start | bytes 786440 | tf_op jit(solution)/shard_map/ppermute | solution.py:483
  76.2 22.0 %collective-permute-start.7 = (bf16[256,512]{1,0:T(8,128)(2,1)S(1)}, bf16[256,512]{1,0:T(8,128)(2,1)S(1)}, u32[]{:S(2)}, u32[]{:S(2)}) collective-permute-start(bf16[256,512]{1,0:T(8,128)(2,1)S(1)} %get-tuple-element.25), channel_id=1, source_target_pairs={{0,1},{1,0},{2,3},{3,2},{4,5},{5,4},{6,7},{7,6},{8,9},{9,8},{10,11... | collective-permute-start | bytes 786440 | tf_op jit(solution)/shard_map/ppermute | solution.py:483
  76.3 23.9 %collective-permute-start.8 = (bf16[256,512]{1,0:T(8,128)(2,1)S(1)}, bf16[256,512]{1,0:T(8,128)(2,1)S(1)}, u32[]{:S(2)}, u32[]{:S(2)}) collective-permute-start(bf16[256,512]{1,0:T(8,128)(2,1)S(1)} %get-tuple-element.26), channel_id=1, source_target_pairs={{0,2},{1,3},{2,0},{3,1},{4,6},{5,7},{6,4},{7,5},{8,10},{9,11},{10,... | collective-permute-start | bytes 786440 | tf_op jit(solution)/shard_map/ppermute | solution.py:483
  79.5 21.2 %collective-permute-start.9 = (bf16[256,512]{1,0:T(8,128)(2,1)S(1)}, bf16[256,512]{1,0:T(8,128)(2,1)S(1)}, u32[]{:S(2)}, u32[]{:S(2)}) collective-permute-start(bf16[256,512]{1,0:T(8,128)(2,1)S(1)} %get-tuple-element.27), channel_id=1, source_target_pairs={{0,3},{1,2},{2,1},{3,0},{4,7},{5,6},{6,5},{7,4},{8,11},{9,10},{10,... | collective-permute-start | bytes 786440 | tf_op jit(solution)/shard_map/ppermute | solution.py:483
  100.2 13.8 %collective-permute-start.25 = (bf16[256,512]{1,0:T(8,128)(2,1)S(1)}, bf16[256,512]{1,0:T(8,128)(2,1)S(1)}, u32[]{:S(2)}, u32[]{:S(2)}) collective-permute-start(bf16[256,512]{1,0:T(8,128)(2,1)S(1)} %get-tuple-element.38), channel_id=1, source_target_pairs={{0,3},{1,2},{2,1},{3,0},{4,7},{5,6},{6,5},{7,4},{8,11},{9,10},{10,... | collective-permute-start | bytes 786440 | tf_op jit(solution)/shard_map/ppermute | solution.py:483
  101.4 16.4 %collective-permute-start.10 = (bf16[256,512]{1,0:T(8,128)(2,1)S(1)}, bf16[256,512]{1,0:T(8,128)(2,1)S(1)}, u32[]{:S(2)}, u32[]{:S(2)}) collective-permute-start(bf16[256,512]{1,0:T(8,128)(2,1)S(1)} %get-tuple-element.29.refs_1_), channel_id=1, source_target_pairs={{0,1},{1,0},{2,3},{3,2},{4,5},{5,4},{6,7},{7,6},{8,9},{9,8},{10,11... | collective-permute-start | bytes 786440 | tf_op jit(solution)/shard_map/ppermute | solution.py:483
  101.9 17.1 %collective-permute-start.11 = (bf16[256,512]{1,0:T(8,128)(2,1)S(1)}, bf16[256,512]{1,0:T(8,128)(2,1)S(1)}, u32[]{:S(2)}, u32[]{:S(2)}) collective-permute-start(bf16[256,512]{1,0:T(8,128)(2,1)S(1)} %get-tuple-element.29.refs_1_), channel_id=1, source_target_pairs={{0,2},{1,3},{2,0},{3,1},{4,6},{5,7},{6,4},{7,5},{8,10},{9,11},{10,... | collective-permute-start | bytes 786440 | tf_op jit(solution)/shard_map/ppermute | solution.py:483
  104.8 20.3 %collective-permute-start.12 = (bf16[256,512]{1,0:T(8,128)(2,1)S(1)}, bf16[256,512]{1,0:T(8,128)(2,1)S(1)}, u32[]{:S(2)}, u32[]{:S(2)}) collective-permute-start(bf16[256,512]{1,0:T(8,128)(2,1)S(1)} %get-tuple-element.29.refs_1_), channel_id=1, source_target_pairs={{0,3},{1,2},{2,1},{3,0},{4,7},{5,6},{6,5},{7,4},{8,11},{9,10},{10,... | collective-permute-start | bytes 786440 | tf_op jit(solution)/shard_map/ppermute | solution.py:483
  114.7 25.0 %collective-permute-start.26 = (bf16[288,512]{1,0:T(8,128)(2,1)S(1)}, bf16[288,512]{1,0:T(8,128)(2,1)S(1)}, u32[]{:S(2)}, u32[]{:S(2)}) collective-permute-start(bf16[288,512]{1,0:T(8,128)(2,1)S(1)} %get-tuple-element.40.refs_1_), channel_id=1, source_target_pairs={{0,1},{1,0},{2,3},{3,2},{4,5},{5,4},{6,7},{7,6},{8,9},{9,8},{10,11... | collective-permute-start | bytes 884744 | tf_op jit(solution)/shard_map/ppermute | solution.py:483
  114.8 24.9 %collective-permute-start.27 = (bf16[288,512]{1,0:T(8,128)(2,1)S(1)}, bf16[288,512]{1,0:T(8,128)(2,1)S(1)}, u32[]{:S(2)}, u32[]{:S(2)}) collective-permute-start(bf16[288,512]{1,0:T(8,128)(2,1)S(1)} %get-tuple-element.40.refs_1_), channel_id=1, source_target_pairs={{0,2},{1,3},{2,0},{3,1},{4,6},{5,7},{6,4},{7,5},{8,10},{9,11},{10,... | collective-permute-start | bytes 884744 | tf_op jit(solution)/shard_map/ppermute | solution.py:483
  117.8 22.0 %collective-permute-start.28 = (bf16[288,512]{1,0:T(8,128)(2,1)S(1)}, bf16[288,512]{1,0:T(8,128)(2,1)S(1)}, u32[]{:S(2)}, u32[]{:S(2)}) collective-permute-start(bf16[288,512]{1,0:T(8,128)(2,1)S(1)} %get-tuple-element.40.refs_1_), channel_id=1, source_target_pairs={{0,3},{1,2},{2,1},{3,0},{4,7},{5,6},{6,5},{7,4},{8,11},{9,10},{10,... | collective-permute-start | bytes 884744 | tf_op jit(solution)/shard_map/ppermute | solution.py:483
  139.6 20.8 %collective-permute-start.13 = (bf16[256,512]{1,0:T(8,128)(2,1)S(1)}, bf16[256,512]{1,0:T(8,128)(2,1)S(1)}, u32[]{:S(2)}, u32[]{:S(2)}) collective-permute-start(bf16[256,512]{1,0:T(8,128)(2,1)S(1)} %get-tuple-element.31), channel_id=1, source_target_pairs={{0,1},{1,0},{2,3},{3,2},{4,5},{5,4},{6,7},{7,6},{8,9},{9,8},{10,11... | collective-permute-start | bytes 786440 | tf_op jit(solution)/shard_map/ppermute | solution.py:483
  154.8 29.1 %collective-permute-start.29 = (bf16[272,512]{1,0:T(8,128)(2,1)S(1)}, bf16[272,512]{1,0:T(8,128)(2,1)S(1)}, u32[]{:S(2)}, u32[]{:S(2)}) collective-permute-start(bf16[272,512]{1,0:T(8,128)(2,1)S(1)} %get-tuple-element.43), channel_id=1, source_target_pairs={{0,1},{1,0},{2,3},{3,2},{4,5},{5,4},{6,7},{7,6},{8,9},{9,8},{10,11... | collective-permute-start | bytes 835592 | tf_op jit(solution)/shard_map/ppermute | solution.py:483
  156.3 27.6 %collective-permute-start.30 = (bf16[272,512]{1,0:T(8,128)(2,1)S(1)}, bf16[272,512]{1,0:T(8,128)(2,1)S(1)}, u32[]{:S(2)}, u32[]{:S(2)}) collective-permute-start(bf16[272,512]{1,0:T(8,128)(2,1)S(1)} %get-tuple-element.44), channel_id=1, source_target_pairs={{0,2},{1,3},{2,0},{3,1},{4,6},{5,7},{6,4},{7,5},{8,10},{9,11},{10,... | collective-permute-start | bytes 835592 | tf_op jit(solution)/shard_map/ppermute | solution.py:483
  157.8 26.1 %collective-permute-start.31 = (bf16[272,512]{1,0:T(8,128)(2,1)S(1)}, bf16[272,512]{1,0:T(8,128)(2,1)S(1)}, u32[]{:S(2)}, u32[]{:S(2)}) collective-permute-start(bf16[272,512]{1,0:T(8,128)(2,1)S(1)} %get-tuple-element.45), channel_id=1, source_target_pairs={{0,3},{1,2},{2,1},{3,0},{4,7},{5,6},{6,5},{7,4},{8,11},{9,10},{10,... | collective-permute-start | bytes 835592 | tf_op jit(solution)/shard_map/ppermute | solution.py:483
  158.8 16.4 %collective-permute-start.14 = (bf16[256,512]{1,0:T(8,128)(2,1)S(1)}, bf16[256,512]{1,0:T(8,128)(2,1)S(1)}, u32[]{:S(2)}, u32[]{:S(2)}) collective-permute-start(bf16[256,512]{1,0:T(8,128)(2,1)S(1)} %get-tuple-element.32), channel_id=1, source_target_pairs={{0,2},{1,3},{2,0},{3,1},{4,6},{5,7},{6,4},{7,5},{8,10},{9,11},{10,... | collective-permute-start | bytes 786440 | tf_op jit(solution)/shard_map/ppermute | solution.py:483
  160.4 22.7 %collective-permute-start.15 = (bf16[256,512]{1,0:T(8,128)(2,1)S(1)}, bf16[256,512]{1,0:T(8,128)(2,1)S(1)}, u32[]{:S(2)}, u32[]{:S(2)}) collective-permute-start(bf16[256,512]{1,0:T(8,128)(2,1)S(1)} %get-tuple-element.33), channel_id=1, source_target_pairs={{0,3},{1,2},{2,1},{3,0},{4,7},{5,6},{6,5},{7,4},{8,11},{9,10},{10,... | collective-permute-start | bytes 786440 | tf_op jit(solution)/shard_map/ppermute | solution.py:483
  (21 other events, 189.1 us)
Sparse Core Ops, SparseCore 0:
  10.3 90.8 all-gather.1

commit v2 on v1

--- a/solution.py
+++ b/solution.py
@@ -332,9 +332,80 @@
 STEPS = WIDTH // STEP
 
 
-def ffn_kernel(late, info, *refs):
+def ffn_kernel(info, *refs):
     parts, (gain_ref, w_ref) = refs[:4], refs[4:6]
     outs, (n_sc, r_sc, acc, d_sc, h_sc) = refs[6:10], refs[-5:]
+    i = pl.program_id(0)
+    head = info[AT_HEAD]
+
+    @pl.when(i == 0)
+    def _():
+        for k, part in enumerate(parts):
+            at = pl.multiple_of(lax.bitwise_xor(head, k) * BLOCK, BLOCK)
+            n_sc[:, pl.ds(at, BLOCK)] = part[...]
+        r_sc[...] = jnp.zeros_like(r_sc)
+        acc[...] = jnp.zeros_like(acc)
+
+    at = pl.multiple_of(i * STEP, STEP)
+    value = n_sc[:, pl.ds(at, STEP)]
+    acc[...] = acc[...] + mm(value, w_ref[:, : 2 * HIDDEN])
+    d_sc[pl.ds(at, STEP), :] = w_ref[:, 2 * HIDDEN :]
+    plain = value.astype(F32) / gain_ref[:, pl.ds(at, STEP)].astype(F32)
+    plain = plain * plain
+    r_sc[...] = r_sc[...] + sum(plain[:, c : c + 128] for c in range(0, STEP, 128))
+
+    @pl.when(i == STEPS - 1)
+    def _():
+        squares = jnp.sum(r_sc[...], axis=1, keepdims=True)
+        scale = lax.rsqrt(squares * (1.0 / WIDTH) + norm_eps)
+        gate = acc[:, :HIDDEN] * scale
+        upper = acc[:, HIDDEN:] * scale
+        h_sc[...] = (gate / (1.0 + jnp.exp(-gate)) * upper).astype(BF16)
+        for k, out in enumerate(outs):
+            block = pl.multiple_of(lax.bitwise_xor(head, k) * BLOCK, BLOCK)
+            out[...] = mm(h_sc[...], d_sc[pl.ds(block, BLOCK), :], NT).astype(out.dtype)
+
+
+def ffn_call(info, parts, gain, weights):
+    whole = pl.BlockSpec((SPLIT, BLOCK), lambda i, s: (0, 0))
+    grid = pltpu.PrefetchScalarGridSpec(
+        num_scalar_prefetch=1,
+        grid=(STEPS,),
+        in_specs=[whole] * 4
+        + [
+            pl.BlockSpec((1, WIDTH), lambda i, s: (0, 0)),
+            pl.BlockSpec((STEP, 3 * HIDDEN), lambda i, s: (i, 0)),
+        ],
+        out_specs=[whole] * 4,
+        scratch_shapes=[
+            pltpu.VMEM((SPLIT, WIDTH), BF16),
+            pltpu.VMEM((SPLIT, 128), F32),
+            pltpu.VMEM((SPLIT, 2 * HIDDEN), F32),
+            pltpu.VMEM((WIDTH, HIDDEN), BF16),
+            pltpu.VMEM((SPLIT, HIDDEN), BF16),
+        ],
+    )
+    return pl.pallas_call(
+        ffn_kernel,
+        grid_spec=grid,
+        out_shape=[shaped(SPLIT, BLOCK, F32)] + [shaped(SPLIT, BLOCK, BF16)] * 3,
+        compiler_params=limit(24),
+        cost_estimate=pl.CostEstimate(
+            flops=6 * SPLIT * HIDDEN * WIDTH,
+            transcendentals=SPLIT * HIDDEN,
+            bytes_accessed=20 * 1024 * 1024,
+        ),
+        name="ffn",
+    )(info, *parts, gain, pltpu.with_memory_space_constraint(weights, pltpu.HBM))
+
+
+TILE = 512
+GATE_TILES = HIDDEN // TILE
+
+
+def ffn_late_kernel(info, *refs):
+    parts, (gain_ref, wg, wu, wd) = refs[:4], refs[4:8]
+    outs, (n_sc, r_sc, h_sc) = refs[8:12], refs[-3:]
     i = pl.program_id(0)
     head = info[AT_HEAD]
 
@@ -350,89 +421,83 @@
         r_sc[:SPLIT, :] = jnp.broadcast_to(
             lax.rsqrt(squares * (1.0 / WIDTH) + norm_eps), (SPLIT, 128)
         )
-        if late:
-            squares = jnp.zeros((8, 1), F32)
-            for j in range(4):
-                rows = slice(SPLIT + 8 * j, SPLIT + 8 * j + 8)
-                lanes = slice(j * BLOCK, (j + 1) * BLOCK)
-                both = sum(part[rows, :].astype(F32) for part in parts)
-                total = both + pltpu.roll(both, 5, 0)
-                squares = squares + jnp.sum(total * total, axis=1, keepdims=True)
-                scaled = total * gain_ref[:, lanes].astype(F32)
-                scaled = jnp.concatenate([scaled, jnp.zeros_like(scaled)], axis=0)
-                n_sc[SPLIT:, lanes] = scaled.astype(BF16)
-
-                @pl.when(head == j)
-                def _():
-                    refs[10][...] = total
-
-            scale = lax.rsqrt(squares * (1.0 / WIDTH) + norm_eps)
-            r_sc[SPLIT : SPLIT + 8, :] = jnp.broadcast_to(scale, (8, 128))
-            r_sc[SPLIT + 8 :, :] = jnp.zeros((8, 128), F32)
-
-    at = pl.multiple_of(i * STEP, STEP)
-    product = mm(n_sc[:, pl.ds(at, STEP)], w_ref[:, : 2 * HIDDEN])
-    d_sc[pl.ds(at, STEP), :] = w_ref[:, 2 * HIDDEN :]
-
-    @pl.when(i == 0)
-    def _():
-        acc[...] = product
-
-    @pl.when(i > 0)
-    def _():
-        acc[...] = acc[...] + product
-
-    @pl.when(i == STEPS - 1)
+        squares = jnp.zeros((8, 1), F32)
+        for j in range(4):
+            rows = slice(SPLIT + 8 * j, SPLIT + 8 * j + 8)
+            lanes = slice(j * BLOCK, (j + 1) * BLOCK)
+            both = sum(part[rows, :].astype(F32) for part in parts)
+            total = both + pltpu.roll(both, 5, 0)
+            squares = squares + jnp.sum(total * total, axis=1, keepdims=True)
+            scaled = total * gain_ref[:, lanes].astype(F32)
+            scaled = jnp.concatenate([scaled, jnp.zeros_like(scaled)], axis=0)
+            n_sc[SPLIT:, lanes] = scaled.astype(BF16)
+
+            @pl.when(head == j)
+            def _():
+                refs[12][...] = total
+
+        scale = lax.rsqrt(squares * (1.0 / WIDTH) + norm_eps)
+        r_sc[SPLIT : SPLIT + 8, :] = jnp.broadcast_to(scale, (8, 128))
+        r_sc[SPLIT + 8 :, :] = jnp.zeros((8, 128), F32)
+
+    @pl.when(i < GATE_TILES)
     def _():
         scale = r_sc[:, :1]
-        gate = acc[:, :HIDDEN] * scale
-        upper = acc[:, HIDDEN:] * scale
-        h_sc[...] = (gate / (1.0 + jnp.exp(-gate)) * upper).astype(BF16)
-        for k, out in enumerate(outs):
-            block = pl.multiple_of(lax.bitwise_xor(head, k) * BLOCK, BLOCK)
-            out[...] = mm(h_sc[...], d_sc[pl.ds(block, BLOCK), :], NT).astype(out.dtype)
-
-
-def ffn_call(late, info, parts, gain, weights):
-    rows = SPLIT + EXTRA * late
-    sent = SPLIT + 32 * late
+        gate = mm(n_sc[...], wg[...]) * scale
+        upper = mm(n_sc[...], wu[...]) * scale
+        hidden = (gate / (1.0 + jnp.exp(-gate)) * upper).astype(BF16)
+        h_sc[:, pl.ds(pl.multiple_of(i * TILE, TILE), TILE)] = hidden
+
+    for k, out in enumerate(outs):
+
+        @pl.when(i == GATE_TILES + k)
+        def _():
+            out[...] = mm(h_sc[...], wd[...], NT).astype(out.dtype)
+
+
+def ffn_late_call(info, parts, gain, weights):
+    rows = SPLIT + EXTRA
+    sent = SPLIT + 32
+    last = GATE_TILES - 1
+
+    def down_map(i, s):
+        return (lax.bitwise_xor(s[AT_HEAD], jnp.maximum(i - GATE_TILES, 0)), 2)
+
     whole = pl.BlockSpec((sent, BLOCK), lambda i, s: (0, 0))
     out = pl.BlockSpec((rows, BLOCK), lambda i, s: (0, 0))
     small = pl.BlockSpec((8, BLOCK), lambda i, s: (0, 0))
     grid = pltpu.PrefetchScalarGridSpec(
         num_scalar_prefetch=1,
-        grid=(STEPS,),
+        grid=(GATE_TILES + 4,),
         in_specs=[whole] * 4
         + [
             pl.BlockSpec((1, WIDTH), lambda i, s: (0, 0)),
-            pl.BlockSpec((STEP, 3 * HIDDEN), lambda i, s: (i, 0)),
-        ],
-        out_specs=[out] * 4 + [small] * late,
+            pl.BlockSpec((WIDTH, TILE), lambda i, s: (0, jnp.minimum(i, last))),
+            pl.BlockSpec((WIDTH, TILE), lambda i, s: (0, GATE_TILES + jnp.minimum(i, last))),
+            pl.BlockSpec((BLOCK, HIDDEN), down_map),
+        ],
+        out_specs=[out] * 4 + [small],
         scratch_shapes=[
             pltpu.VMEM((rows, WIDTH), BF16),
             pltpu.VMEM((rows, 128), F32),
-            pltpu.VMEM((rows, 2 * HIDDEN), F32),
-            pltpu.VMEM((WIDTH, HIDDEN), BF16),
             pltpu.VMEM((rows, HIDDEN), BF16),
         ],
     )
 
-    def kernel(*refs):
-        ffn_kernel(late, *refs)
-
-    return pl.pallas_call(
-        kernel,
+    return pl.pallas_call(
+        ffn_late_kernel,
         grid_spec=grid,
         out_shape=[shaped(rows, BLOCK, F32)]
         + [shaped(rows, BLOCK, BF16)] * 3
-        + [shaped(8, BLOCK, F32)] * late,
-        compiler_params=limit(32),
+        + [shaped(8, BLOCK, F32)],
+        compiler_params=limit(22),
         cost_estimate=pl.CostEstimate(
             flops=6 * rows * HIDDEN * WIDTH,
             transcendentals=rows * HIDDEN,
             bytes_accessed=20 * 1024 * 1024,
         ),
-    )(info, *parts, gain, pltpu.with_memory_space_constraint(weights, pltpu.HBM))
+        name="ffn_late",
+    )(info, *parts, gain, weights, weights, weights)
 
 
 def finish_first(s_ref, own, r1, r2, r3, p_ref):
@@ -558,9 +623,9 @@
         info, att, prefill_states, piece, other
     )
     parts0 = exchanged([q1, q2, q3])
+    decoded = decode_call(info, *both, decode_cache, cosine, sine)
+    decoded, p1, p2, p3 = lax.optimization_barrier((decoded, p1, p2, p3))
     parts1 = exchanged([p1, p2, p3])
-
-    decoded = decode_call(info, *both, decode_cache, cosine, sine)
     decoded = jnp.concatenate(spread(decoded), axis=0)
     states = jnp.pad(decode_states, ((3, 2), (0, 0)))
     late = return_call(info, decoded, w_all, states)
@@ -569,9 +634,9 @@
     scaled0 = shared(scaled0)
     summed1, scaled1 = combine_call(info, gain, own1, parts1, (late,))
     scaled1 = shared(scaled1)
-    own0, *parts0 = ffn_call(0, info, scaled0, gain, weights)
+    own0, *parts0 = ffn_call(info, scaled0, gain, weights)
     parts0 = exchanged(parts0)
-    own1, *parts1, late = ffn_call(1, info, scaled1, gain, weights)
+    own1, *parts1, late = ffn_late_call(info, scaled1, gain, weights)
     parts1 = exchanged(parts1)
     result = finish_call(summed0, own0, parts0)
     return finish_call(summed1, own1, parts1, result, late)

time: 193 us -> 187 us (0.969)
  Pallas kernels: 48.4 us -> 42.7 us
    pallas_call x2, Pallas kernels: 29.5 us -> 23.5 us  [the longest x1 14.2 us: ffn_call(): pl.pallas_call(ffn_kernel, grid_spec=grid, out_shape=[shaped(SPLIT, BLOCK...]
  transfers between devices with their start and end apart: 33 -> 33, of which waited for: 13 -> 13; matrix products, arithmetic and copies ran while one was open for 2% -> 2% of each run, Pallas kernels for 25% -> 23%
where the time goes in v2:
time: 187 us; the launch traced here: 186 us
  waiting for transfers between devices  76.5 us (41%)
  starting transfers between devices  45 us (24%)
  Pallas kernels  42.7 us (23%)
  between operations  15 us (8%)
  other arithmetic  3.43 us (2%)
  local copies, waits for them, and re-layouts  2.93 us (2%)
    ppermute x32, waiting for transfers between devices, swap(): return lax.ppermute(value, axis, [(i, i ^ k) for i in range(SIZE[axis])])  76.5 us
    ppermute x32, starting transfers between devices, swap(): return lax.ppermute(value, axis, [(i, i ^ k) for i in range(SIZE[axis])])  44.9 us
    pallas_call x1, Pallas kernels, ffn_call(): pl.pallas_call(ffn_kernel, grid_spec=grid, out_shape=[shaped(SPLIT, BLOCK...  14.2 us
    pallas_call x1, Pallas kernels, ffn_late_call(): pl.pallas_call(ffn_late_kernel, grid_spec=grid, out_shape=[shaped(rows, B...  9.38 us
    pallas_call x1, Pallas kernels, prefill_call(): pl.pallas_call(prefill_kernel, grid_spec=grid, out_shape=jax.ShapeDtypeSt...  8.61 us
    pallas_call x1, Pallas kernels, decode_call(): pl.pallas_call(decode_kernel, grid_spec=grid, out_shape=jax.ShapeDtypeStr...  3.77 us
  transfers between devices with their start and end apart: 33, of which 13 were waited for; matrix products, arithmetic and copies ran while one was open for 2% of the time, Pallas kernels for 23%

profile of v2, /device:TPU:1, one launch (start us, length us, event | category | flops | bytes accessed | tf_op | source)
XLA Modules:
  0.0 185.5 jit_solution(16463570483065980538)
XLA Ops:
  11.7 2.6 %collective-permute-start.1 = (bf16[80,512]{1,0:T(8,128)(2,1)S(1)}, bf16[80,512]{1,0:T(8,128)(2,1)S(1)}, u32[]{:S(2)}, u32[]{:S(2)}) collective-permute-start(bf16[80,512]{1,0:T(8,128)(2,1)S(1)} %concatenate.44), channel_id=1, source_target_pairs={{0,16},{8,24},{16,0},{24,8},{1,17},{9,25},{17,1},{25,9},{2,18},{10... | collective-permute-start | bytes 245768 | tf_op jit(solution)/shard_map/ppermute | solution.py:548
  14.3 3.3 %collective-permute-done.1 = bf16[80,512]{1,0:T(8,128)(2,1)S(1)} collective-permute-done((bf16[80,512]{1,0:T(8,128)(2,1)S(1)}, bf16[80,512]{1,0:T(8,128)(2,1)S(1)}, u32[]{:S(2)}, u32[]{:S(2)}) %collective-permute-start.1) | collective-permute-done | bytes 81952 | tf_op jit(solution)/shard_map/ppermute | solution.py:548
  17.7 2.3 %collective-permute-done.2 = bf16[80,512]{1,0:T(8,128)(2,1)S(1)} collective-permute-done((bf16[80,512]{1,0:T(8,128)(2,1)S(1)}, bf16[80,512]{1,0:T(8,128)(2,1)S(1)}, u32[]{:S(2)}, u32[]{:S(2)}) %collective-permute-start.2) | collective-permute-done | bytes 81952 | tf_op jit(solution)/shard_map/ppermute | solution.py:548
  21.3 2.5 %collective-permute-start.4 = (bf16[320,512]{1,0:T(8,128)(2,1)S(1)}, bf16[320,512]{1,0:T(8,128)(2,1)S(1)}, u32[]{:S(2)}, u32[]{:S(2)}) collective-permute-start(bf16[320,512]{1,0:T(8,128)(2,1)S(1)} %pad_maximum_fusion.2), channel_id=1, source_target_pairs={{0,64},{32,96},{64,0},{96,32},{1,65},{33,97},{65,1},{97,33},{2,66}... | collective-permute-start | bytes 983048 | tf_op jit(solution)/shard_map/ppermute | solution.py:548
  24.0 5.8 %collective-permute-done.3 = bf16[320,512]{1,0:T(8,128)(2,1)S(1)} collective-permute-done((bf16[320,512]{1,0:T(8,128)(2,1)S(1)}, bf16[320,512]{1,0:T(8,128)(2,1)S(1)}, u32[]{:S(2)}, u32[]{:S(2)}) %collective-permute-start.3) | collective-permute-done | bytes 327712 | tf_op jit(solution)/shard_map/ppermute | solution.py:548
  29.8 16.8 %collective-permute-done.4 = bf16[320,512]{1,0:T(8,128)(2,1)S(1)} collective-permute-done((bf16[320,512]{1,0:T(8,128)(2,1)S(1)}, bf16[320,512]{1,0:T(8,128)(2,1)S(1)}, u32[]{:S(2)}, u32[]{:S(2)}) %collective-permute-start.4) | collective-permute-done | bytes 327712 | tf_op jit(solution)/shard_map/ppermute | solution.py:548
  46.7 4.1 %collective-permute-start.6 = (bf16[1280,512]{1,0:T(8,128)(2,1)S(1)}, bf16[1280,512]{1,0:T(8,128)(2,1)S(1)}, u32[]{:S(2)}, u32[]{:S(2)}) collective-permute-start(bf16[1280,512]{1,0:T(8,128)(2,1)S(1)} %pad_maximum_fusion.w0_ref), channel_id=1, source_target_pairs={{0,4},{4,0},{1,5},{5,1},{2,6},{6,2},{3,7},{7,3},{8,12},{12,8},{9,1... | collective-permute-start | bytes 3932168 | tf_op jit(solution)/shard_map/ppermute | solution.py:548
  55.4 8.6 %prefill_attention.1.a_ref = bf16[512,512]{1,0:T(8,128)(2,1)S(1)} custom-call(s32[12]{0:T(128)S(1)} %concatenate.39.info, bf16[512,512]{1,0:T(8,128)(2,1)S(1)} %copy-done.2, bf16[512,512]{1,0:T(8,128)(2,1)S(1)} %bitcast.19, bf16[512,512]{1,0:T(8,128)(2,1)S(1)} %bitcast.20, bf16[1,2,2048,256]{3,2,1,0:T(8,128)(2,1)S(1)} %copy-done.1, ...), custom_call_target="tpu_custom_call" | custom-call | flops 2684354560 | bytes 4194304 | tf_op jit(solution)/shard_map/prefill_attention/pallas_call | solution.py:119
  64.1 2.2 %project.1 = (f32[256,512]{1,0:T(8,128)S(1)}, bf16[256,512]{1,0:T(8,128)(2,1)S(1)}, bf16[256,512]{1,0:T(8,128)(2,1)S(1)}, bf16[256,512]{1,0:T(8,128)(2,1)S(1)}, ...) custom-call(s32[12]{0:T(128)S(1)} %concatenate.39.info, ...), custom_call_target="tpu_custom_call" | custom-call | flops 1073741824 | bytes 6291456 | tf_op jit(solution)/shard_map/project/pallas_call | solution.py:261
  66.4 3.8 %decode_attention.1 = bf16[8,256]{1,0:T(8,128)(2,1)S(1)} custom-call(s32[12]{0:T(128)S(1)} %concatenate.39.info, bf16[16,80,512]{2,1,0:T(8,128)(2,1)S(1)} %bitcast.17, bf16[16,80,512]{2,1,0:T(8,128)(2,1)S(1)} %bitcast.18, bf16[3,2,2048,256]{3,2,1,0:T(8,128)(2,1)S(1)} %bitcast.16, f32[520,128]{1,0:T(8,128)S(1)} %get-tuple-element.57.cos_ref, ...), custom_call_target="tpu_custom_call" | custom-call | flops 1610612736 | bytes 7340032 | tf_op jit(solution)/shard_map/decode_attention/pallas_call | solution.py:208
  70.8 3.3 %collective-permute-start.18 = (bf16[8,256]{1,0:T(8,128)(2,1)S(1)}, bf16[8,256]{1,0:T(8,128)(2,1)S(1)}, u32[]{:S(2)}, u32[]{:S(2)}) collective-permute-start(bf16[8,256]{1,0:T(8,128)(2,1)S(1)} %decode_attention.1), channel_id=1, source_target_pairs={{0,24},{8,16},{16,8},{24,0},{1,25},{9,17},{17,9},{25,1},{2,26},{10... | collective-permute-start | bytes 12296 | tf_op jit(solution)/shard_map/ppermute | solution.py:548
  75.8 3.3 %collective-permute-start.8 = (bf16[256,512]{1,0:T(8,128)(2,1)S(1)}, bf16[256,512]{1,0:T(8,128)(2,1)S(1)}, u32[]{:S(2)}, u32[]{:S(2)}) collective-permute-start(bf16[256,512]{1,0:T(8,128)(2,1)S(1)} %get-tuple-element.30), channel_id=1, source_target_pairs={{0,2},{1,3},{2,0},{3,1},{4,6},{5,7},{6,4},{7,5},{8,10},{9,11},{10,... | collective-permute-start | bytes 786440 | tf_op jit(solution)/shard_map/ppermute | solution.py:548
  79.7 3.5 %collective-permute-done.19 = bf16[32,256]{1,0:T(8,128)(2,1)S(1)} collective-permute-done((bf16[32,256]{1,0:T(8,128)(2,1)S(1)}, bf16[32,256]{1,0:T(8,128)(2,1)S(1)}, u32[]{:S(2)}, u32[]{:S(2)}) %collective-permute-start.19) | collective-permute-done | bytes 16416 | tf_op jit(solution)/shard_map/ppermute | solution.py:548
  83.1 4.6 %collective-permute-done.20 = bf16[32,256]{1,0:T(8,128)(2,1)S(1)} collective-permute-done((bf16[32,256]{1,0:T(8,128)(2,1)S(1)}, bf16[32,256]{1,0:T(8,128)(2,1)S(1)}, u32[]{:S(2)}, u32[]{:S(2)}) %collective-permute-start.20) | collective-permute-done | bytes 16416 | tf_op jit(solution)/shard_map/ppermute | solution.py:548
  87.9 4.6 %collective-permute-done.21 = bf16[32,256]{1,0:T(8,128)(2,1)S(1)} collective-permute-done((bf16[32,256]{1,0:T(8,128)(2,1)S(1)}, bf16[32,256]{1,0:T(8,128)(2,1)S(1)}, u32[]{:S(2)}, u32[]{:S(2)}) %collective-permute-start.21) | collective-permute-done | bytes 16416 | tf_op jit(solution)/shard_map/ppermute | solution.py:548
  92.5 5.3 %collective-permute-start.22 = (bf16[128,256]{1,0:T(8,128)(2,1)S(1)}, bf16[128,256]{1,0:T(8,128)(2,1)S(1)}, u32[]{:S(2)}, u32[]{:S(2)}) collective-permute-start(bf16[128,256]{1,0:T(8,128)(2,1)S(1)} %pad_maximum_fusion.6), channel_id=1, source_target_pairs={{0,4},{4,0},{1,5},{5,1},{2,6},{6,2},{3,7},{7,3},{8,12},{12,8},{9,1... | collective-permute-start | bytes 196616 | tf_op jit(solution)/shard_map/ppermute | solution.py:548
  101.5 3.0 %collective-permute-start.11 = (bf16[256,512]{1,0:T(8,128)(2,1)S(1)}, bf16[256,512]{1,0:T(8,128)(2,1)S(1)}, u32[]{:S(2)}, u32[]{:S(2)}) collective-permute-start(bf16[256,512]{1,0:T(8,128)(2,1)S(1)} %get-tuple-element.33.refs_0_), channel_id=1, source_target_pairs={{0,2},{1,3},{2,0},{3,1},{4,6},{5,7},{6,4},{7,5},{8,10},{9,11},{10,... | collective-permute-start | bytes 786440 | tf_op jit(solution)/shard_map/ppermute | solution.py:548
  107.3 6.3 %collective-permute-done.25.refs_4_ = bf16[256,512]{1,0:T(8,128)(2,1)S(1)} collective-permute-done((bf16[256,512]{1,0:T(8,128)(2,1)S(1)}, bf16[256,512]{1,0:T(8,128)(2,1)S(1)}, u32[]{:S(2)}, u32[]{:S(2)}) %collective-permute-start.25) | collective-permute-done | bytes 262176 | tf_op jit(solution)/shard_map/ppermute | solution.py:548
  114.4 2.9 %collective-permute-start.27 = (bf16[288,512]{1,0:T(8,128)(2,1)S(1)}, bf16[288,512]{1,0:T(8,128)(2,1)S(1)}, u32[]{:S(2)}, u32[]{:S(2)}) collective-permute-start(bf16[288,512]{1,0:T(8,128)(2,1)S(1)} %get-tuple-element.48.refs_0_), channel_id=1, source_target_pairs={{0,2},{1,3},{2,0},{3,1},{4,6},{5,7},{6,4},{7,5},{8,10},{9,11},{10,... | collective-permute-start | bytes 884744 | tf_op jit(solution)/shard_map/ppermute | solution.py:548
  118.5 6.2 %collective-permute-done.12.refs_3_ = bf16[256,512]{1,0:T(8,128)(2,1)S(1)} collective-permute-done((bf16[256,512]{1,0:T(8,128)(2,1)S(1)}, bf16[256,512]{1,0:T(8,128)(2,1)S(1)}, u32[]{:S(2)}, u32[]{:S(2)}) %collective-permute-start.12) | collective-permute-done | bytes 262176 | tf_op jit(solution)/shard_map/ppermute | solution.py:548
  124.8 14.2 %ffn.1 = (f32[256,512]{1,0:T(8,128)S(1)}, bf16[256,512]{1,0:T(8,128)(2,1)S(1)}, bf16[256,512]{1,0:T(8,128)(2,1)S(1)}, bf16[256,512]{1,0:T(8,128)(2,1)S(1)}) custom-call(s32[12]{0:T(128)S(1)} %concatenate.39.info, bf16[256,512]{1,0:T(8,128)(2,1)S(1)} %get-tuple-element.33.refs_0_, bf16[256,512]{1,0:T(8,128)(2,1)S(1)} %collective-permute-done.10.refs_1_, ...), custom_call_target="tpu_custom_call" | custom-call | flops 4831838208 | bytes 20971520 | tf_op jit(solution)/shard_map/ffn/pallas_call | solution.py:388
  139.3 9.4 %ffn_late.1 = (f32[272,512]{1,0:T(8,128)S(1)}, bf16[272,512]{1,0:T(8,128)(2,1)S(1)}, bf16[272,512]{1,0:T(8,128)(2,1)S(1)}, bf16[272,512]{1,0:T(8,128)(2,1)S(1)}, f32[8,512]{1,0:T(8,128)S(1)}) custom-call(s32[12]{0:T(128)S(1)} %concatenate.39.info, bf16[288,512]{1,0:T(8,128)(2,1)S(1)} %get-tuple-element.48.refs_0_, ...), custom_call_target="tpu_custom_call" | custom-call | flops 5133828096 | bytes 20971520 | tf_op jit(solution)/shard_map/ffn_late/pallas_call | solution.py:487
  155.2 13.8 %collective-permute-done.14.r2 = bf16[256,512]{1,0:T(8,128)(2,1)S(1)} collective-permute-done((bf16[256,512]{1,0:T(8,128)(2,1)S(1)}, bf16[256,512]{1,0:T(8,128)(2,1)S(1)}, u32[]{:S(2)}, u32[]{:S(2)}) %collective-permute-start.14) | collective-permute-done | bytes 262176 | tf_op jit(solution)/shard_map/ppermute | solution.py:548
  169.1 7.9 %collective-permute-done.15.r3 = bf16[256,512]{1,0:T(8,128)(2,1)S(1)} collective-permute-done((bf16[256,512]{1,0:T(8,128)(2,1)S(1)}, bf16[256,512]{1,0:T(8,128)(2,1)S(1)}, u32[]{:S(2)}, u32[]{:S(2)}) %collective-permute-start.15) | collective-permute-done | bytes 262176 | tf_op jit(solution)/shard_map/ppermute | solution.py:548
  (103 shorter events, 30.2 us)
Async XLA Ops:
  7.2 117.6 %all-gather.2.cloned.1.call-start = ((), (), s32[]{:S(2)}) async-start(), calls=%async_computation | async-start | bytes 19464192 | tf_op jit(solution)/shard_map/all_gather | solution.py:585
  20.0 9.7 %collective-permute-start.3 = (bf16[320,512]{1,0:T(8,128)(2,1)S(1)}, bf16[320,512]{1,0:T(8,128)(2,1)S(1)}, u32[]{:S(2)}, u32[]{:S(2)}) collective-permute-start(bf16[320,512]{1,0:T(8,128)(2,1)S(1)} %pad_maximum_fusion.2), channel_id=1, source_target_pairs={{0,32},{32,0},{64,96},{96,64},{1,33},{33,1},{65,97},{97,65},{2,34}... | collective-permute-start | bytes 983048 | tf_op jit(solution)/shard_map/ppermute | solution.py:548
  21.3 25.3 %collective-permute-start.4 = (bf16[320,512]{1,0:T(8,128)(2,1)S(1)}, bf16[320,512]{1,0:T(8,128)(2,1)S(1)}, u32[]{:S(2)}, u32[]{:S(2)}) collective-permute-start(bf16[320,512]{1,0:T(8,128)(2,1)S(1)} %pad_maximum_fusion.2), channel_id=1, source_target_pairs={{0,64},{32,96},{64,0},{96,32},{1,65},{33,97},{65,1},{97,33},{2,66}... | collective-permute-start | bytes 983048 | tf_op jit(solution)/shard_map/ppermute | solution.py:548
  23.8 22.8 %collective-permute-start.5 = (bf16[320,512]{1,0:T(8,128)(2,1)S(1)}, bf16[320,512]{1,0:T(8,128)(2,1)S(1)}, u32[]{:S(2)}, u32[]{:S(2)}) collective-permute-start(bf16[320,512]{1,0:T(8,128)(2,1)S(1)} %pad_maximum_fusion.2), channel_id=1, source_target_pairs={{0,96},{32,64},{64,32},{96,0},{1,97},{33,65},{65,33},{97,1},{2,98}... | collective-permute-start | bytes 983048 | tf_op jit(solution)/shard_map/ppermute | solution.py:548
  46.7 17.4 %collective-permute-start.6 = (bf16[1280,512]{1,0:T(8,128)(2,1)S(1)}, bf16[1280,512]{1,0:T(8,128)(2,1)S(1)}, u32[]{:S(2)}, u32[]{:S(2)}) collective-permute-start(bf16[1280,512]{1,0:T(8,128)(2,1)S(1)} %pad_maximum_fusion.w0_ref), channel_id=1, source_target_pairs={{0,4},{4,0},{1,5},{5,1},{2,6},{6,2},{3,7},{7,3},{8,12},{12,8},{9,1... | collective-permute-start | bytes 3932168 | tf_op jit(solution)/shard_map/ppermute | solution.py:548
  74.1 30.3 %collective-permute-start.23 = (bf16[256,512]{1,0:T(8,128)(2,1)S(1)}, bf16[256,512]{1,0:T(8,128)(2,1)S(1)}, u32[]{:S(2)}, u32[]{:S(2)}) collective-permute-start(bf16[256,512]{1,0:T(8,128)(2,1)S(1)} %get-tuple-element.44), channel_id=1, source_target_pairs={{0,1},{1,0},{2,3},{3,2},{4,5},{5,4},{6,7},{7,6},{8,9},{9,8},{10,11... | collective-permute-start | bytes 786440 | tf_op jit(solution)/shard_map/ppermute | solution.py:548
  75.8 22.0 %collective-permute-start.7 = (bf16[256,512]{1,0:T(8,128)(2,1)S(1)}, bf16[256,512]{1,0:T(8,128)(2,1)S(1)}, u32[]{:S(2)}, u32[]{:S(2)}) collective-permute-start(bf16[256,512]{1,0:T(8,128)(2,1)S(1)} %get-tuple-element.29), channel_id=1, source_target_pairs={{0,1},{1,0},{2,3},{3,2},{4,5},{5,4},{6,7},{7,6},{8,9},{9,8},{10,11... | collective-permute-start | bytes 786440 | tf_op jit(solution)/shard_map/ppermute | solution.py:548
  75.8 24.0 %collective-permute-start.8 = (bf16[256,512]{1,0:T(8,128)(2,1)S(1)}, bf16[256,512]{1,0:T(8,128)(2,1)S(1)}, u32[]{:S(2)}, u32[]{:S(2)}) collective-permute-start(bf16[256,512]{1,0:T(8,128)(2,1)S(1)} %get-tuple-element.30), channel_id=1, source_target_pairs={{0,2},{1,3},{2,0},{3,1},{4,6},{5,7},{6,4},{7,5},{8,10},{9,11},{10,... | collective-permute-start | bytes 786440 | tf_op jit(solution)/shard_map/ppermute | solution.py:548
  79.1 21.1 %collective-permute-start.9 = (bf16[256,512]{1,0:T(8,128)(2,1)S(1)}, bf16[256,512]{1,0:T(8,128)(2,1)S(1)}, u32[]{:S(2)}, u32[]{:S(2)}) collective-permute-start(bf16[256,512]{1,0:T(8,128)(2,1)S(1)} %get-tuple-element.31), channel_id=1, source_target_pairs={{0,3},{1,2},{2,1},{3,0},{4,7},{5,6},{6,5},{7,4},{8,11},{9,10},{10,... | collective-permute-start | bytes 786440 | tf_op jit(solution)/shard_map/ppermute | solution.py:548
  92.5 8.9 %collective-permute-start.22 = (bf16[128,256]{1,0:T(8,128)(2,1)S(1)}, bf16[128,256]{1,0:T(8,128)(2,1)S(1)}, u32[]{:S(2)}, u32[]{:S(2)}) collective-permute-start(bf16[128,256]{1,0:T(8,128)(2,1)S(1)} %pad_maximum_fusion.6), channel_id=1, source_target_pairs={{0,4},{4,0},{1,5},{5,1},{2,6},{6,2},{3,7},{7,3},{8,12},{12,8},{9,1... | collective-permute-start | bytes 196616 | tf_op jit(solution)/shard_map/ppermute | solution.py:548
  97.8 9.5 %collective-permute-start.24 = (bf16[256,512]{1,0:T(8,128)(2,1)S(1)}, bf16[256,512]{1,0:T(8,128)(2,1)S(1)}, u32[]{:S(2)}, u32[]{:S(2)}) collective-permute-start(bf16[256,512]{1,0:T(8,128)(2,1)S(1)} %get-tuple-element.45), channel_id=1, source_target_pairs={{0,2},{1,3},{2,0},{3,1},{4,6},{5,7},{6,4},{7,5},{8,10},{9,11},{10,... | collective-permute-start | bytes 786440 | tf_op jit(solution)/shard_map/ppermute | solution.py:548
  99.8 13.8 %collective-permute-start.25 = (bf16[256,512]{1,0:T(8,128)(2,1)S(1)}, bf16[256,512]{1,0:T(8,128)(2,1)S(1)}, u32[]{:S(2)}, u32[]{:S(2)}) collective-permute-start(bf16[256,512]{1,0:T(8,128)(2,1)S(1)} %get-tuple-element.46), channel_id=1, source_target_pairs={{0,3},{1,2},{2,1},{3,0},{4,7},{5,6},{6,5},{7,4},{8,11},{9,10},{10,... | collective-permute-start | bytes 786440 | tf_op jit(solution)/shard_map/ppermute | solution.py:548
  101.0 16.4 %collective-permute-start.10 = (bf16[256,512]{1,0:T(8,128)(2,1)S(1)}, bf16[256,512]{1,0:T(8,128)(2,1)S(1)}, u32[]{:S(2)}, u32[]{:S(2)}) collective-permute-start(bf16[256,512]{1,0:T(8,128)(2,1)S(1)} %get-tuple-element.33.refs_0_), channel_id=1, source_target_pairs={{0,1},{1,0},{2,3},{3,2},{4,5},{5,4},{6,7},{7,6},{8,9},{9,8},{10,11... | collective-permute-start | bytes 786440 | tf_op jit(solution)/shard_map/ppermute | solution.py:548
  101.5 17.1 %collective-permute-start.11 = (bf16[256,512]{1,0:T(8,128)(2,1)S(1)}, bf16[256,512]{1,0:T(8,128)(2,1)S(1)}, u32[]{:S(2)}, u32[]{:S(2)}) collective-permute-start(bf16[256,512]{1,0:T(8,128)(2,1)S(1)} %get-tuple-element.33.refs_0_), channel_id=1, source_target_pairs={{0,2},{1,3},{2,0},{3,1},{4,6},{5,7},{6,4},{7,5},{8,10},{9,11},{10,... | collective-permute-start | bytes 786440 | tf_op jit(solution)/shard_map/ppermute | solution.py:548
  104.4 20.4 %collective-permute-start.12 = (bf16[256,512]{1,0:T(8,128)(2,1)S(1)}, bf16[256,512]{1,0:T(8,128)(2,1)S(1)}, u32[]{:S(2)}, u32[]{:S(2)}) collective-permute-start(bf16[256,512]{1,0:T(8,128)(2,1)S(1)} %get-tuple-element.33.refs_0_), channel_id=1, source_target_pairs={{0,3},{1,2},{2,1},{3,0},{4,7},{5,6},{6,5},{7,4},{8,11},{9,10},{10,... | collective-permute-start | bytes 786440 | tf_op jit(solution)/shard_map/ppermute | solution.py:548
  114.3 25.0 %collective-permute-start.26 = (bf16[288,512]{1,0:T(8,128)(2,1)S(1)}, bf16[288,512]{1,0:T(8,128)(2,1)S(1)}, u32[]{:S(2)}, u32[]{:S(2)}) collective-permute-start(bf16[288,512]{1,0:T(8,128)(2,1)S(1)} %get-tuple-element.48.refs_0_), channel_id=1, source_target_pairs={{0,1},{1,0},{2,3},{3,2},{4,5},{5,4},{6,7},{7,6},{8,9},{9,8},{10,11... | collective-permute-start | bytes 884744 | tf_op jit(solution)/shard_map/ppermute | solution.py:548
  114.4 24.9 %collective-permute-start.27 = (bf16[288,512]{1,0:T(8,128)(2,1)S(1)}, bf16[288,512]{1,0:T(8,128)(2,1)S(1)}, u32[]{:S(2)}, u32[]{:S(2)}) collective-permute-start(bf16[288,512]{1,0:T(8,128)(2,1)S(1)} %get-tuple-element.48.refs_0_), channel_id=1, source_target_pairs={{0,2},{1,3},{2,0},{3,1},{4,6},{5,7},{6,4},{7,5},{8,10},{9,11},{10,... | collective-permute-start | bytes 884744 | tf_op jit(solution)/shard_map/ppermute | solution.py:548
  117.3 21.9 %collective-permute-start.28 = (bf16[288,512]{1,0:T(8,128)(2,1)S(1)}, bf16[288,512]{1,0:T(8,128)(2,1)S(1)}, u32[]{:S(2)}, u32[]{:S(2)}) collective-permute-start(bf16[288,512]{1,0:T(8,128)(2,1)S(1)} %get-tuple-element.48.refs_0_), channel_id=1, source_target_pairs={{0,3},{1,2},{2,1},{3,0},{4,7},{5,6},{6,5},{7,4},{8,11},{9,10},{10,... | collective-permute-start | bytes 884744 | tf_op jit(solution)/shard_map/ppermute | solution.py:548
  138.9 15.3 %collective-permute-start.13 = (bf16[256,512]{1,0:T(8,128)(2,1)S(1)}, bf16[256,512]{1,0:T(8,128)(2,1)S(1)}, u32[]{:S(2)}, u32[]{:S(2)}) collective-permute-start(bf16[256,512]{1,0:T(8,128)(2,1)S(1)} %get-tuple-element.35), channel_id=1, source_target_pairs={{0,1},{1,0},{2,3},{3,2},{4,5},{5,4},{6,7},{7,6},{8,9},{9,8},{10,11... | collective-permute-start | bytes 786440 | tf_op jit(solution)/shard_map/ppermute | solution.py:548
  148.7 29.1 %collective-permute-start.29 = (bf16[272,512]{1,0:T(8,128)(2,1)S(1)}, bf16[272,512]{1,0:T(8,128)(2,1)S(1)}, u32[]{:S(2)}, u32[]{:S(2)}) collective-permute-start(bf16[272,512]{1,0:T(8,128)(2,1)S(1)} %get-tuple-element.51), channel_id=1, source_target_pairs={{0,1},{1,0},{2,3},{3,2},{4,5},{5,4},{6,7},{7,6},{8,9},{9,8},{10,11... | collective-permute-start | bytes 835592 | tf_op jit(solution)/shard_map/ppermute | solution.py:548
  150.2 27.6 %collective-permute-start.30 = (bf16[272,512]{1,0:T(8,128)(2,1)S(1)}, bf16[272,512]{1,0:T(8,128)(2,1)S(1)}, u32[]{:S(2)}, u32[]{:S(2)}) collective-permute-start(bf16[272,512]{1,0:T(8,128)(2,1)S(1)} %get-tuple-element.52), channel_id=1, source_target_pairs={{0,2},{1,3},{2,0},{3,1},{4,6},{5,7},{6,4},{7,5},{8,10},{9,11},{10,... | collective-permute-start | bytes 835592 | tf_op jit(solution)/shard_map/ppermute | solution.py:548
  151.7 26.1 %collective-permute-start.31 = (bf16[272,512]{1,0:T(8,128)(2,1)S(1)}, bf16[272,512]{1,0:T(8,128)(2,1)S(1)}, u32[]{:S(2)}, u32[]{:S(2)}) collective-permute-start(bf16[272,512]{1,0:T(8,128)(2,1)S(1)} %get-tuple-element.53), channel_id=1, source_target_pairs={{0,3},{1,2},{2,1},{3,0},{4,7},{5,6},{6,5},{7,4},{8,11},{9,10},{10,... | collective-permute-start | bytes 835592 | tf_op jit(solution)/shard_map/ppermute | solution.py:548
  152.7 16.4 %collective-permute-start.14 = (bf16[256,512]{1,0:T(8,128)(2,1)S(1)}, bf16[256,512]{1,0:T(8,128)(2,1)S(1)}, u32[]{:S(2)}, u32[]{:S(2)}) collective-permute-start(bf16[256,512]{1,0:T(8,128)(2,1)S(1)} %get-tuple-element.36), channel_id=1, source_target_pairs={{0,2},{1,3},{2,0},{3,1},{4,6},{5,7},{6,4},{7,5},{8,10},{9,11},{10,... | collective-permute-start | bytes 786440 | tf_op jit(solution)/shard_map/ppermute | solution.py:548
  154.3 22.7 %collective-permute-start.15 = (bf16[256,512]{1,0:T(8,128)(2,1)S(1)}, bf16[256,512]{1,0:T(8,128)(2,1)S(1)}, u32[]{:S(2)}, u32[]{:S(2)}) collective-permute-start(bf16[256,512]{1,0:T(8,128)(2,1)S(1)} %get-tuple-element.37), channel_id=1, source_target_pairs={{0,3},{1,2},{2,1},{3,0},{4,7},{5,6},{6,5},{7,4},{8,11},{9,10},{10,... | collective-permute-start | bytes 786440 | tf_op jit(solution)/shard_map/ppermute | solution.py:548
  (22 other events, 209.3 us)
Sparse Core Ops, SparseCore 0:
  10.3 90.9 all-gather.1

commit v3 on v2

--- a/solution.py
+++ b/solution.py
@@ -328,7 +328,7 @@
     )(info, gain, *late, own, *parts)
 
 
-STEP = 256
+STEP = 512
 STEPS = WIDTH // STEP
 
 
@@ -344,11 +344,19 @@
             at = pl.multiple_of(lax.bitwise_xor(head, k) * BLOCK, BLOCK)
             n_sc[:, pl.ds(at, BLOCK)] = part[...]
         r_sc[...] = jnp.zeros_like(r_sc)
-        acc[...] = jnp.zeros_like(acc)
 
     at = pl.multiple_of(i * STEP, STEP)
     value = n_sc[:, pl.ds(at, STEP)]
-    acc[...] = acc[...] + mm(value, w_ref[:, : 2 * HIDDEN])
+    product = mm(value, w_ref[:, : 2 * HIDDEN])
+
+    @pl.when(i == 0)
+    def _():
+        acc[...] = product
+
+    @pl.when(i > 0)
+    def _():
+        acc[...] = acc[...] + product
+
     d_sc[pl.ds(at, STEP), :] = w_ref[:, 2 * HIDDEN :]
     plain = value.astype(F32) / gain_ref[:, pl.ds(at, STEP)].astype(F32)
     plain = plain * plain
@@ -389,7 +397,7 @@
         ffn_kernel,
         grid_spec=grid,
         out_shape=[shaped(SPLIT, BLOCK, F32)] + [shaped(SPLIT, BLOCK, BF16)] * 3,
-        compiler_params=limit(24),
+        compiler_params=limit(30),
         cost_estimate=pl.CostEstimate(
             flops=6 * SPLIT * HIDDEN * WIDTH,
             transcendentals=SPLIT * HIDDEN,

time: 187 us -> 186 us (level)
  transfers between devices with their start and end apart: 33 -> 33, of which waited for: 13 -> 13; matrix products, arithmetic and copies ran while one was open for 2% -> 2% of each run, Pallas kernels for 23% -> 22%
where the time goes in v3:
time: 186 us; the launch traced here: 185 us
  waiting for transfers between devices  76.5 us (41%)
  starting transfers between devices  45 us (24%)
  Pallas kernels  42.1 us (23%)
  between operations  15 us (8%)
  other arithmetic  3.43 us (2%)
  local copies, waits for them, and re-layouts  2.93 us (2%)
    ppermute x32, waiting for transfers between devices, swap(): return lax.ppermute(value, axis, [(i, i ^ k) for i in range(SIZE[axis])])  76.5 us
    ppermute x32, starting transfers between devices, swap(): return lax.ppermute(value, axis, [(i, i ^ k) for i in range(SIZE[axis])])  44.9 us
    pallas_call x1, Pallas kernels, ffn_call(): pl.pallas_call(ffn_kernel, grid_spec=grid, out_shape=[shaped(SPLIT, BLOCK...  13.6 us
    pallas_call x1, Pallas kernels, ffn_late_call(): pl.pallas_call(ffn_late_kernel, grid_spec=grid, out_shape=[shaped(rows, B...  9.38 us
    pallas_call x1, Pallas kernels, prefill_call(): pl.pallas_call(prefill_kernel, grid_spec=grid, out_shape=jax.ShapeDtypeSt...  8.61 us
    pallas_call x1, Pallas kernels, decode_call(): pl.pallas_call(decode_kernel, grid_spec=grid, out_shape=jax.ShapeDtypeStr...  3.77 us
  transfers between devices with their start and end apart: 33, of which 13 were waited for; matrix products, arithmetic and copies ran while one was open for 2% of the time, Pallas kernels for 22%

profile of v3, /device:TPU:1, one launch (start us, length us, event | category | flops | bytes accessed | tf_op | source)
XLA Modules:
  0.0 184.9 jit_solution(17476571530492094616)
XLA Ops:
  11.7 2.6 %collective-permute-start.1 = (bf16[80,512]{1,0:T(8,128)(2,1)S(1)}, bf16[80,512]{1,0:T(8,128)(2,1)S(1)}, u32[]{:S(2)}, u32[]{:S(2)}) collective-permute-start(bf16[80,512]{1,0:T(8,128)(2,1)S(1)} %concatenate.44), channel_id=1, source_target_pairs={{0,16},{8,24},{16,0},{24,8},{1,17},{9,25},{17,1},{25,9},{2,18},{10... | collective-permute-start | bytes 245768 | tf_op jit(solution)/shard_map/ppermute | solution.py:556
  14.3 3.3 %collective-permute-done.1 = bf16[80,512]{1,0:T(8,128)(2,1)S(1)} collective-permute-done((bf16[80,512]{1,0:T(8,128)(2,1)S(1)}, bf16[80,512]{1,0:T(8,128)(2,1)S(1)}, u32[]{:S(2)}, u32[]{:S(2)}) %collective-permute-start.1) | collective-permute-done | bytes 81952 | tf_op jit(solution)/shard_map/ppermute | solution.py:556
  17.7 2.3 %collective-permute-done.2 = bf16[80,512]{1,0:T(8,128)(2,1)S(1)} collective-permute-done((bf16[80,512]{1,0:T(8,128)(2,1)S(1)}, bf16[80,512]{1,0:T(8,128)(2,1)S(1)}, u32[]{:S(2)}, u32[]{:S(2)}) %collective-permute-start.2) | collective-permute-done | bytes 81952 | tf_op jit(solution)/shard_map/ppermute | solution.py:556
  21.3 2.5 %collective-permute-start.4 = (bf16[320,512]{1,0:T(8,128)(2,1)S(1)}, bf16[320,512]{1,0:T(8,128)(2,1)S(1)}, u32[]{:S(2)}, u32[]{:S(2)}) collective-permute-start(bf16[320,512]{1,0:T(8,128)(2,1)S(1)} %pad_maximum_fusion.2), channel_id=1, source_target_pairs={{0,64},{32,96},{64,0},{96,32},{1,65},{33,97},{65,1},{97,33},{2,66}... | collective-permute-start | bytes 983048 | tf_op jit(solution)/shard_map/ppermute | solution.py:556
  24.0 5.8 %collective-permute-done.3 = bf16[320,512]{1,0:T(8,128)(2,1)S(1)} collective-permute-done((bf16[320,512]{1,0:T(8,128)(2,1)S(1)}, bf16[320,512]{1,0:T(8,128)(2,1)S(1)}, u32[]{:S(2)}, u32[]{:S(2)}) %collective-permute-start.3) | collective-permute-done | bytes 327712 | tf_op jit(solution)/shard_map/ppermute | solution.py:556
  29.8 16.8 %collective-permute-done.4 = bf16[320,512]{1,0:T(8,128)(2,1)S(1)} collective-permute-done((bf16[320,512]{1,0:T(8,128)(2,1)S(1)}, bf16[320,512]{1,0:T(8,128)(2,1)S(1)}, u32[]{:S(2)}, u32[]{:S(2)}) %collective-permute-start.4) | collective-permute-done | bytes 327712 | tf_op jit(solution)/shard_map/ppermute | solution.py:556
  46.7 4.1 %collective-permute-start.6 = (bf16[1280,512]{1,0:T(8,128)(2,1)S(1)}, bf16[1280,512]{1,0:T(8,128)(2,1)S(1)}, u32[]{:S(2)}, u32[]{:S(2)}) collective-permute-start(bf16[1280,512]{1,0:T(8,128)(2,1)S(1)} %pad_maximum_fusion.w0_ref), channel_id=1, source_target_pairs={{0,4},{4,0},{1,5},{5,1},{2,6},{6,2},{3,7},{7,3},{8,12},{12,8},{9,1... | collective-permute-start | bytes 3932168 | tf_op jit(solution)/shard_map/ppermute | solution.py:556
  55.4 8.6 %prefill_attention.1.a_ref = bf16[512,512]{1,0:T(8,128)(2,1)S(1)} custom-call(s32[12]{0:T(128)S(1)} %concatenate.39.info, bf16[512,512]{1,0:T(8,128)(2,1)S(1)} %copy-done.2, bf16[512,512]{1,0:T(8,128)(2,1)S(1)} %bitcast.19, bf16[512,512]{1,0:T(8,128)(2,1)S(1)} %bitcast.20, bf16[1,2,2048,256]{3,2,1,0:T(8,128)(2,1)S(1)} %copy-done.1, ...), custom_call_target="tpu_custom_call" | custom-call | flops 2684354560 | bytes 4194304 | tf_op jit(solution)/shard_map/prefill_attention/pallas_call | solution.py:119
  64.1 2.2 %project.1 = (f32[256,512]{1,0:T(8,128)S(1)}, bf16[256,512]{1,0:T(8,128)(2,1)S(1)}, bf16[256,512]{1,0:T(8,128)(2,1)S(1)}, bf16[256,512]{1,0:T(8,128)(2,1)S(1)}, ...) custom-call(s32[12]{0:T(128)S(1)} %concatenate.39.info, ...), custom_call_target="tpu_custom_call" | custom-call | flops 1073741824 | bytes 6291456 | tf_op jit(solution)/shard_map/project/pallas_call | solution.py:261
  66.4 3.8 %decode_attention.1 = bf16[8,256]{1,0:T(8,128)(2,1)S(1)} custom-call(s32[12]{0:T(128)S(1)} %concatenate.39.info, bf16[16,80,512]{2,1,0:T(8,128)(2,1)S(1)} %bitcast.17, bf16[16,80,512]{2,1,0:T(8,128)(2,1)S(1)} %bitcast.18, bf16[3,2,2048,256]{3,2,1,0:T(8,128)(2,1)S(1)} %bitcast.16, f32[520,128]{1,0:T(8,128)S(1)} %get-tuple-element.57.cos_ref, ...), custom_call_target="tpu_custom_call" | custom-call | flops 1610612736 | bytes 7340032 | tf_op jit(solution)/shard_map/decode_attention/pallas_call | solution.py:208
  70.8 3.3 %collective-permute-start.18 = (bf16[8,256]{1,0:T(8,128)(2,1)S(1)}, bf16[8,256]{1,0:T(8,128)(2,1)S(1)}, u32[]{:S(2)}, u32[]{:S(2)}) collective-permute-start(bf16[8,256]{1,0:T(8,128)(2,1)S(1)} %decode_attention.1), channel_id=1, source_target_pairs={{0,24},{8,16},{16,8},{24,0},{1,25},{9,17},{17,9},{25,1},{2,26},{10... | collective-permute-start | bytes 12296 | tf_op jit(solution)/shard_map/ppermute | solution.py:556
  75.8 3.3 %collective-permute-start.8 = (bf16[256,512]{1,0:T(8,128)(2,1)S(1)}, bf16[256,512]{1,0:T(8,128)(2,1)S(1)}, u32[]{:S(2)}, u32[]{:S(2)}) collective-permute-start(bf16[256,512]{1,0:T(8,128)(2,1)S(1)} %get-tuple-element.30), channel_id=1, source_target_pairs={{0,2},{1,3},{2,0},{3,1},{4,6},{5,7},{6,4},{7,5},{8,10},{9,11},{10,... | collective-permute-start | bytes 786440 | tf_op jit(solution)/shard_map/ppermute | solution.py:556
  79.7 3.5 %collective-permute-done.19 = bf16[32,256]{1,0:T(8,128)(2,1)S(1)} collective-permute-done((bf16[32,256]{1,0:T(8,128)(2,1)S(1)}, bf16[32,256]{1,0:T(8,128)(2,1)S(1)}, u32[]{:S(2)}, u32[]{:S(2)}) %collective-permute-start.19) | collective-permute-done | bytes 16416 | tf_op jit(solution)/shard_map/ppermute | solution.py:556
  83.1 4.6 %collective-permute-done.20 = bf16[32,256]{1,0:T(8,128)(2,1)S(1)} collective-permute-done((bf16[32,256]{1,0:T(8,128)(2,1)S(1)}, bf16[32,256]{1,0:T(8,128)(2,1)S(1)}, u32[]{:S(2)}, u32[]{:S(2)}) %collective-permute-start.20) | collective-permute-done | bytes 16416 | tf_op jit(solution)/shard_map/ppermute | solution.py:556
  87.9 4.6 %collective-permute-done.21 = bf16[32,256]{1,0:T(8,128)(2,1)S(1)} collective-permute-done((bf16[32,256]{1,0:T(8,128)(2,1)S(1)}, bf16[32,256]{1,0:T(8,128)(2,1)S(1)}, u32[]{:S(2)}, u32[]{:S(2)}) %collective-permute-start.21) | collective-permute-done | bytes 16416 | tf_op jit(solution)/shard_map/ppermute | solution.py:556
  92.5 5.3 %collective-permute-start.22 = (bf16[128,256]{1,0:T(8,128)(2,1)S(1)}, bf16[128,256]{1,0:T(8,128)(2,1)S(1)}, u32[]{:S(2)}, u32[]{:S(2)}) collective-permute-start(bf16[128,256]{1,0:T(8,128)(2,1)S(1)} %pad_maximum_fusion.6), channel_id=1, source_target_pairs={{0,4},{4,0},{1,5},{5,1},{2,6},{6,2},{3,7},{7,3},{8,12},{12,8},{9,1... | collective-permute-start | bytes 196616 | tf_op jit(solution)/shard_map/ppermute | solution.py:556
  101.5 3.0 %collective-permute-start.11 = (bf16[256,512]{1,0:T(8,128)(2,1)S(1)}, bf16[256,512]{1,0:T(8,128)(2,1)S(1)}, u32[]{:S(2)}, u32[]{:S(2)}) collective-permute-start(bf16[256,512]{1,0:T(8,128)(2,1)S(1)} %get-tuple-element.33.refs_0_), channel_id=1, source_target_pairs={{0,2},{1,3},{2,0},{3,1},{4,6},{5,7},{6,4},{7,5},{8,10},{9,11},{10,... | collective-permute-start | bytes 786440 | tf_op jit(solution)/shard_map/ppermute | solution.py:556
  107.3 6.3 %collective-permute-done.25.refs_4_ = bf16[256,512]{1,0:T(8,128)(2,1)S(1)} collective-permute-done((bf16[256,512]{1,0:T(8,128)(2,1)S(1)}, bf16[256,512]{1,0:T(8,128)(2,1)S(1)}, u32[]{:S(2)}, u32[]{:S(2)}) %collective-permute-start.25) | collective-permute-done | bytes 262176 | tf_op jit(solution)/shard_map/ppermute | solution.py:556
  114.4 2.9 %collective-permute-start.27 = (bf16[288,512]{1,0:T(8,128)(2,1)S(1)}, bf16[288,512]{1,0:T(8,128)(2,1)S(1)}, u32[]{:S(2)}, u32[]{:S(2)}) collective-permute-start(bf16[288,512]{1,0:T(8,128)(2,1)S(1)} %get-tuple-element.48.refs_0_), channel_id=1, source_target_pairs={{0,2},{1,3},{2,0},{3,1},{4,6},{5,7},{6,4},{7,5},{8,10},{9,11},{10,... | collective-permute-start | bytes 884744 | tf_op jit(solution)/shard_map/ppermute | solution.py:556
  118.5 6.2 %collective-permute-done.12.refs_3_ = bf16[256,512]{1,0:T(8,128)(2,1)S(1)} collective-permute-done((bf16[256,512]{1,0:T(8,128)(2,1)S(1)}, bf16[256,512]{1,0:T(8,128)(2,1)S(1)}, u32[]{:S(2)}, u32[]{:S(2)}) %collective-permute-start.12) | collective-permute-done | bytes 262176 | tf_op jit(solution)/shard_map/ppermute | solution.py:556
  124.8 13.6 %ffn.1 = (f32[256,512]{1,0:T(8,128)S(1)}, bf16[256,512]{1,0:T(8,128)(2,1)S(1)}, bf16[256,512]{1,0:T(8,128)(2,1)S(1)}, bf16[256,512]{1,0:T(8,128)(2,1)S(1)}) custom-call(s32[12]{0:T(128)S(1)} %concatenate.39.info, bf16[256,512]{1,0:T(8,128)(2,1)S(1)} %get-tuple-element.33.refs_0_, bf16[256,512]{1,0:T(8,128)(2,1)S(1)} %collective-permute-done.10.refs_1_, ...), custom_call_target="tpu_custom_call" | custom-call | flops 4831838208 | bytes 20971520 | tf_op jit(solution)/shard_map/ffn/pallas_call | solution.py:396
  138.7 9.4 %ffn_late.1 = (f32[272,512]{1,0:T(8,128)S(1)}, bf16[272,512]{1,0:T(8,128)(2,1)S(1)}, bf16[272,512]{1,0:T(8,128)(2,1)S(1)}, bf16[272,512]{1,0:T(8,128)(2,1)S(1)}, f32[8,512]{1,0:T(8,128)S(1)}) custom-call(s32[12]{0:T(128)S(1)} %concatenate.39.info, bf16[288,512]{1,0:T(8,128)(2,1)S(1)} %get-tuple-element.48.refs_0_, ...), custom_call_target="tpu_custom_call" | custom-call | flops 5133828096 | bytes 20971520 | tf_op jit(solution)/shard_map/ffn_late/pallas_call | solution.py:495
  154.7 13.8 %collective-permute-done.14.r2 = bf16[256,512]{1,0:T(8,128)(2,1)S(1)} collective-permute-done((bf16[256,512]{1,0:T(8,128)(2,1)S(1)}, bf16[256,512]{1,0:T(8,128)(2,1)S(1)}, u32[]{:S(2)}, u32[]{:S(2)}) %collective-permute-start.14) | collective-permute-done | bytes 262176 | tf_op jit(solution)/shard_map/ppermute | solution.py:556
  168.5 7.9 %collective-permute-done.15.r3 = bf16[256,512]{1,0:T(8,128)(2,1)S(1)} collective-permute-done((bf16[256,512]{1,0:T(8,128)(2,1)S(1)}, bf16[256,512]{1,0:T(8,128)(2,1)S(1)}, u32[]{:S(2)}, u32[]{:S(2)}) %collective-permute-start.15) | collective-permute-done | bytes 262176 | tf_op jit(solution)/shard_map/ppermute | solution.py:556
  (103 shorter events, 30.2 us)
Async XLA Ops:
  7.2 117.6 %all-gather.2.cloned.1.call-start = ((), (), s32[]{:S(2)}) async-start(), calls=%async_computation | async-start | bytes 19464192 | tf_op jit(solution)/shard_map/all_gather | solution.py:593
  20.0 9.7 %collective-permute-start.3 = (bf16[320,512]{1,0:T(8,128)(2,1)S(1)}, bf16[320,512]{1,0:T(8,128)(2,1)S(1)}, u32[]{:S(2)}, u32[]{:S(2)}) collective-permute-start(bf16[320,512]{1,0:T(8,128)(2,1)S(1)} %pad_maximum_fusion.2), channel_id=1, source_target_pairs={{0,32},{32,0},{64,96},{96,64},{1,33},{33,1},{65,97},{97,65},{2,34}... | collective-permute-start | bytes 983048 | tf_op jit(solution)/shard_map/ppermute | solution.py:556
  21.3 25.3 %collective-permute-start.4 = (bf16[320,512]{1,0:T(8,128)(2,1)S(1)}, bf16[320,512]{1,0:T(8,128)(2,1)S(1)}, u32[]{:S(2)}, u32[]{:S(2)}) collective-permute-start(bf16[320,512]{1,0:T(8,128)(2,1)S(1)} %pad_maximum_fusion.2), channel_id=1, source_target_pairs={{0,64},{32,96},{64,0},{96,32},{1,65},{33,97},{65,1},{97,33},{2,66}... | collective-permute-start | bytes 983048 | tf_op jit(solution)/shard_map/ppermute | solution.py:556
  23.8 22.8 %collective-permute-start.5 = (bf16[320,512]{1,0:T(8,128)(2,1)S(1)}, bf16[320,512]{1,0:T(8,128)(2,1)S(1)}, u32[]{:S(2)}, u32[]{:S(2)}) collective-permute-start(bf16[320,512]{1,0:T(8,128)(2,1)S(1)} %pad_maximum_fusion.2), channel_id=1, source_target_pairs={{0,96},{32,64},{64,32},{96,0},{1,97},{33,65},{65,33},{97,1},{2,98}... | collective-permute-start | bytes 983048 | tf_op jit(solution)/shard_map/ppermute | solution.py:556
  46.7 17.4 %collective-permute-start.6 = (bf16[1280,512]{1,0:T(8,128)(2,1)S(1)}, bf16[1280,512]{1,0:T(8,128)(2,1)S(1)}, u32[]{:S(2)}, u32[]{:S(2)}) collective-permute-start(bf16[1280,512]{1,0:T(8,128)(2,1)S(1)} %pad_maximum_fusion.w0_ref), channel_id=1, source_target_pairs={{0,4},{4,0},{1,5},{5,1},{2,6},{6,2},{3,7},{7,3},{8,12},{12,8},{9,1... | collective-permute-start | bytes 3932168 | tf_op jit(solution)/shard_map/ppermute | solution.py:556
  74.1 30.3 %collective-permute-start.23 = (bf16[256,512]{1,0:T(8,128)(2,1)S(1)}, bf16[256,512]{1,0:T(8,128)(2,1)S(1)}, u32[]{:S(2)}, u32[]{:S(2)}) collective-permute-start(bf16[256,512]{1,0:T(8,128)(2,1)S(1)} %get-tuple-element.44), channel_id=1, source_target_pairs={{0,1},{1,0},{2,3},{3,2},{4,5},{5,4},{6,7},{7,6},{8,9},{9,8},{10,11... | collective-permute-start | bytes 786440 | tf_op jit(solution)/shard_map/ppermute | solution.py:556
  75.8 22.0 %collective-permute-start.7 = (bf16[256,512]{1,0:T(8,128)(2,1)S(1)}, bf16[256,512]{1,0:T(8,128)(2,1)S(1)}, u32[]{:S(2)}, u32[]{:S(2)}) collective-permute-start(bf16[256,512]{1,0:T(8,128)(2,1)S(1)} %get-tuple-element.29), channel_id=1, source_target_pairs={{0,1},{1,0},{2,3},{3,2},{4,5},{5,4},{6,7},{7,6},{8,9},{9,8},{10,11... | collective-permute-start | bytes 786440 | tf_op jit(solution)/shard_map/ppermute | solution.py:556
  75.8 24.0 %collective-permute-start.8 = (bf16[256,512]{1,0:T(8,128)(2,1)S(1)}, bf16[256,512]{1,0:T(8,128)(2,1)S(1)}, u32[]{:S(2)}, u32[]{:S(2)}) collective-permute-start(bf16[256,512]{1,0:T(8,128)(2,1)S(1)} %get-tuple-element.30), channel_id=1, source_target_pairs={{0,2},{1,3},{2,0},{3,1},{4,6},{5,7},{6,4},{7,5},{8,10},{9,11},{10,... | collective-permute-start | bytes 786440 | tf_op jit(solution)/shard_map/ppermute | solution.py:556
  79.1 21.1 %collective-permute-start.9 = (bf16[256,512]{1,0:T(8,128)(2,1)S(1)}, bf16[256,512]{1,0:T(8,128)(2,1)S(1)}, u32[]{:S(2)}, u32[]{:S(2)}) collective-permute-start(bf16[256,512]{1,0:T(8,128)(2,1)S(1)} %get-tuple-element.31), channel_id=1, source_target_pairs={{0,3},{1,2},{2,1},{3,0},{4,7},{5,6},{6,5},{7,4},{8,11},{9,10},{10,... | collective-permute-start | bytes 786440 | tf_op jit(solution)/shard_map/ppermute | solution.py:556
  92.5 8.9 %collective-permute-start.22 = (bf16[128,256]{1,0:T(8,128)(2,1)S(1)}, bf16[128,256]{1,0:T(8,128)(2,1)S(1)}, u32[]{:S(2)}, u32[]{:S(2)}) collective-permute-start(bf16[128,256]{1,0:T(8,128)(2,1)S(1)} %pad_maximum_fusion.6), channel_id=1, source_target_pairs={{0,4},{4,0},{1,5},{5,1},{2,6},{6,2},{3,7},{7,3},{8,12},{12,8},{9,1... | collective-permute-start | bytes 196616 | tf_op jit(solution)/shard_map/ppermute | solution.py:556
  97.8 9.5 %collective-permute-start.24 = (bf16[256,512]{1,0:T(8,128)(2,1)S(1)}, bf16[256,512]{1,0:T(8,128)(2,1)S(1)}, u32[]{:S(2)}, u32[]{:S(2)}) collective-permute-start(bf16[256,512]{1,0:T(8,128)(2,1)S(1)} %get-tuple-element.45), channel_id=1, source_target_pairs={{0,2},{1,3},{2,0},{3,1},{4,6},{5,7},{6,4},{7,5},{8,10},{9,11},{10,... | collective-permute-start | bytes 786440 | tf_op jit(solution)/shard_map/ppermute | solution.py:556
  99.8 13.8 %collective-permute-start.25 = (bf16[256,512]{1,0:T(8,128)(2,1)S(1)}, bf16[256,512]{1,0:T(8,128)(2,1)S(1)}, u32[]{:S(2)}, u32[]{:S(2)}) collective-permute-start(bf16[256,512]{1,0:T(8,128)(2,1)S(1)} %get-tuple-element.46), channel_id=1, source_target_pairs={{0,3},{1,2},{2,1},{3,0},{4,7},{5,6},{6,5},{7,4},{8,11},{9,10},{10,... | collective-permute-start | bytes 786440 | tf_op jit(solution)/shard_map/ppermute | solution.py:556
  101.0 16.4 %collective-permute-start.10 = (bf16[256,512]{1,0:T(8,128)(2,1)S(1)}, bf16[256,512]{1,0:T(8,128)(2,1)S(1)}, u32[]{:S(2)}, u32[]{:S(2)}) collective-permute-start(bf16[256,512]{1,0:T(8,128)(2,1)S(1)} %get-tuple-element.33.refs_0_), channel_id=1, source_target_pairs={{0,1},{1,0},{2,3},{3,2},{4,5},{5,4},{6,7},{7,6},{8,9},{9,8},{10,11... | collective-permute-start | bytes 786440 | tf_op jit(solution)/shard_map/ppermute | solution.py:556
  101.5 17.1 %collective-permute-start.11 = (bf16[256,512]{1,0:T(8,128)(2,1)S(1)}, bf16[256,512]{1,0:T(8,128)(2,1)S(1)}, u32[]{:S(2)}, u32[]{:S(2)}) collective-permute-start(bf16[256,512]{1,0:T(8,128)(2,1)S(1)} %get-tuple-element.33.refs_0_), channel_id=1, source_target_pairs={{0,2},{1,3},{2,0},{3,1},{4,6},{5,7},{6,4},{7,5},{8,10},{9,11},{10,... | collective-permute-start | bytes 786440 | tf_op jit(solution)/shard_map/ppermute | solution.py:556
  104.4 20.4 %collective-permute-start.12 = (bf16[256,512]{1,0:T(8,128)(2,1)S(1)}, bf16[256,512]{1,0:T(8,128)(2,1)S(1)}, u32[]{:S(2)}, u32[]{:S(2)}) collective-permute-start(bf16[256,512]{1,0:T(8,128)(2,1)S(1)} %get-tuple-element.33.refs_0_), channel_id=1, source_target_pairs={{0,3},{1,2},{2,1},{3,0},{4,7},{5,6},{6,5},{7,4},{8,11},{9,10},{10,... | collective-permute-start | bytes 786440 | tf_op jit(solution)/shard_map/ppermute | solution.py:556
  114.3 24.4 %collective-permute-start.26 = (bf16[288,512]{1,0:T(8,128)(2,1)S(1)}, bf16[288,512]{1,0:T(8,128)(2,1)S(1)}, u32[]{:S(2)}, u32[]{:S(2)}) collective-permute-start(bf16[288,512]{1,0:T(8,128)(2,1)S(1)} %get-tuple-element.48.refs_0_), channel_id=1, source_target_pairs={{0,1},{1,0},{2,3},{3,2},{4,5},{5,4},{6,7},{7,6},{8,9},{9,8},{10,11... | collective-permute-start | bytes 884744 | tf_op jit(solution)/shard_map/ppermute | solution.py:556
  114.4 24.3 %collective-permute-start.27 = (bf16[288,512]{1,0:T(8,128)(2,1)S(1)}, bf16[288,512]{1,0:T(8,128)(2,1)S(1)}, u32[]{:S(2)}, u32[]{:S(2)}) collective-permute-start(bf16[288,512]{1,0:T(8,128)(2,1)S(1)} %get-tuple-element.48.refs_0_), channel_id=1, source_target_pairs={{0,2},{1,3},{2,0},{3,1},{4,6},{5,7},{6,4},{7,5},{8,10},{9,11},{10,... | collective-permute-start | bytes 884744 | tf_op jit(solution)/shard_map/ppermute | solution.py:556
  117.3 21.4 %collective-permute-start.28 = (bf16[288,512]{1,0:T(8,128)(2,1)S(1)}, bf16[288,512]{1,0:T(8,128)(2,1)S(1)}, u32[]{:S(2)}, u32[]{:S(2)}) collective-permute-start(bf16[288,512]{1,0:T(8,128)(2,1)S(1)} %get-tuple-element.48.refs_0_), channel_id=1, source_target_pairs={{0,3},{1,2},{2,1},{3,0},{4,7},{5,6},{6,5},{7,4},{8,11},{9,10},{10,... | collective-permute-start | bytes 884744 | tf_op jit(solution)/shard_map/ppermute | solution.py:556
  138.4 15.3 %collective-permute-start.13 = (bf16[256,512]{1,0:T(8,128)(2,1)S(1)}, bf16[256,512]{1,0:T(8,128)(2,1)S(1)}, u32[]{:S(2)}, u32[]{:S(2)}) collective-permute-start(bf16[256,512]{1,0:T(8,128)(2,1)S(1)} %get-tuple-element.35), channel_id=1, source_target_pairs={{0,1},{1,0},{2,3},{3,2},{4,5},{5,4},{6,7},{7,6},{8,9},{9,8},{10,11... | collective-permute-start | bytes 786440 | tf_op jit(solution)/shard_map/ppermute | solution.py:556
  148.1 29.1 %collective-permute-start.29 = (bf16[272,512]{1,0:T(8,128)(2,1)S(1)}, bf16[272,512]{1,0:T(8,128)(2,1)S(1)}, u32[]{:S(2)}, u32[]{:S(2)}) collective-permute-start(bf16[272,512]{1,0:T(8,128)(2,1)S(1)} %get-tuple-element.51), channel_id=1, source_target_pairs={{0,1},{1,0},{2,3},{3,2},{4,5},{5,4},{6,7},{7,6},{8,9},{9,8},{10,11... | collective-permute-start | bytes 835592 | tf_op jit(solution)/shard_map/ppermute | solution.py:556
  149.6 27.6 %collective-permute-start.30 = (bf16[272,512]{1,0:T(8,128)(2,1)S(1)}, bf16[272,512]{1,0:T(8,128)(2,1)S(1)}, u32[]{:S(2)}, u32[]{:S(2)}) collective-permute-start(bf16[272,512]{1,0:T(8,128)(2,1)S(1)} %get-tuple-element.52), channel_id=1, source_target_pairs={{0,2},{1,3},{2,0},{3,1},{4,6},{5,7},{6,4},{7,5},{8,10},{9,11},{10,... | collective-permute-start | bytes 835592 | tf_op jit(solution)/shard_map/ppermute | solution.py:556
  151.2 26.1 %collective-permute-start.31 = (bf16[272,512]{1,0:T(8,128)(2,1)S(1)}, bf16[272,512]{1,0:T(8,128)(2,1)S(1)}, u32[]{:S(2)}, u32[]{:S(2)}) collective-permute-start(bf16[272,512]{1,0:T(8,128)(2,1)S(1)} %get-tuple-element.53), channel_id=1, source_target_pairs={{0,3},{1,2},{2,1},{3,0},{4,7},{5,6},{6,5},{7,4},{8,11},{9,10},{10,... | collective-permute-start | bytes 835592 | tf_op jit(solution)/shard_map/ppermute | solution.py:556
  152.1 16.4 %collective-permute-start.14 = (bf16[256,512]{1,0:T(8,128)(2,1)S(1)}, bf16[256,512]{1,0:T(8,128)(2,1)S(1)}, u32[]{:S(2)}, u32[]{:S(2)}) collective-permute-start(bf16[256,512]{1,0:T(8,128)(2,1)S(1)} %get-tuple-element.36), channel_id=1, source_target_pairs={{0,2},{1,3},{2,0},{3,1},{4,6},{5,7},{6,4},{7,5},{8,10},{9,11},{10,... | collective-permute-start | bytes 786440 | tf_op jit(solution)/shard_map/ppermute | solution.py:556
  153.7 22.7 %collective-permute-start.15 = (bf16[256,512]{1,0:T(8,128)(2,1)S(1)}, bf16[256,512]{1,0:T(8,128)(2,1)S(1)}, u32[]{:S(2)}, u32[]{:S(2)}) collective-permute-start(bf16[256,512]{1,0:T(8,128)(2,1)S(1)} %get-tuple-element.37), channel_id=1, source_target_pairs={{0,3},{1,2},{2,1},{3,0},{4,7},{5,6},{6,5},{7,4},{8,11},{9,10},{10,... | collective-permute-start | bytes 786440 | tf_op jit(solution)/shard_map/ppermute | solution.py:556
  (22 other events, 208.7 us)
Sparse Core Ops, SparseCore 0:
  10.3 90.9 all-gather.1

commit v4 on v3

--- a/solution.py
+++ b/solution.py
@@ -14,7 +14,9 @@
 HEAD_SIZE = 128
 NEW = 512
 EXTRA = 16
-SPLIT = 256
+HALF = 256
+SPLIT = 320
+REST = 192
 BLOCK = 512
 WIDTH = 2048
 CACHE = 2048
@@ -66,16 +68,16 @@
     def run(length, masked):
         old_keys = c_ref[0, 0, :length, :]
         old_values = c_ref[0, 1, :length, :]
-        for r in range(NEW // SPLIT):
-            seen = (r + 1) * SPLIT
+        for r in range(NEW // HALF):
+            seen = (r + 1) * HALF
             for h in range(2):
-                q = qr[r * SPLIT : seen, h * HEAD_SIZE : (h + 1) * HEAD_SIZE]
+                q = qr[r * HALF : seen, h * HEAD_SIZE : (h + 1) * HEAD_SIZE]
                 old = mm(q, old_keys, NT)
                 if masked:
                     at = lax.broadcasted_iota(jnp.int32, old.shape, 1)
                     old = jnp.where(at < start, old, UNSEEN)
                 new = mm(q, kr[:seen, :], NT)
-                row = lax.broadcasted_iota(jnp.int32, new.shape, 0) + r * SPLIT
+                row = lax.broadcasted_iota(jnp.int32, new.shape, 0) + r * HALF
                 col = lax.broadcasted_iota(jnp.int32, new.shape, 1)
                 new = jnp.where(col <= row, new, UNSEEN)
                 top = jnp.maximum(
@@ -85,7 +87,7 @@
                 new = jnp.exp2((new - top) * EXP_SCALE)
                 total = jnp.sum(old, axis=1, keepdims=True) + jnp.sum(new, axis=1, keepdims=True)
                 blend = mm(old.astype(BF16), old_values) + mm(new.astype(BF16), vf_ref[:seen, :])
-                o_ref[r * SPLIT : seen, h * HEAD_SIZE : (h + 1) * HEAD_SIZE] = (
+                o_ref[r * HALF : seen, h * HEAD_SIZE : (h + 1) * HEAD_SIZE] = (
                     blend / total
                 ).astype(BF16)
 
@@ -257,12 +259,14 @@
 
 
 def project_call(info, att, prefill_states, *weights):
-    half = [shaped(SPLIT, BLOCK, F32)] + [shaped(SPLIT, BLOCK, BF16)] * 3
+    shapes = []
+    for rows in (SPLIT, REST):
+        shapes += [shaped(rows, BLOCK, F32)] + [shaped(rows, BLOCK, BF16)] * 3
     return pl.pallas_call(
         project_kernel,
         in_specs=[SM] + [VM] * 4,
         out_specs=[VM] * 9,
-        out_shape=half + half + [shaped(WIDTH, BLOCK, BF16)],
+        out_shape=shapes + [shaped(WIDTH, BLOCK, BF16)],
         compiler_params=limit(20),
         cost_estimate=pl.CostEstimate(
             flops=2 * NEW * BLOCK * WIDTH, transcendentals=0, bytes_accessed=6 * 1024 * 1024
@@ -312,19 +316,20 @@
     total = own_ref[...] + r1[...].astype(F32) + r2[...].astype(F32) + r3[...].astype(F32)
     summed_ref[...] = total
     at = pl.multiple_of(info[AT_HEAD] * BLOCK, BLOCK)
-    g_ref[:SPLIT, :] = (total * gain_ref[:, pl.ds(at, BLOCK)].astype(F32)).astype(BF16)
+    rows = own_ref.shape[0]
+    g_ref[:rows, :] = (total * gain_ref[:, pl.ds(at, BLOCK)].astype(F32)).astype(BF16)
     if len(refs) == 7:
-        g_ref[SPLIT:, :] = refs[0][...]
+        g_ref[rows:, :] = refs[0][...]
 
 
 def combine_call(info, gain, own, parts, late=()):
-    sent = SPLIT + 32 * len(late)
+    rows = own.shape[0]
     return pl.pallas_call(
         combine_kernel,
         in_specs=[SM] + [VM] * (5 + len(late)),
         out_specs=[VM] * 2,
-        out_shape=[shaped(SPLIT, BLOCK, F32), shaped(sent, BLOCK, BF16)],
-        compiler_params=limit(8),
+        out_shape=[shaped(rows, BLOCK, F32), shaped(rows + 32 * len(late), BLOCK, BF16)],
+        compiler_params=limit(10),
     )(info, gain, *late, own, *parts)
 
 
@@ -397,7 +402,7 @@
         ffn_kernel,
         grid_spec=grid,
         out_shape=[shaped(SPLIT, BLOCK, F32)] + [shaped(SPLIT, BLOCK, BF16)] * 3,
-        compiler_params=limit(30),
+        compiler_params=limit(32),
         cost_estimate=pl.CostEstimate(
             flops=6 * SPLIT * HIDDEN * WIDTH,
             transcendentals=SPLIT * HIDDEN,
@@ -419,34 +424,34 @@
 
     @pl.when(i == 0)
     def _():
-        squares = jnp.zeros((SPLIT, 1), F32)
+        squares = jnp.zeros((REST, 1), F32)
         for k, part in enumerate(parts):
             at = pl.multiple_of(lax.bitwise_xor(head, k) * BLOCK, BLOCK)
-            value = part[:SPLIT, :]
-            n_sc[:SPLIT, pl.ds(at, BLOCK)] = value
+            value = part[:REST, :]
+            n_sc[:REST, pl.ds(at, BLOCK)] = value
             plain = value.astype(F32) / gain_ref[:, pl.ds(at, BLOCK)].astype(F32)
             squares = squares + jnp.sum(plain * plain, axis=1, keepdims=True)
-        r_sc[:SPLIT, :] = jnp.broadcast_to(
-            lax.rsqrt(squares * (1.0 / WIDTH) + norm_eps), (SPLIT, 128)
+        r_sc[:REST, :] = jnp.broadcast_to(
+            lax.rsqrt(squares * (1.0 / WIDTH) + norm_eps), (REST, 128)
         )
         squares = jnp.zeros((8, 1), F32)
         for j in range(4):
-            rows = slice(SPLIT + 8 * j, SPLIT + 8 * j + 8)
+            rows = slice(REST + 8 * j, REST + 8 * j + 8)
             lanes = slice(j * BLOCK, (j + 1) * BLOCK)
             both = sum(part[rows, :].astype(F32) for part in parts)
             total = both + pltpu.roll(both, 5, 0)
             squares = squares + jnp.sum(total * total, axis=1, keepdims=True)
             scaled = total * gain_ref[:, lanes].astype(F32)
             scaled = jnp.concatenate([scaled, jnp.zeros_like(scaled)], axis=0)
-            n_sc[SPLIT:, lanes] = scaled.astype(BF16)
+            n_sc[REST:, lanes] = scaled.astype(BF16)
 
             @pl.when(head == j)
             def _():
                 refs[12][...] = total
 
         scale = lax.rsqrt(squares * (1.0 / WIDTH) + norm_eps)
-        r_sc[SPLIT : SPLIT + 8, :] = jnp.broadcast_to(scale, (8, 128))
-        r_sc[SPLIT + 8 :, :] = jnp.zeros((8, 128), F32)
+        r_sc[REST : REST + 8, :] = jnp.broadcast_to(scale, (8, 128))
+        r_sc[REST + 8 :, :] = jnp.zeros((8, 128), F32)
 
     @pl.when(i < GATE_TILES)
     def _():
@@ -464,8 +469,8 @@
 
 
 def ffn_late_call(info, parts, gain, weights):
-    rows = SPLIT + EXTRA
-    sent = SPLIT + 32
+    rows = REST + EXTRA
+    sent = REST + 32
     last = GATE_TILES - 1
 
     def down_map(i, s):
@@ -515,35 +520,26 @@
 
 def finish_second(old_ref, s_ref, l_ref, own, r1, r2, r3, p_ref, d_ref):
     total = own[...] + r1[...].astype(F32) + r2[...].astype(F32) + r3[...].astype(F32)
-    p_ref[...] = (s_ref[...] + total[:SPLIT, :]).astype(BF16)
-    d_ref[...] = (l_ref[...] + total[SPLIT : SPLIT + 8, :]).astype(BF16)[:3, :]
+    p_ref[:SPLIT, :] = old_ref[...]
+    p_ref[SPLIT:, :] = (s_ref[...] + total[:REST, :]).astype(BF16)
+    d_ref[...] = (l_ref[...] + total[REST : REST + 8, :]).astype(BF16)[:3, :]
 
 
 def finish_call(summed, own, parts, old=None, late=None):
-    rows = SPLIT if old is None else SPLIT + EXTRA
-
-    def block(n):
-        return pl.BlockSpec((n, BLOCK), lambda i: (0, 0))
-
-    first = pl.BlockSpec((SPLIT, BLOCK), lambda i: (0 if old is None else 1, 0))
-    in_specs = [block(SPLIT)] + [block(rows)] * 4
     if old is None:
         return pl.pallas_call(
             finish_first,
-            grid=(1,),
-            in_specs=in_specs,
-            out_specs=first,
-            out_shape=shaped(NEW, BLOCK, BF16),
+            in_specs=[VM] * 5,
+            out_specs=VM,
+            out_shape=shaped(SPLIT, BLOCK, BF16),
             compiler_params=limit(6),
             name="finish_0",
         )(summed, own, *parts)
     return pl.pallas_call(
         finish_second,
-        grid=(1,),
-        in_specs=[pl.BlockSpec(memory_space=pl.ANY), block(SPLIT), block(8)] + [block(rows)] * 4,
-        out_specs=[first, block(3)],
+        in_specs=[VM] * 7,
+        out_specs=[VM] * 2,
         out_shape=[shaped(NEW, BLOCK, BF16), shaped(3, BLOCK, BF16)],
-        input_output_aliases={0: 0},
         compiler_params=limit(6),
         name="finish_1",
     )(old, summed, late, own, *parts)

time: 186 us -> 171 us (0.919)
  waiting for transfers between devices: 76.5 us -> 60 us
    ppermute x32, waiting for transfers between devices: 76.5 us -> 59.9 us  [swap(): return lax.ppermute(value, axis, [(i, i ^ k) for i in range(SIZE[axis])])]
  transfers between devices with their start and end apart: 33 -> 33, of which waited for: 13 -> 15; matrix products, arithmetic and copies ran while one was open for 2% -> 2% of each run, Pallas kernels for 22% -> 24%
where the time goes in v4:
time: 171 us; the launch traced here: 169 us
  waiting for transfers between devices  60 us (35%)
  starting transfers between devices  45.8 us (27%)
  Pallas kernels  41.9 us (25%)
  between operations  15 us (9%)
  other arithmetic  3.43 us (2%)
  local copies, waits for them, and re-layouts  2.93 us (2%)
    ppermute x32, waiting for transfers between devices, swap(): return lax.ppermute(value, axis, [(i, i ^ k) for i in range(SIZE[axis])])  59.9 us
    ppermute x32, starting transfers between devices, swap(): return lax.ppermute(value, axis, [(i, i ^ k) for i in range(SIZE[axis])])  45.7 us
    pallas_call x1, Pallas kernels, ffn_call(): pl.pallas_call(ffn_kernel, grid_spec=grid, out_shape=[shaped(SPLIT, BLOCK...  14.8 us
    pallas_call x1, Pallas kernels, prefill_call(): pl.pallas_call(prefill_kernel, grid_spec=grid, out_shape=jax.ShapeDtypeSt...  8.61 us
    pallas_call x1, Pallas kernels, ffn_late_call(): pl.pallas_call(ffn_late_kernel, grid_spec=grid, out_shape=[shaped(rows, B...  8.58 us
    pallas_call x1, Pallas kernels, decode_call(): pl.pallas_call(decode_kernel, grid_spec=grid, out_shape=jax.ShapeDtypeStr...  3.77 us
  transfers between devices with their start and end apart: 33, of which 15 were waited for; matrix products, arithmetic and copies ran while one was open for 2% of the time, Pallas kernels for 24%

profile of v4, /device:TPU:1, one launch (start us, length us, event | category | flops | bytes accessed | tf_op | source)
XLA Modules:
  0.0 169.0 jit_solution(8901843261861040421)
XLA Ops:
  11.7 2.6 %collective-permute-start.1 = (bf16[80,512]{1,0:T(8,128)(2,1)S(1)}, bf16[80,512]{1,0:T(8,128)(2,1)S(1)}, u32[]{:S(2)}, u32[]{:S(2)}) collective-permute-start(bf16[80,512]{1,0:T(8,128)(2,1)S(1)} %concatenate.44), channel_id=1, source_target_pairs={{0,16},{8,24},{16,0},{24,8},{1,17},{9,25},{17,1},{25,9},{2,18},{10... | collective-permute-start | bytes 245768 | tf_op jit(solution)/shard_map/ppermute | solution.py:552
  14.3 3.3 %collective-permute-done.1 = bf16[80,512]{1,0:T(8,128)(2,1)S(1)} collective-permute-done((bf16[80,512]{1,0:T(8,128)(2,1)S(1)}, bf16[80,512]{1,0:T(8,128)(2,1)S(1)}, u32[]{:S(2)}, u32[]{:S(2)}) %collective-permute-start.1) | collective-permute-done | bytes 81952 | tf_op jit(solution)/shard_map/ppermute | solution.py:552
  17.7 2.3 %collective-permute-done.2 = bf16[80,512]{1,0:T(8,128)(2,1)S(1)} collective-permute-done((bf16[80,512]{1,0:T(8,128)(2,1)S(1)}, bf16[80,512]{1,0:T(8,128)(2,1)S(1)}, u32[]{:S(2)}, u32[]{:S(2)}) %collective-permute-start.2) | collective-permute-done | bytes 81952 | tf_op jit(solution)/shard_map/ppermute | solution.py:552
  21.3 2.5 %collective-permute-start.4 = (bf16[320,512]{1,0:T(8,128)(2,1)S(1)}, bf16[320,512]{1,0:T(8,128)(2,1)S(1)}, u32[]{:S(2)}, u32[]{:S(2)}) collective-permute-start(bf16[320,512]{1,0:T(8,128)(2,1)S(1)} %pad_maximum_fusion.2), channel_id=1, source_target_pairs={{0,64},{32,96},{64,0},{96,32},{1,65},{33,97},{65,1},{97,33},{2,66}... | collective-permute-start | bytes 983048 | tf_op jit(solution)/shard_map/ppermute | solution.py:552
  24.0 5.8 %collective-permute-done.3 = bf16[320,512]{1,0:T(8,128)(2,1)S(1)} collective-permute-done((bf16[320,512]{1,0:T(8,128)(2,1)S(1)}, bf16[320,512]{1,0:T(8,128)(2,1)S(1)}, u32[]{:S(2)}, u32[]{:S(2)}) %collective-permute-start.3) | collective-permute-done | bytes 327712 | tf_op jit(solution)/shard_map/ppermute | solution.py:552
  29.8 16.8 %collective-permute-done.4 = bf16[320,512]{1,0:T(8,128)(2,1)S(1)} collective-permute-done((bf16[320,512]{1,0:T(8,128)(2,1)S(1)}, bf16[320,512]{1,0:T(8,128)(2,1)S(1)}, u32[]{:S(2)}, u32[]{:S(2)}) %collective-permute-start.4) | collective-permute-done | bytes 327712 | tf_op jit(solution)/shard_map/ppermute | solution.py:552
  46.7 4.1 %collective-permute-start.6 = (bf16[1280,512]{1,0:T(8,128)(2,1)S(1)}, bf16[1280,512]{1,0:T(8,128)(2,1)S(1)}, u32[]{:S(2)}, u32[]{:S(2)}) collective-permute-start(bf16[1280,512]{1,0:T(8,128)(2,1)S(1)} %pad_maximum_fusion.w0_ref), channel_id=1, source_target_pairs={{0,4},{4,0},{1,5},{5,1},{2,6},{6,2},{3,7},{7,3},{8,12},{12,8},{9,1... | collective-permute-start | bytes 3932168 | tf_op jit(solution)/shard_map/ppermute | solution.py:552
  55.4 8.6 %prefill_attention.1.a_ref = bf16[512,512]{1,0:T(8,128)(2,1)S(1)} custom-call(s32[12]{0:T(128)S(1)} %concatenate.39.info, bf16[512,512]{1,0:T(8,128)(2,1)S(1)} %copy-done.2, bf16[512,512]{1,0:T(8,128)(2,1)S(1)} %bitcast.19, bf16[512,512]{1,0:T(8,128)(2,1)S(1)} %bitcast.20, bf16[1,2,2048,256]{3,2,1,0:T(8,128)(2,1)S(1)} %copy-done.1, ...), custom_call_target="tpu_custom_call" | custom-call | flops 2684354560 | bytes 4194304 | tf_op jit(solution)/shard_map/prefill_attention/pallas_call | solution.py:121
  64.1 2.2 %project.1 = (f32[320,512]{1,0:T(8,128)S(1)}, bf16[320,512]{1,0:T(8,128)(2,1)S(1)}, bf16[320,512]{1,0:T(8,128)(2,1)S(1)}, bf16[320,512]{1,0:T(8,128)(2,1)S(1)}, ...) custom-call(s32[12]{0:T(128)S(1)} %concatenate.39.info, ...), custom_call_target="tpu_custom_call" | custom-call | flops 1073741824 | bytes 6291456 | tf_op jit(solution)/shard_map/project/pallas_call | solution.py:265
  68.1 3.1 %collective-permute-start.8 = (bf16[320,512]{1,0:T(8,128)(2,1)S(1)}, bf16[320,512]{1,0:T(8,128)(2,1)S(1)}, u32[]{:S(2)}, u32[]{:S(2)}) collective-permute-start(bf16[320,512]{1,0:T(8,128)(2,1)S(1)} %get-tuple-element.30), channel_id=1, source_target_pairs={{0,2},{1,3},{2,0},{3,1},{4,6},{5,7},{6,4},{7,5},{8,10},{9,11},{10,... | collective-permute-start | bytes 983048 | tf_op jit(solution)/shard_map/ppermute | solution.py:552
  71.2 3.8 %decode_attention.1 = bf16[8,256]{1,0:T(8,128)(2,1)S(1)} custom-call(s32[12]{0:T(128)S(1)} %concatenate.39.info, bf16[16,80,512]{2,1,0:T(8,128)(2,1)S(1)} %bitcast.17, bf16[16,80,512]{2,1,0:T(8,128)(2,1)S(1)} %bitcast.18, bf16[3,2,2048,256]{3,2,1,0:T(8,128)(2,1)S(1)} %bitcast.16, f32[520,128]{1,0:T(8,128)S(1)} %get-tuple-element.57.cos_ref, ...), custom_call_target="tpu_custom_call" | custom-call | flops 1610612736 | bytes 7340032 | tf_op jit(solution)/shard_map/decode_attention/pallas_call | solution.py:210
  79.4 3.0 %collective-permute-done.18 = bf16[8,256]{1,0:T(8,128)(2,1)S(1)} collective-permute-done((bf16[8,256]{1,0:T(8,128)(2,1)S(1)}, bf16[8,256]{1,0:T(8,128)(2,1)S(1)}, u32[]{:S(2)}, u32[]{:S(2)}) %collective-permute-start.18) | collective-permute-done | bytes 4128 | tf_op jit(solution)/shard_map/ppermute | solution.py:552
  87.4 3.5 %collective-permute-start.11 = (bf16[320,512]{1,0:T(8,128)(2,1)S(1)}, bf16[320,512]{1,0:T(8,128)(2,1)S(1)}, u32[]{:S(2)}, u32[]{:S(2)}) collective-permute-start(bf16[320,512]{1,0:T(8,128)(2,1)S(1)} %get-tuple-element.33.refs_0_), channel_id=1, source_target_pairs={{0,2},{1,3},{2,0},{3,1},{4,6},{5,7},{6,4},{7,5},{8,10},{9,11},{10,... | collective-permute-start | bytes 983048 | tf_op jit(solution)/shard_map/ppermute | solution.py:552
  91.3 4.4 %collective-permute-start.22 = (bf16[128,256]{1,0:T(8,128)(2,1)S(1)}, bf16[128,256]{1,0:T(8,128)(2,1)S(1)}, u32[]{:S(2)}, u32[]{:S(2)}) collective-permute-start(bf16[128,256]{1,0:T(8,128)(2,1)S(1)} %pad_maximum_fusion.6), channel_id=1, source_target_pairs={{0,4},{4,0},{1,5},{5,1},{2,6},{6,2},{3,7},{7,3},{8,12},{12,8},{9,1... | collective-permute-start | bytes 196616 | tf_op jit(solution)/shard_map/ppermute | solution.py:552
  101.0 5.0 %collective-permute-done.24.refs_3_ = bf16[192,512]{1,0:T(8,128)(2,1)S(1)} collective-permute-done((bf16[192,512]{1,0:T(8,128)(2,1)S(1)}, bf16[192,512]{1,0:T(8,128)(2,1)S(1)}, u32[]{:S(2)}, u32[]{:S(2)}) %collective-permute-start.24) | collective-permute-done | bytes 196640 | tf_op jit(solution)/shard_map/ppermute | solution.py:552
  106.0 8.9 %collective-permute-done.25.refs_4_ = bf16[192,512]{1,0:T(8,128)(2,1)S(1)} collective-permute-done((bf16[192,512]{1,0:T(8,128)(2,1)S(1)}, bf16[192,512]{1,0:T(8,128)(2,1)S(1)}, u32[]{:S(2)}, u32[]{:S(2)}) %collective-permute-start.25) | collective-permute-done | bytes 196640 | tf_op jit(solution)/shard_map/ppermute | solution.py:552
  117.2 2.3 %collective-permute-start.28 = (bf16[224,512]{1,0:T(8,128)(2,1)S(1)}, bf16[224,512]{1,0:T(8,128)(2,1)S(1)}, u32[]{:S(2)}, u32[]{:S(2)}) collective-permute-start(bf16[224,512]{1,0:T(8,128)(2,1)S(1)} %get-tuple-element.48.refs_0_), channel_id=1, source_target_pairs={{0,3},{1,2},{2,1},{3,0},{4,7},{5,6},{6,5},{7,4},{8,11},{9,10},{10,... | collective-permute-start | bytes 688136 | tf_op jit(solution)/shard_map/ppermute | solution.py:552
  119.5 14.8 %ffn.1 = (f32[320,512]{1,0:T(8,128)S(1)}, bf16[320,512]{1,0:T(8,128)(2,1)S(1)}, bf16[320,512]{1,0:T(8,128)(2,1)S(1)}, bf16[320,512]{1,0:T(8,128)(2,1)S(1)}) custom-call(s32[12]{0:T(128)S(1)} %concatenate.39.info, bf16[320,512]{1,0:T(8,128)(2,1)S(1)} %get-tuple-element.33.refs_0_, bf16[320,512]{1,0:T(8,128)(2,1)S(1)} %collective-permute-done.10.refs_1_, ...), custom_call_target="tpu_custom_call" | custom-call | flops 6039797760 | bytes 20971520 | tf_op jit(solution)/shard_map/ffn/pallas_call | solution.py:401
  135.9 2.3 %collective-permute-start.15 = (bf16[320,512]{1,0:T(8,128)(2,1)S(1)}, bf16[320,512]{1,0:T(8,128)(2,1)S(1)}, u32[]{:S(2)}, u32[]{:S(2)}) collective-permute-start(bf16[320,512]{1,0:T(8,128)(2,1)S(1)} %get-tuple-element.37), channel_id=1, source_target_pairs={{0,3},{1,2},{2,1},{3,0},{4,7},{5,6},{6,5},{7,4},{8,11},{9,10},{10,... | collective-permute-start | bytes 983048 | tf_op jit(solution)/shard_map/ppermute | solution.py:552
  138.2 8.6 %ffn_late.1 = (f32[208,512]{1,0:T(8,128)S(1)}, bf16[208,512]{1,0:T(8,128)(2,1)S(1)}, bf16[208,512]{1,0:T(8,128)(2,1)S(1)}, bf16[208,512]{1,0:T(8,128)(2,1)S(1)}, f32[8,512]{1,0:T(8,128)S(1)}) custom-call(s32[12]{0:T(128)S(1)} %concatenate.39.info, bf16[224,512]{1,0:T(8,128)(2,1)S(1)} %get-tuple-element.48.refs_0_, ...), custom_call_target="tpu_custom_call" | custom-call | flops 3925868544 | bytes 20971520 | tf_op jit(solution)/shard_map/ffn_late/pallas_call | solution.py:500
  148.4 2.3 %collective-permute-start.31 = (bf16[208,512]{1,0:T(8,128)(2,1)S(1)}, bf16[208,512]{1,0:T(8,128)(2,1)S(1)}, u32[]{:S(2)}, u32[]{:S(2)}) collective-permute-start(bf16[208,512]{1,0:T(8,128)(2,1)S(1)} %get-tuple-element.53), channel_id=1, source_target_pairs={{0,3},{1,2},{2,1},{3,0},{4,7},{5,6},{6,5},{7,4},{8,11},{9,10},{10,... | collective-permute-start | bytes 638984 | tf_op jit(solution)/shard_map/ppermute | solution.py:552
  151.0 2.4 %collective-permute-done.29.r1 = bf16[208,512]{1,0:T(8,128)(2,1)S(1)} collective-permute-done((bf16[208,512]{1,0:T(8,128)(2,1)S(1)}, bf16[208,512]{1,0:T(8,128)(2,1)S(1)}, u32[]{:S(2)}, u32[]{:S(2)}) %collective-permute-start.29) | collective-permute-done | bytes 213024 | tf_op jit(solution)/shard_map/ppermute | solution.py:552
  153.3 3.2 %collective-permute-done.30.r2 = bf16[208,512]{1,0:T(8,128)(2,1)S(1)} collective-permute-done((bf16[208,512]{1,0:T(8,128)(2,1)S(1)}, bf16[208,512]{1,0:T(8,128)(2,1)S(1)}, u32[]{:S(2)}, u32[]{:S(2)}) %collective-permute-start.30) | collective-permute-done | bytes 213024 | tf_op jit(solution)/shard_map/ppermute | solution.py:552
  156.5 4.7 %collective-permute-done.31.r3 = bf16[208,512]{1,0:T(8,128)(2,1)S(1)} collective-permute-done((bf16[208,512]{1,0:T(8,128)(2,1)S(1)}, bf16[208,512]{1,0:T(8,128)(2,1)S(1)}, u32[]{:S(2)}, u32[]{:S(2)}) %collective-permute-start.31) | collective-permute-done | bytes 213024 | tf_op jit(solution)/shard_map/ppermute | solution.py:552
  (103 shorter events, 33.6 us)
Async XLA Ops:
  7.2 112.2 %all-gather.2.cloned.1.call-start = ((), (), s32[]{:S(2)}) async-start(), calls=%async_computation | async-start | bytes 19464192 | tf_op jit(solution)/shard_map/all_gather | solution.py:589
  20.0 9.7 %collective-permute-start.3 = (bf16[320,512]{1,0:T(8,128)(2,1)S(1)}, bf16[320,512]{1,0:T(8,128)(2,1)S(1)}, u32[]{:S(2)}, u32[]{:S(2)}) collective-permute-start(bf16[320,512]{1,0:T(8,128)(2,1)S(1)} %pad_maximum_fusion.2), channel_id=1, source_target_pairs={{0,32},{32,0},{64,96},{96,64},{1,33},{33,1},{65,97},{97,65},{2,34}... | collective-permute-start | bytes 983048 | tf_op jit(solution)/shard_map/ppermute | solution.py:552
  21.3 25.3 %collective-permute-start.4 = (bf16[320,512]{1,0:T(8,128)(2,1)S(1)}, bf16[320,512]{1,0:T(8,128)(2,1)S(1)}, u32[]{:S(2)}, u32[]{:S(2)}) collective-permute-start(bf16[320,512]{1,0:T(8,128)(2,1)S(1)} %pad_maximum_fusion.2), channel_id=1, source_target_pairs={{0,64},{32,96},{64,0},{96,32},{1,65},{33,97},{65,1},{97,33},{2,66}... | collective-permute-start | bytes 983048 | tf_op jit(solution)/shard_map/ppermute | solution.py:552
  23.8 22.8 %collective-permute-start.5 = (bf16[320,512]{1,0:T(8,128)(2,1)S(1)}, bf16[320,512]{1,0:T(8,128)(2,1)S(1)}, u32[]{:S(2)}, u32[]{:S(2)}) collective-permute-start(bf16[320,512]{1,0:T(8,128)(2,1)S(1)} %pad_maximum_fusion.2), channel_id=1, source_target_pairs={{0,96},{32,64},{64,32},{96,0},{1,97},{33,65},{65,33},{97,1},{2,98}... | collective-permute-start | bytes 983048 | tf_op jit(solution)/shard_map/ppermute | solution.py:552
  46.7 17.4 %collective-permute-start.6 = (bf16[1280,512]{1,0:T(8,128)(2,1)S(1)}, bf16[1280,512]{1,0:T(8,128)(2,1)S(1)}, u32[]{:S(2)}, u32[]{:S(2)}) collective-permute-start(bf16[1280,512]{1,0:T(8,128)(2,1)S(1)} %pad_maximum_fusion.w0_ref), channel_id=1, source_target_pairs={{0,4},{4,0},{1,5},{5,1},{2,6},{6,2},{3,7},{7,3},{8,12},{12,8},{9,1... | collective-permute-start | bytes 3932168 | tf_op jit(solution)/shard_map/ppermute | solution.py:552
  66.3 16.1 %collective-permute-start.7 = (bf16[320,512]{1,0:T(8,128)(2,1)S(1)}, bf16[320,512]{1,0:T(8,128)(2,1)S(1)}, u32[]{:S(2)}, u32[]{:S(2)}) collective-permute-start(bf16[320,512]{1,0:T(8,128)(2,1)S(1)} %get-tuple-element.29), channel_id=1, source_target_pairs={{0,1},{1,0},{2,3},{3,2},{4,5},{5,4},{6,7},{7,6},{8,9},{9,8},{10,11... | collective-permute-start | bytes 983048 | tf_op jit(solution)/shard_map/ppermute | solution.py:552
  68.1 17.0 %collective-permute-start.8 = (bf16[320,512]{1,0:T(8,128)(2,1)S(1)}, bf16[320,512]{1,0:T(8,128)(2,1)S(1)}, u32[]{:S(2)}, u32[]{:S(2)}) collective-permute-start(bf16[320,512]{1,0:T(8,128)(2,1)S(1)} %get-tuple-element.30), channel_id=1, source_target_pairs={{0,2},{1,3},{2,0},{3,1},{4,6},{5,7},{6,4},{7,5},{8,10},{9,11},{10,... | collective-permute-start | bytes 983048 | tf_op jit(solution)/shard_map/ppermute | solution.py:552
  71.2 15.5 %collective-permute-start.9 = (bf16[320,512]{1,0:T(8,128)(2,1)S(1)}, bf16[320,512]{1,0:T(8,128)(2,1)S(1)}, u32[]{:S(2)}, u32[]{:S(2)}) collective-permute-start(bf16[320,512]{1,0:T(8,128)(2,1)S(1)} %get-tuple-element.31), channel_id=1, source_target_pairs={{0,3},{1,2},{2,1},{3,0},{4,7},{5,6},{6,5},{7,4},{8,11},{9,10},{10,... | collective-permute-start | bytes 983048 | tf_op jit(solution)/shard_map/ppermute | solution.py:552
  79.4 18.5 %collective-permute-start.23 = (bf16[192,512]{1,0:T(8,128)(2,1)S(1)}, bf16[192,512]{1,0:T(8,128)(2,1)S(1)}, u32[]{:S(2)}, u32[]{:S(2)}) collective-permute-start(bf16[192,512]{1,0:T(8,128)(2,1)S(1)} %get-tuple-element.44), channel_id=1, source_target_pairs={{0,1},{1,0},{2,3},{3,2},{4,5},{5,4},{6,7},{7,6},{8,9},{9,8},{10,11... | collective-permute-start | bytes 589832 | tf_op jit(solution)/shard_map/ppermute | solution.py:552
  82.4 8.5 %collective-permute-start.20 = (bf16[32,256]{1,0:T(8,128)(2,1)S(1)}, bf16[32,256]{1,0:T(8,128)(2,1)S(1)}, u32[]{:S(2)}, u32[]{:S(2)}) collective-permute-start(bf16[32,256]{1,0:T(8,128)(2,1)S(1)} %pad_maximum_fusion.7), channel_id=1, source_target_pairs={{0,64},{32,96},{64,0},{96,32},{1,65},{33,97},{65,1},{97,33},{2,66}... | collective-permute-start | bytes 49160 | tf_op jit(solution)/shard_map/ppermute | solution.py:552
  87.3 29.8 %collective-permute-start.10 = (bf16[320,512]{1,0:T(8,128)(2,1)S(1)}, bf16[320,512]{1,0:T(8,128)(2,1)S(1)}, u32[]{:S(2)}, u32[]{:S(2)}) collective-permute-start(bf16[320,512]{1,0:T(8,128)(2,1)S(1)} %get-tuple-element.33.refs_0_), channel_id=1, source_target_pairs={{0,1},{1,0},{2,3},{3,2},{4,5},{5,4},{6,7},{7,6},{8,9},{9,8},{10,11... | collective-permute-start | bytes 983048 | tf_op jit(solution)/shard_map/ppermute | solution.py:552
  87.4 32.0 %collective-permute-start.11 = (bf16[320,512]{1,0:T(8,128)(2,1)S(1)}, bf16[320,512]{1,0:T(8,128)(2,1)S(1)}, u32[]{:S(2)}, u32[]{:S(2)}) collective-permute-start(bf16[320,512]{1,0:T(8,128)(2,1)S(1)} %get-tuple-element.33.refs_0_), channel_id=1, source_target_pairs={{0,2},{1,3},{2,0},{3,1},{4,6},{5,7},{6,4},{7,5},{8,10},{9,11},{10,... | collective-permute-start | bytes 983048 | tf_op jit(solution)/shard_map/ppermute | solution.py:552
  90.9 28.5 %collective-permute-start.12 = (bf16[320,512]{1,0:T(8,128)(2,1)S(1)}, bf16[320,512]{1,0:T(8,128)(2,1)S(1)}, u32[]{:S(2)}, u32[]{:S(2)}) collective-permute-start(bf16[320,512]{1,0:T(8,128)(2,1)S(1)} %get-tuple-element.33.refs_0_), channel_id=1, source_target_pairs={{0,3},{1,2},{2,1},{3,0},{4,7},{5,6},{6,5},{7,4},{8,11},{9,10},{10,... | collective-permute-start | bytes 983048 | tf_op jit(solution)/shard_map/ppermute | solution.py:552
  96.7 9.3 %collective-permute-start.24 = (bf16[192,512]{1,0:T(8,128)(2,1)S(1)}, bf16[192,512]{1,0:T(8,128)(2,1)S(1)}, u32[]{:S(2)}, u32[]{:S(2)}) collective-permute-start(bf16[192,512]{1,0:T(8,128)(2,1)S(1)} %get-tuple-element.45), channel_id=1, source_target_pairs={{0,2},{1,3},{2,0},{3,1},{4,6},{5,7},{6,4},{7,5},{8,10},{9,11},{10,... | collective-permute-start | bytes 589832 | tf_op jit(solution)/shard_map/ppermute | solution.py:552
  97.9 17.0 %collective-permute-start.25 = (bf16[192,512]{1,0:T(8,128)(2,1)S(1)}, bf16[192,512]{1,0:T(8,128)(2,1)S(1)}, u32[]{:S(2)}, u32[]{:S(2)}) collective-permute-start(bf16[192,512]{1,0:T(8,128)(2,1)S(1)} %get-tuple-element.46), channel_id=1, source_target_pairs={{0,3},{1,2},{2,1},{3,0},{4,7},{5,6},{6,5},{7,4},{8,11},{9,10},{10,... | collective-permute-start | bytes 589832 | tf_op jit(solution)/shard_map/ppermute | solution.py:552
  115.5 20.4 %collective-permute-start.26 = (bf16[224,512]{1,0:T(8,128)(2,1)S(1)}, bf16[224,512]{1,0:T(8,128)(2,1)S(1)}, u32[]{:S(2)}, u32[]{:S(2)}) collective-permute-start(bf16[224,512]{1,0:T(8,128)(2,1)S(1)} %get-tuple-element.48.refs_0_), channel_id=1, source_target_pairs={{0,1},{1,0},{2,3},{3,2},{4,5},{5,4},{6,7},{7,6},{8,9},{9,8},{10,11... | collective-permute-start | bytes 688136 | tf_op jit(solution)/shard_map/ppermute | solution.py:552
  115.6 22.6 %collective-permute-start.27 = (bf16[224,512]{1,0:T(8,128)(2,1)S(1)}, bf16[224,512]{1,0:T(8,128)(2,1)S(1)}, u32[]{:S(2)}, u32[]{:S(2)}) collective-permute-start(bf16[224,512]{1,0:T(8,128)(2,1)S(1)} %get-tuple-element.48.refs_0_), channel_id=1, source_target_pairs={{0,2},{1,3},{2,0},{3,1},{4,6},{5,7},{6,4},{7,5},{8,10},{9,11},{10,... | collective-permute-start | bytes 688136 | tf_op jit(solution)/shard_map/ppermute | solution.py:552
  117.2 21.0 %collective-permute-start.28 = (bf16[224,512]{1,0:T(8,128)(2,1)S(1)}, bf16[224,512]{1,0:T(8,128)(2,1)S(1)}, u32[]{:S(2)}, u32[]{:S(2)}) collective-permute-start(bf16[224,512]{1,0:T(8,128)(2,1)S(1)} %get-tuple-element.48.refs_0_), channel_id=1, source_target_pairs={{0,3},{1,2},{2,1},{3,0},{4,7},{5,6},{6,5},{7,4},{8,11},{9,10},{10,... | collective-permute-start | bytes 688136 | tf_op jit(solution)/shard_map/ppermute | solution.py:552
  134.2 14.2 %collective-permute-start.13 = (bf16[320,512]{1,0:T(8,128)(2,1)S(1)}, bf16[320,512]{1,0:T(8,128)(2,1)S(1)}, u32[]{:S(2)}, u32[]{:S(2)}) collective-permute-start(bf16[320,512]{1,0:T(8,128)(2,1)S(1)} %get-tuple-element.35), channel_id=1, source_target_pairs={{0,1},{1,0},{2,3},{3,2},{4,5},{5,4},{6,7},{7,6},{8,9},{9,8},{10,11... | collective-permute-start | bytes 983048 | tf_op jit(solution)/shard_map/ppermute | solution.py:552
  134.3 16.4 %collective-permute-start.14 = (bf16[320,512]{1,0:T(8,128)(2,1)S(1)}, bf16[320,512]{1,0:T(8,128)(2,1)S(1)}, u32[]{:S(2)}, u32[]{:S(2)}) collective-permute-start(bf16[320,512]{1,0:T(8,128)(2,1)S(1)} %get-tuple-element.36), channel_id=1, source_target_pairs={{0,2},{1,3},{2,0},{3,1},{4,6},{5,7},{6,4},{7,5},{8,10},{9,11},{10,... | collective-permute-start | bytes 983048 | tf_op jit(solution)/shard_map/ppermute | solution.py:552
  135.9 14.8 %collective-permute-start.15 = (bf16[320,512]{1,0:T(8,128)(2,1)S(1)}, bf16[320,512]{1,0:T(8,128)(2,1)S(1)}, u32[]{:S(2)}, u32[]{:S(2)}) collective-permute-start(bf16[320,512]{1,0:T(8,128)(2,1)S(1)} %get-tuple-element.37), channel_id=1, source_target_pairs={{0,3},{1,2},{2,1},{3,0},{4,7},{5,6},{6,5},{7,4},{8,11},{9,10},{10,... | collective-permute-start | bytes 983048 | tf_op jit(solution)/shard_map/ppermute | solution.py:552
  146.8 6.6 %collective-permute-start.29 = (bf16[208,512]{1,0:T(8,128)(2,1)S(1)}, bf16[208,512]{1,0:T(8,128)(2,1)S(1)}, u32[]{:S(2)}, u32[]{:S(2)}) collective-permute-start(bf16[208,512]{1,0:T(8,128)(2,1)S(1)} %get-tuple-element.51), channel_id=1, source_target_pairs={{0,1},{1,0},{2,3},{3,2},{4,5},{5,4},{6,7},{7,6},{8,9},{9,8},{10,11... | collective-permute-start | bytes 638984 | tf_op jit(solution)/shard_map/ppermute | solution.py:552
  146.9 9.7 %collective-permute-start.30 = (bf16[208,512]{1,0:T(8,128)(2,1)S(1)}, bf16[208,512]{1,0:T(8,128)(2,1)S(1)}, u32[]{:S(2)}, u32[]{:S(2)}) collective-permute-start(bf16[208,512]{1,0:T(8,128)(2,1)S(1)} %get-tuple-element.52), channel_id=1, source_target_pairs={{0,2},{1,3},{2,0},{3,1},{4,6},{5,7},{6,4},{7,5},{8,10},{9,11},{10,... | collective-permute-start | bytes 638984 | tf_op jit(solution)/shard_map/ppermute | solution.py:552
  148.4 12.8 %collective-permute-start.31 = (bf16[208,512]{1,0:T(8,128)(2,1)S(1)}, bf16[208,512]{1,0:T(8,128)(2,1)S(1)}, u32[]{:S(2)}, u32[]{:S(2)}) collective-permute-start(bf16[208,512]{1,0:T(8,128)(2,1)S(1)} %get-tuple-element.53), channel_id=1, source_target_pairs={{0,3},{1,2},{2,1},{3,0},{4,7},{5,6},{6,5},{7,4},{8,11},{9,10},{10,... | collective-permute-start | bytes 638984 | tf_op jit(solution)/shard_map/ppermute | solution.py:552
  (22 other events, 188.8 us)
Sparse Core Ops, SparseCore 0:
  10.3 90.9 all-gather.1
